TPU v7x, 32 devices: a whole 2x2x4 slice. The times are simulated.
32 devices in a mesh: dp: 4 (over z), ctx: 2 (over x), tp: 4 (over y, core).
Axes of the slice: x: 2, y: 2, z: 4, core: 2. Of those that a mesh axis runs over, the one named last changes fastest.
Arguments:
- image_tokens: bfloat16 [4, 1024, 1536], P('dp', 'ctx'), may hold values from -6 to 6
- text_tokens: bfloat16 [4, 154, 1536], P('dp', 'ctx'), may hold values from -6 to 6
- conditioning: bfloat16 [4, 1536], P(None, ('dp', 'ctx')), may hold values from -5 to 5
- ada_weight: bfloat16 [2, 1536, 6, 1536], P(None, ('dp', 'ctx'), None, 'tp'), may hold values from -0.15625 to 0.15625
- ada_bias: bfloat16 [2, 6, 1536], P(None, None, 'tp'), may hold values from -1.5 to 1.5
- qkv_weight: bfloat16 [2, 1536, 3, 1536], P(None, ('dp', 'ctx'), None, 'tp'), may hold values from -0.15625 to 0.15625
- qv_bias: bfloat16 [2, 2, 1536], P(None, None, 'tp'), may hold values from -1.5 to 1.5
- out_weight: bfloat16 [2, 1536, 1536], P(None, ('dp', 'ctx'), 'tp'), may hold values from -0.875 to 0.875
- out_bias: bfloat16 [2, 1536], P(None, ('dp', 'ctx')), may hold values from -1.5 to 1.5
- up_weight: bfloat16 [2, 1536, 6144], P(None, ('dp', 'ctx'), 'tp'), may hold values from -0.15625 to 0.15625
- up_bias: bfloat16 [2, 6144], P(None, 'tp'), may hold values from -1.5 to 1.5
- down_weight: bfloat16 [2, 1536, 6144], P(None, ('dp', 'ctx'), 'tp'), may hold values from -0.078125 to 0.078125
- down_bias: bfloat16 [2, 1536], P(None, ('dp', 'ctx')), may hold values from -1.5 to 1.5
- image_cotangent: bfloat16 [4, 1024, 1536], P('dp', 'ctx'), may hold values from -6 to 6
- text_cotangent: bfloat16 [4, 154, 1536], P('dp', 'ctx'), may hold values from -6 to 6
Outputs:
- image_out: bfloat16 [4, 1024, 1536], P('dp', 'ctx')
- text_out: bfloat16 [4, 154, 1536], P('dp', 'ctx')
- image_grad: bfloat16 [4, 1024, 1536], P('dp', 'ctx')
- text_grad: bfloat16 [4, 154, 1536], P('dp', 'ctx')
- cond_grad: float32 [4, 1536], P(None, ('dp', 'ctx'))
- ada_weight_grad: float32 [2, 1536, 6, 1536], P(None, ('dp', 'ctx'), None, 'tp')
- ada_bias_grad: float32 [2, 6, 1536], P(None, None, 'tp')
- qkv_weight_grad: float32 [2, 1536, 3, 1536], P(None, ('dp', 'ctx'), None, 'tp')
- qv_bias_grad: float32 [2, 2, 1536], P(None, None, 'tp')
- out_weight_grad: float32 [2, 1536, 1536], P(None, ('dp', 'ctx'), 'tp')
- out_bias_grad: float32 [2, 1536], P(None, ('dp', 'ctx'))
- up_weight_grad: float32 [2, 1536, 6144], P(None, ('dp', 'ctx'), 'tp')
- up_bias_grad: float32 [2, 6144], P(None, 'tp')
- down_weight_grad: float32 [2, 1536, 6144], P(None, ('dp', 'ctx'), 'tp')
- down_bias_grad: float32 [2, 1536], P(None, ('dp', 'ctx'))
- root_means: float32 [6], replicated
All inputs are finite; a program needn't handle non-finite values.
Results may differ from a plain program's by a relative error of at most 0.013.
Values may be sent and summed in bfloat16 or wider, within the bound.
A program may use at most 192 MiB of HBM per device.

v0:
```python
import jax
import jax.numpy as jnp
from jax import lax
from jax.sharding import PartitionSpec as P

HEAD_DIM = 64


def modulate(inputs, shift_by, scale_by):
    centred = inputs - jnp.mean(inputs, axis=-1, keepdims=True)
    spread = jnp.mean(centred * centred, axis=-1, keepdims=True)
    return centred * lax.rsqrt(spread + 1e-06) * (1.0 + scale_by) + shift_by


def gelu_tanh(inputs):
    return jax.nn.gelu(inputs, approximate=True)


def split_heads(matrix):
    return matrix.reshape(matrix.shape[0], matrix.shape[1] // HEAD_DIM, HEAD_DIM)


def attend_forward(operands):
    queries, keys_full, values_full = operands
    query_heads = split_heads(queries)
    key_heads = split_heads(keys_full)
    value_heads = split_heads(values_full)
    scores = jnp.einsum(
        "qhe,khe->hqk", query_heads, key_heads, preferred_element_type=jnp.float32
    ) * HEAD_DIM ** (-0.5)
    highest = jnp.max(scores, axis=-1, keepdims=True)
    log_total = highest + jnp.log(jnp.sum(jnp.exp(scores - highest), axis=-1, keepdims=True))
    weights = jnp.exp(scores - log_total).astype(jnp.bfloat16)
    blended = jnp.einsum("hqk,khe->qhe", weights, value_heads, preferred_element_type=jnp.float32)
    return (blended.reshape(queries.shape).astype(jnp.bfloat16), log_total)


def attend_backward(operands):
    queries, keys_full, values_full, log_total, grad_blended = operands
    query_heads = split_heads(queries)
    key_heads = split_heads(keys_full)
    value_heads = split_heads(values_full)
    grad_heads = split_heads(grad_blended)
    scores = jnp.einsum(
        "qhe,khe->hqk", query_heads, key_heads, preferred_element_type=jnp.float32
    ) * HEAD_DIM ** (-0.5)
    probability = jnp.exp(scores - log_total)
    grad_values = jnp.einsum(
        "hqk,qhe->khe",
        probability.astype(jnp.bfloat16),
        grad_heads,
        preferred_element_type=jnp.float32,
    )
    grad_probs = jnp.einsum(
        "qhe,khe->hqk", grad_heads, value_heads, preferred_element_type=jnp.float32
    )
    row_inner = jnp.sum(probability * grad_probs, axis=-1, keepdims=True)
    grad_scores = (probability * (grad_probs - row_inner)).astype(jnp.bfloat16)
    grad_queries = jnp.einsum(
        "hqk,khe->qhe", grad_scores, key_heads, preferred_element_type=jnp.float32
    ) * HEAD_DIM ** (-0.5)
    grad_keys = jnp.einsum(
        "hqk,qhe->khe", grad_scores, query_heads, preferred_element_type=jnp.float32
    ) * HEAD_DIM ** (-0.5)
    return (
        grad_queries.reshape(queries.shape),
        grad_keys.reshape(keys_full.shape),
        grad_values.reshape(values_full.shape),
    )


def branch_total(parts):
    return lax.psum(parts, "tp")


def input_total(parts):
    return lax.psum(parts, "tp")


def column_sum(matrix):
    return jnp.sum(matrix.astype(jnp.float32), axis=(0, 1))


def on_device(
    image_tokens,
    text_tokens,
    conditioning,
    ada_weight,
    ada_bias,
    qkv_weight,
    qv_bias,
    out_weight,
    out_bias,
    up_weight,
    up_bias,
    down_weight,
    down_bias,
    image_cotangent,
    text_cotangent,
):
    seq_count = image_tokens.shape[0]
    image_length = image_tokens.shape[1]
    text_length = text_tokens.shape[1]
    width = image_tokens.shape[2]
    slice_width = qkv_weight.shape[3]
    cond_float = conditioning.astype(jnp.float32)
    activated_low = jax.nn.silu(cond_float).astype(jnp.bfloat16)
    partial_mod = jnp.einsum(
        "nd,adkf->nakf", activated_low, ada_weight, preferred_element_type=jnp.float32
    )
    mod_slices = lax.psum(partial_mod, ("dp", "ctx")) + ada_bias.astype(jnp.float32)
    own_slices = lax.dynamic_slice_in_dim(
        mod_slices, lax.axis_index("dp") * seq_count, seq_count, 0
    )
    modulation = lax.all_gather(own_slices, "tp", axis=3, tiled=True)
    qkv_full, out_full, out_bias_full, up_full, down_full, down_bias_full = (
        lax.all_gather(qkv_weight, ("dp", "ctx"), axis=1, tiled=True),
        lax.all_gather(out_weight, ("dp", "ctx"), axis=1, tiled=True),
        lax.all_gather(out_bias, ("dp", "ctx"), axis=1, tiled=True),
        lax.all_gather(up_weight, ("dp", "ctx"), axis=1, tiled=True),
        lax.all_gather(down_weight, ("dp", "ctx"), axis=1, tiled=True),
        lax.all_gather(down_bias, ("dp", "ctx"), axis=1, tiled=True),
    )
    inputs_list = (image_tokens.astype(jnp.float32), text_tokens.astype(jnp.float32))
    cotangents = (image_cotangent, text_cotangent)
    normed_low = []
    query_parts = []
    key_parts = []
    value_parts = []
    for stream in range(2):
        normed = modulate(
            inputs_list[stream], modulation[:, stream, 0, None], modulation[:, stream, 1, None]
        ).astype(jnp.bfloat16)
        normed_low.append(normed)
        projected = jnp.einsum(
            "srd,dkf->srkf", normed, qkv_full[stream], preferred_element_type=jnp.float32
        )
        query_parts.append(
            (projected[:, :, 0] + qv_bias[stream, 0].astype(jnp.float32)).astype(jnp.bfloat16)
        )
        key_parts.append(projected[:, :, 1].astype(jnp.bfloat16))
        value_parts.append(
            (projected[:, :, 2] + qv_bias[stream, 1].astype(jnp.float32)).astype(jnp.bfloat16)
        )
    queries = jnp.concatenate(query_parts, 1)
    keys_local = jnp.concatenate(key_parts, 1)
    values_local = jnp.concatenate(value_parts, 1)
    keys_full, values_full = (
        lax.all_gather(keys_local, "ctx", axis=1, tiled=True),
        lax.all_gather(values_local, "ctx", axis=1, tiled=True),
    )
    blended, log_total = lax.map(attend_forward, (queries, keys_full, values_full))
    blended_parts = (blended[:, :image_length], blended[:, image_length:])
    attention_sums = branch_total(
        tuple(
            (
                jnp.einsum(
                    "srf,df->srd",
                    blended_parts[stream],
                    out_full[stream],
                    preferred_element_type=jnp.float32,
                )
                for stream in range(2)
            )
        )
    )
    attention = [
        attention_sums[stream] + out_bias_full[stream].astype(jnp.float32) for stream in range(2)
    ]
    middles = []
    second_low = []
    hidden_list = []
    gelu_low = []
    for stream in range(2):
        middle = inputs_list[stream] + modulation[:, stream, 2, None] * attention[stream]
        second = modulate(
            middle, modulation[:, stream, 3, None], modulation[:, stream, 4, None]
        ).astype(jnp.bfloat16)
        hidden = jnp.einsum(
            "srd,df->srf", second, up_full[stream], preferred_element_type=jnp.float32
        ) + up_bias[stream].astype(jnp.float32)
        middles.append(middle)
        second_low.append(second)
        hidden_list.append(hidden)
        gelu_low.append(gelu_tanh(hidden).astype(jnp.bfloat16))
    feed_sums = branch_total(
        tuple(
            (
                jnp.einsum(
                    "srf,df->srd",
                    gelu_low[stream],
                    down_full[stream],
                    preferred_element_type=jnp.float32,
                )
                for stream in range(2)
            )
        )
    )
    feed = [feed_sums[stream] + down_bias_full[stream].astype(jnp.float32) for stream in range(2)]
    outputs = []
    square_terms = []
    for stream in range(2):
        gated_attention = modulation[:, stream, 2, None] * attention[stream]
        gated_feed = modulation[:, stream, 5, None] * feed[stream]
        result = middles[stream] + gated_feed
        outputs.append(result.astype(jnp.bfloat16))
        square_terms.append(
            (
                jnp.sum(result * result),
                jnp.sum(gated_attention * gated_attention),
                jnp.sum(gated_feed * gated_feed),
            )
        )
    squares_local = jnp.stack(
        [
            square_terms[0][0],
            square_terms[1][0],
            square_terms[0][1],
            square_terms[1][1],
            square_terms[0][2],
            square_terms[1][2],
        ]
    )
    squares_total = lax.psum(squares_local, ("dp", "ctx"))
    qkv_full, out_full, up_full, down_full = (
        lax.all_gather(qkv_weight, ("dp", "ctx"), axis=1, tiled=True),
        lax.all_gather(out_weight, ("dp", "ctx"), axis=1, tiled=True),
        lax.all_gather(up_weight, ("dp", "ctx"), axis=1, tiled=True),
        lax.all_gather(down_weight, ("dp", "ctx"), axis=1, tiled=True),
    )
    grad_outputs = [cotangents[stream].astype(jnp.float32) for stream in range(2)]
    down_bias_grads = []
    down_weight_grads = []
    up_bias_grads = []
    up_weight_grads = []
    second_parts = []
    gate_two_grads = []
    for stream in range(2):
        gate_two_grads.append(jnp.sum(grad_outputs[stream] * feed[stream], axis=1))
        grad_feed = (grad_outputs[stream] * modulation[:, stream, 5, None]).astype(jnp.bfloat16)
        down_bias_grads.append(column_sum(grad_feed))
        down_weight_grads.append(
            jnp.einsum(
                "srd,srf->df", grad_feed, gelu_low[stream], preferred_element_type=jnp.float32
            )
        )
        grad_gelu = jnp.einsum(
            "srd,df->srf", grad_feed, down_full[stream], preferred_element_type=jnp.float32
        )
        gelu_pull = jax.vjp(gelu_tanh, hidden_list[stream])[1]
        grad_hidden = gelu_pull(grad_gelu)[0].astype(jnp.bfloat16)
        up_bias_grads.append(column_sum(grad_hidden))
        up_weight_grads.append(
            jnp.einsum(
                "srd,srf->df", second_low[stream], grad_hidden, preferred_element_type=jnp.float32
            )
        )
        second_parts.append(
            jnp.einsum(
                "srf,df->srd", grad_hidden, up_full[stream], preferred_element_type=jnp.float32
            )
        )
    grad_second = input_total(tuple(second_parts))
    grad_middles = []
    shift_two_grads = []
    scale_two_grads = []
    gate_one_grads = []
    out_bias_grads = []
    out_weight_grads = []
    blended_grads = []
    for stream in range(2):
        second_pull = jax.vjp(
            modulate,
            middles[stream],
            modulation[:, stream, 3, None],
            modulation[:, stream, 4, None],
        )[1]
        grad_middle, grad_shift, grad_scale = second_pull(grad_second[stream])
        grad_middle = grad_middle + grad_outputs[stream]
        grad_middles.append(grad_middle)
        shift_two_grads.append(grad_shift[:, 0])
        scale_two_grads.append(grad_scale[:, 0])
        gate_one_grads.append(jnp.sum(grad_middle * attention[stream], axis=1))
        grad_attention = (grad_middle * modulation[:, stream, 2, None]).astype(jnp.bfloat16)
        out_bias_grads.append(column_sum(grad_attention))
        out_weight_grads.append(
            jnp.einsum(
                "srd,srf->df",
                grad_attention,
                blended_parts[stream],
                preferred_element_type=jnp.float32,
            )
        )
        blended_grads.append(
            jnp.einsum(
                "srd,df->srf", grad_attention, out_full[stream], preferred_element_type=jnp.float32
            )
        )
    grad_blended = jnp.concatenate(blended_grads, 1).astype(jnp.bfloat16)
    grad_queries, grad_keys_full, grad_values_full = lax.map(
        attend_backward, (queries, keys_full, values_full, log_total, grad_blended)
    )
    grad_keys, grad_values = (
        lax.psum_scatter(grad_keys_full, "ctx", scatter_dimension=1, tiled=True),
        lax.psum_scatter(grad_values_full, "ctx", scatter_dimension=1, tiled=True),
    )
    grad_projected_all = jnp.stack([grad_queries, grad_keys, grad_values], axis=2).astype(
        jnp.bfloat16
    )
    projected_parts = (grad_projected_all[:, :image_length], grad_projected_all[:, image_length:])
    qv_bias_grads = []
    qkv_weight_grads = []
    normed_parts = []
    for stream in range(2):
        grad_projected = projected_parts[stream]
        sums_projected = jnp.sum(grad_projected.astype(jnp.float32), axis=(0, 1))
        qv_bias_grads.append(jnp.stack([sums_projected[0], sums_projected[2]]))
        qkv_weight_grads.append(
            jnp.einsum(
                "srd,srkf->dkf",
                normed_low[stream],
                grad_projected,
                preferred_element_type=jnp.float32,
            )
        )
        normed_parts.append(
            jnp.einsum(
                "srkf,dkf->srd",
                grad_projected,
                qkv_full[stream],
                preferred_element_type=jnp.float32,
            )
        )
    grad_normed = input_total(tuple(normed_parts))
    token_grads = []
    mod_grad_streams = []
    for stream in range(2):
        first_pull = jax.vjp(
            modulate,
            inputs_list[stream],
            modulation[:, stream, 0, None],
            modulation[:, stream, 1, None],
        )[1]
        grad_input, grad_shift, grad_scale = first_pull(grad_normed[stream])
        token_grads.append((grad_input + grad_middles[stream]).astype(jnp.bfloat16))
        mod_grad_streams.append(
            jnp.stack(
                [
                    grad_shift[:, 0],
                    grad_scale[:, 0],
                    gate_one_grads[stream],
                    shift_two_grads[stream],
                    scale_two_grads[stream],
                    gate_two_grads[stream],
                ],
                axis=1,
            )
        )
    grad_mod = jnp.stack(mod_grad_streams, axis=1)
    grad_mod_cols = lax.dynamic_slice_in_dim(
        grad_mod, lax.axis_index("tp") * slice_width, slice_width, 3
    )
    gathered_grad = lax.all_gather(grad_mod_cols, ("dp", "ctx"), axis=0, tiled=True)
    inner_shape = grad_mod_cols.shape[1:]
    grad_mod_all = jnp.sum(
        gathered_grad.reshape((lax.axis_size("dp"), lax.axis_size("ctx"), seq_count) + inner_shape),
        axis=1,
    )
    grad_mod_low = grad_mod_all.reshape((lax.axis_size("dp") * seq_count,) + inner_shape).astype(
        jnp.bfloat16
    )
    ada_bias_grad = jnp.sum(grad_mod_low.astype(jnp.float32), axis=0)
    ada_weight_grad = jnp.einsum(
        "nd,nakf->adkf", activated_low, grad_mod_low, preferred_element_type=jnp.float32
    )
    cond_partial = jnp.einsum(
        "nakf,adkf->nd", grad_mod_low, ada_weight, preferred_element_type=jnp.float32
    )
    cond_total = lax.psum(cond_partial, "tp")
    cond_grad = jax.vjp(jax.nn.silu, cond_float)[1](cond_total)[0]
    (
        qkv_weight_grad,
        out_weight_grad,
        out_bias_grad,
        up_weight_grad,
        down_weight_grad,
        down_bias_grad,
    ) = (
        lax.psum_scatter(
            jnp.stack(qkv_weight_grads), ("dp", "ctx"), scatter_dimension=1, tiled=True
        ),
        lax.psum_scatter(
            jnp.stack(out_weight_grads), ("dp", "ctx"), scatter_dimension=1, tiled=True
        ),
        lax.psum_scatter(jnp.stack(out_bias_grads), ("dp", "ctx"), scatter_dimension=1, tiled=True),
        lax.psum_scatter(
            jnp.stack(up_weight_grads), ("dp", "ctx"), scatter_dimension=1, tiled=True
        ),
        lax.psum_scatter(
            jnp.stack(down_weight_grads), ("dp", "ctx"), scatter_dimension=1, tiled=True
        ),
        lax.psum_scatter(
            jnp.stack(down_bias_grads), ("dp", "ctx"), scatter_dimension=1, tiled=True
        ),
    )
    qv_local = jnp.stack(qv_bias_grads)
    up_local = jnp.stack(up_bias_grads)
    qv_bias_grad, up_bias_grad = lax.psum((qv_local, up_local), ("dp", "ctx"))
    devices_along = lax.axis_size("dp") * lax.axis_size("ctx") * seq_count * width
    counts = jnp.array([image_length, text_length] * 3, jnp.float32) * devices_along
    root_means = jnp.sqrt(squares_total / counts)
    return (
        outputs[0],
        outputs[1],
        token_grads[0],
        token_grads[1],
        cond_grad,
        ada_weight_grad,
        ada_bias_grad,
        qkv_weight_grad,
        qv_bias_grad,
        out_weight_grad,
        out_bias_grad,
        up_weight_grad,
        up_bias_grad,
        down_weight_grad,
        down_bias_grad,
        root_means,
    )


def solution(mesh):
    placed = (
        P("dp", "ctx", None),
        P("dp", "ctx", None),
        P(None, ("dp", "ctx")),
        P(None, ("dp", "ctx"), None, "tp"),
        P(None, None, "tp"),
        P(None, ("dp", "ctx"), None, "tp"),
        P(None, None, "tp"),
        P(None, ("dp", "ctx"), "tp"),
        P(None, ("dp", "ctx")),
        P(None, ("dp", "ctx"), "tp"),
        P(None, "tp"),
        P(None, ("dp", "ctx"), "tp"),
        P(None, ("dp", "ctx")),
        P("dp", "ctx", None),
        P("dp", "ctx", None),
    )
    return jax.shard_map(
        on_device,
        mesh=mesh,
        in_specs=placed,
        out_specs=(
            P("dp", "ctx", None),
            P("dp", "ctx", None),
            P("dp", "ctx", None),
            P("dp", "ctx", None),
            P(None, ("dp", "ctx")),
            P(None, ("dp", "ctx"), None, "tp"),
            P(None, None, "tp"),
            P(None, ("dp", "ctx"), None, "tp"),
            P(None, None, "tp"),
            P(None, ("dp", "ctx"), "tp"),
            P(None, ("dp", "ctx")),
            P(None, ("dp", "ctx"), "tp"),
            P(None, "tp"),
            P(None, ("dp", "ctx"), "tp"),
            P(None, ("dp", "ctx")),
            P(),
        ),
        check_vma=False,
    )
```

profile of v0, /device:TPU:0, one launch (start us, length us, event | category | flops | bytes accessed | tf_op | source)
XLA Modules:
  0.0 2737.6 jit_solution(12025889301689288748)
XLA Ops:
  18.3 64.9 %all-reduce.13.cloned.1.call-done = f32[4,2,6,384]{3,0,2,1:T(4,128)} async-done(((f32[4,2,6,384]{3,0,2,1:T(4,128)}), f32[4,2,6,384]{3,0,2,1:T(4,128)}) %all-reduce.13.cloned.1.call-update) | async-done | bytes 73744 | tf_op jit(solution)/shard_map/psum | solution.py:111
  84.1 5.3 all_gather.34
  90.2 104.0 %all-gather.7.cloned.1.call-done = bf16[2,1536,3,384]{3,1,2,0:T(8,128)(2,1)} async-done(((bf16[2,192,3,384]{3,1,2,0:T(8,128)(2,1)}), bf16[2,1536,3,384]{3,1,2,0:T(8,128)(2,1)}) %all-gather.7.cloned.1.call-update) | async-done | bytes 7077904 | tf_op jit(solution)/shard_map/all_gather | solution.py:117
  197.3 4.5 fusion.43
  202.7 26.9 all_gather.36
  231.2 4.8 copy.78
  238.9 21.7 all_gather.37
  260.6 4.9 copy.82
  270.9 10.2 fusion.157
  281.1 8.8 exponential_reduce_fusion
  290.5 10.0 fusion.52
  300.6 4.2 convolution_bitcast_fusion.6
  308.2 18.0 all-gather
  326.4 55.5 %all-reduce.19.cloned.1.call-done = (f32[1,512,1536]{2,1,0:T(8,128)}, f32[1,77,1536]{2,1,0:T(8,128)}) async-done(((f32[1,512,1536]{2,1,0:T(8,128)}, f32[1,77,1536]{2,1,0:T(8,128)}), (f32[1,512,1536]{2,1,0:T(8,128)}, f32[1,77,1536]{2,1,0:T(8,128)})) %all-reduce.19.cloned.1.call-update) | async-done | bytes 3618832 | tf_op jit(solution)/shard_map/psum | solution.py:73
  388.7 133.7 %all-gather.11.cloned.1.call-done = bf16[2,1536,1536]{2,1,0:T(8,128)(2,1)} async-done(((bf16[2,192,1536]{2,1,0:T(8,128)(2,1)}), bf16[2,1536,1536]{2,1,0:T(8,128)(2,1)}) %all-gather.11.cloned.1.call-update) | async-done | bytes 9437200 | tf_op jit(solution)/shard_map/all_gather | solution.py:120
  522.4 7.6 fusion.17
  530.0 130.9 %all-gather.13.cloned.1.call-done = bf16[2,1536,1536]{2,1,0:T(8,128)(2,1)} async-done(((bf16[2,192,1536]{2,1,0:T(8,128)(2,1)}), bf16[2,1536,1536]{2,1,0:T(8,128)(2,1)}) %all-gather.13.cloned.1.call-update) | async-done | bytes 9437200 | tf_op jit(solution)/shard_map/all_gather | solution.py:121
  661.0 7.8 fusion.15
  678.0 5.0 convert_reduce_fusion.2
  684.1 4.3 fusion.16
  689.0 18.0 all-gather.1
  716.4 106.5 %all-reduce.17.cloned.1.call-done = (f32[1,512,1536]{2,1,0:T(8,128)}, f32[1,77,1536]{2,1,0:T(8,128)}, f32[1,77,1536]{2,1,0:T(8,128)}, f32[1,512,1536]{2,1,0:T(8,128)}) async-done(((f32[1,512,1536]{2,1,0:T(8,128)}, f32[1,77,1536]{2,1,0:T(8,128)}, f32[1,77,1536]{2,1,0:T(8,128)}, f32[1,512,1536]{2,1,0:T(8,128)}), (f32[1,512,1536]{2,1,0:T(8,128)}, f32[1,77,1536]{2,1,0:T(8,128)}, f32[1,77,1536]{2,1,0:T(8,128)}, ...) | async-done | bytes 7237648 | tf_op jit(solution)/shard_map/psum | solution.py:73
  827.7 8.4 multiply_reduce_fusion.1
  844.9 5.2 fusion.35
  850.1 11.8 multiply_reduce_fusion
  861.9 12.8 multiply_convert_fusion
  877.7 3.4 fusion.51
  881.2 5.1 copy.89
  886.3 5.1 copy.87
  891.4 654.3 %all-reduce.20 = (bf16[1,1178,384]{2,0,1:T(2,128)(2,1)}, bf16[1,1178,384]{2,0,1:T(2,128)(2,1)}) all-reduce(f32[1,1178,384]{2,0,1:T(1,128)} %copy.89, f32[1,1178,384]{2,0,1:T(1,128)} %copy.87), channel_id=3, replica_groups=mesh['dp'=4,'ctx'=2,'tp'=4] {'ctx'}, use_global_device_ids=true, to_apply=%region_23.24.clone | all-reduce | flops 904704 | bytes 5428224
  1559.5 6.3 convolution_bitcast_fusion.7
  1565.8 4.0 fusion.40
  1577.0 5.2 convolution_bitcast_fusion.4
  1582.2 5.4 convolution_bitcast_fusion.5
  1587.6 11.0 pad_maximum_fusion.2
  1605.0 6.8 pad_maximum_fusion
  1618.1 6.9 pad_maximum_fusion.1
  1625.8 3.9 stack.183
  1631.2 38.1 %all-reduce.2 = (f32[2,2,384]{2,1,0:T(2,128)}, f32[2,1536]{1,0:T(2,128)}, f32[6]{0:T(128)S(1)}) all-reduce(f32[2,2,384]{2,1,0:T(2,128)S(1)} %pad_maximum_fusion.17, f32[2,1536]{1,0:T(2,128)S(1)} %pad_maximum_fusion.15, f32[6]{0:T(128)S(1)} %stack.183), channel_id=1, replica_groups=mesh['dp'=4,'ctx'=2,'tp'=4] {'dp','ctx'}, use_global_device_ids=true, to_apply=%region_48.49 | all-reduce | flops 4614 | bytes 36912 | tf_op jit(solution)/shard_map/psum | solution.py:408
  1671.4 12.2 reduce-scatter.21.cloned.1.call-done
  1685.1 76.5 %all-reduce.15.cloned.1.call-done = (f32[1,512,1536]{2,1,0:T(8,128)}, f32[1,77,1536]{2,1,0:T(8,128)}) async-done(((f32[1,512,1536]{2,1,0:T(8,128)}, f32[1,77,1536]{2,1,0:T(8,128)}), (f32[1,512,1536]{2,1,0:T(8,128)}, f32[1,77,1536]{2,1,0:T(8,128)})) %all-reduce.15.cloned.1.call-update) | async-done | bytes 3618832 | tf_op jit(solution)/shard_map/psum | solution.py:77
  1769.5 31.8 %all_gather.43 = f32[8,2,6,384]{3,1,2,0:T(2,128)S(1)} all-gather(f32[1,2,6,384]{3,1,2,0:T(2,128)S(1)} %fusion.112), channel_id=1, replica_groups=mesh['dp'=4,'ctx'=2,'tp'=4] {'dp','ctx'}, dimensions={0}, use_global_device_ids=true | all-gather | bytes 165888 | tf_op jit(solution)/shard_map/all_gather | solution.py:363
  1801.9 6.1 psum.100
  1814.1 3.8 add_convert_fusion
  1817.9 44.8 %reduce-scatter.13.cloned.1.call-done = f32[2,192,384]{2,1,0:T(8,128)} async-done(((f32[2,1536,384]{2,1,0:T(8,128)}), f32[2,192,384]{2,1,0:T(8,128)}) %reduce-scatter.13.cloned.1.call-update) | async-done | bytes 589840 | tf_op jit(solution)/shard_map/reduce_scatter | solution.py:392
  1862.7 233.5 %reduce-scatter.11.cloned.1.call-done = f32[2,192,3,384]{3,1,2,0:T(8,128)} async-done(((f32[2,1536,3,384]{3,1,2,0:T(8,128)}), f32[2,192,3,384]{3,1,2,0:T(8,128)}) %reduce-scatter.11.cloned.1.call-update) | async-done | bytes 1769488 | tf_op jit(solution)/shard_map/reduce_scatter | solution.py:389
  2096.2 317.4 %reduce-scatter.15.cloned.1.call-done = f32[2,192,1536]{2,1,0:T(8,128)} async-done(((f32[2,1536,1536]{2,1,0:T(8,128)}), f32[2,192,1536]{2,1,0:T(8,128)}) %reduce-scatter.15.cloned.1.call-update) | async-done | bytes 2359312 | tf_op jit(solution)/shard_map/reduce_scatter | solution.py:396
  2413.6 317.3 %reduce-scatter.17.cloned.1.call-done = f32[2,192,1536]{2,1,0:T(8,128)} async-done(((f32[2,1536,1536]{2,1,0:T(8,128)}), f32[2,192,1536]{2,1,0:T(8,128)}) %reduce-scatter.17.cloned.1.call-update) | async-done | bytes 2359312 | tf_op jit(solution)/shard_map/reduce_scatter | solution.py:399
  (400 shorter events, 126.8 us)
Async XLA Ops:
  7.2 76.0 %all-reduce.13.cloned.1.call-start = ((), (), s32[]{:S(2)}) async-start(), calls=%async_computation.6 | async-start | bytes 147456 | tf_op jit(solution)/shard_map/psum | solution.py:111
  10.3 183.9 %all-gather.7.cloned.1.call-start = ((), (), s32[]{:S(2)}) async-start(), calls=%async_computation.7 | async-start | bytes 7962624 | tf_op jit(solution)/shard_map/all_gather | solution.py:117
  11.1 289.5 %all-gather.9.cloned.1.call-start = ((), (), s32[]{:S(2)}) async-start(), calls=%async_computation.8 | async-start | bytes 2654208 | tf_op jit(solution)/shard_map/all_gather | solution.py:118
  11.8 370.1 %all-reduce.19.cloned.1.call-start = ((), (), s32[]{:S(2)}) async-start(), calls=%async_computation.19 | async-start | bytes 7274496 | tf_op jit(solution)/shard_map/psum | solution.py:73
  13.7 183.5 %copy-start.87 = (f32[77]{0:T(128)}, f32[77]{0:T(128)S(1)}, u32[]{:S(2)}) copy-start(f32[77]{0:T(128)S(1)} %broadcast_multiply_fusion.3) | copy-start | bytes 928
  15.5 181.7 %copy-start.100 = (f32[77]{0:T(128)}, f32[77]{0:T(128)S(1)}, u32[]{:S(2)}) copy-start(f32[77]{0:T(128)S(1)} %fusion.133) | copy-start | bytes 928
  15.8 181.5 %copy-start.55 = (f32[512]{0:T(512)}, f32[512]{0:T(512)S(1)}, u32[]{:S(2)}) copy-start(f32[512]{0:T(512)S(1)} %broadcast_multiply_fusion.1) | copy-start | bytes 6148
  16.9 184.8 %copy-start.76 = (f32[512]{0:T(512)}, f32[512]{0:T(512)S(1)}, u32[]{:S(2)}) copy-start(f32[512]{0:T(512)S(1)} %fusion.128) | copy-start | bytes 6148
  90.2 111.6 %copy-start.38 = (f32[1536]{0:T(1024)}, f32[1536]{0:T(1024)S(1)}, u32[]{:S(2)}) copy-start(f32[1536]{0:T(1024)S(1)} %get-tuple-element.129) | copy-start | bytes 18436
  90.2 111.6 %copy-start.42 = (f32[1536]{0:T(1024)}, f32[1536]{0:T(1024)S(1)}, u32[]{:S(2)}) copy-start(f32[1536]{0:T(1024)S(1)} %get-tuple-element.131) | copy-start | bytes 18436
  90.2 111.6 %copy-start.65 = (f32[1536]{0:T(1024)}, f32[1536]{0:T(1024)S(1)}, u32[]{:S(2)}) copy-start(f32[1536]{0:T(1024)S(1)} %get-tuple-element.128) | copy-start | bytes 18436
  90.2 111.6 %copy-start.96 = (f32[1536]{0:T(1024)}, f32[1536]{0:T(1024)S(1)}, u32[]{:S(2)}) copy-start(f32[1536]{0:T(1024)S(1)} %get-tuple-element.130) | copy-start | bytes 18436
  90.2 578.6 %copy-start.44 = (f32[1536]{0:T(1024)}, f32[1536]{0:T(1024)S(1)}, u32[]{:S(2)}) copy-start(f32[1536]{0:T(1024)S(1)} %get-tuple-element.122) | copy-start | bytes 18436
  90.2 735.9 %copy-start.40 = (f32[1536]{0:T(1024)}, f32[1536]{0:T(1024)S(1)}, u32[]{:S(2)}) copy-start(f32[1536]{0:T(1024)S(1)} %get-tuple-element.123) | copy-start | bytes 18436
  197.2 32.4 %copy-start.36 = (f32[1,77,3,384]{3,1,2,0:T(8,128)}, f32[1,77,3,384]{3,1,2,0:T(8,128)S(1)}, u32[]{:S(2)}) copy-start(f32[1,77,3,384]{3,1,2,0:T(8,128)S(1)} %fusion.58) | copy-start | bytes 1064452
  201.8 28.4 %copy-start.28 = (f32[1,512,3,384]{3,1,2,0:T(8,128)}, f32[1,512,3,384]{3,1,2,0:T(8,128)S(1)}, u32[]{:S(2)}) copy-start(f32[1,512,3,384]{3,1,2,0:T(8,128)S(1)} %fusion.43) | copy-start | bytes 7077892
  307.0 19.3 copy-start.75
  307.0 75.0 %copy-start.46 = (f32[1536]{0:T(1024)S(1)}, f32[1536]{0:T(1024)}, u32[]{:S(2)}) copy-start(f32[1536]{0:T(1024)} %get-tuple-element.124) | copy-start | bytes 18436
  307.0 77.1 %copy-start.53 = (f32[1536]{0:T(1024)S(1)}, f32[1536]{0:T(1024)}, u32[]{:S(2)}) copy-start(f32[1536]{0:T(1024)} %get-tuple-element.132) | copy-start | bytes 18436
  307.0 215.4 %all-gather.11.cloned.1.call-start = ((), (), s32[]{:S(2)}) async-start(), calls=%async_computation.9 | async-start | bytes 10616832 | tf_op jit(solution)/shard_map/all_gather | solution.py:120
  307.6 353.4 %all-gather.13.cloned.1.call-start = ((), (), s32[]{:S(2)}) async-start(), calls=%async_computation.10 | async-start | bytes 10616832 | tf_op jit(solution)/shard_map/all_gather | solution.py:121
  308.2 514.7 %all-reduce.17.cloned.1.call-start = ((), (), s32[]{:S(2)}) async-start(), calls=%async_computation.18 | async-start | bytes 14548992 | tf_op jit(solution)/shard_map/psum | solution.py:73
  326.4 60.1 %copy-start.51 = (f32[1536]{0:T(1024)}, f32[1536]{0:T(1024)S(1)}, u32[]{:S(2)}) copy-start(f32[1536]{0:T(1024)S(1)} %get-tuple-element.138) | copy-start | bytes 18436
  383.2 442.9 %copy-start.89 = (f32[77]{0:T(128)}, f32[77]{0:T(128)S(1)}, u32[]{:S(2)}) copy-start(f32[77]{0:T(128)S(1)} %broadcast_multiply_fusion.2) | copy-start | bytes 928
  383.5 442.7 %copy-start.98 = (f32[77]{0:T(128)}, f32[77]{0:T(128)S(1)}, u32[]{:S(2)}) copy-start(f32[77]{0:T(128)S(1)} %fusion.134) | copy-start | bytes 928
  386.5 135.9 %copy-start.49 = (f32[1536]{0:T(1024)S(1)}, f32[1536]{0:T(1024)}, u32[]{:S(2)}) copy-start(f32[1536]{0:T(1024)} %get-tuple-element.126) | copy-start | bytes 18436
  386.5 135.9 %copy-start.94 = (f32[1536]{0:T(1024)S(1)}, f32[1536]{0:T(1024)}, u32[]{:S(2)}) copy-start(f32[1536]{0:T(1024)} %get-tuple-element.125) | copy-start | bytes 18436
  386.6 449.6 %copy-start.57 = (f32[512]{0:T(512)}, f32[512]{0:T(512)S(1)}, u32[]{:S(2)}) copy-start(f32[512]{0:T(512)S(1)} %broadcast_multiply_fusion) | copy-start | bytes 6148
  388.7 447.5 %copy-start.79 = (f32[512]{0:T(512)}, f32[512]{0:T(512)S(1)}, u32[]{:S(2)}) copy-start(f32[512]{0:T(512)S(1)} %fusion.129) | copy-start | bytes 6148
  688.4 18.7 copy-start.111
  688.4 981.4 %reduce-scatter.19.cloned.1.call-start = ((), (), s32[]{:S(2)}) async-start(), calls=%async_computation.15 | async-start | bytes 884736
  827.7 17.1 slice-start
  827.7 17.1 slice-start.1
  861.9 12.8 copy-start.32
  1554.0 129.5 %reduce-scatter.21.cloned.1.call-start = ((), (), s32[]{:S(2)}) async-start(), calls=%async_computation.16 | async-start | bytes 884736
  1559.5 202.1 %all-reduce.15.cloned.1.call-start = ((), (), s32[]{:S(2)}) async-start(), calls=%async_computation.17 | async-start | bytes 7274496 | tf_op jit(solution)/shard_map/psum | solution.py:77
  1569.8 292.9 %reduce-scatter.13.cloned.1.call-start = ((), (), s32[]{:S(2)}) async-start(), calls=%async_computation.12 | async-start | bytes 5308416 | tf_op jit(solution)/shard_map/reduce_scatter | solution.py:392
  1576.4 519.8 %reduce-scatter.11.cloned.1.call-start = ((), (), s32[]{:S(2)}) async-start(), calls=%async_computation.11 | async-start | bytes 15925248 | tf_op jit(solution)/shard_map/reduce_scatter | solution.py:389
  1598.7 814.9 %reduce-scatter.15.cloned.1.call-start = ((), (), s32[]{:S(2)}) async-start(), calls=%async_computation.13 | async-start | bytes 21233664 | tf_op jit(solution)/shard_map/reduce_scatter | solution.py:396
  1611.9 1119.0 %reduce-scatter.17.cloned.1.call-start = ((), (), s32[]{:S(2)}) async-start(), calls=%async_computation.14 | async-start | bytes 21233664 | tf_op jit(solution)/shard_map/reduce_scatter | solution.py:399
  1625.0 44.3 %copy-start.110 = (f32[6]{0:T(128)S(1)}, f32[6]{0:T(128)}, u32[]{:S(2)}) copy-start(f32[6]{0:T(128)} %constant.121) | copy-start | bytes 76
  1625.0 136.5 %copy-start.88 = (f32[77]{0:T(128)S(1)}, f32[77]{0:T(128)}, u32[]{:S(2)}) copy-start(f32[77]{0:T(128)} %copy-done.87) | copy-start | bytes 928
  1625.0 138.1 %copy-start.107 = (f32[77]{0:T(128)S(1)}, f32[77]{0:T(128)}, u32[]{:S(2)}) copy-start(f32[77]{0:T(128)} %copy-done.106) | copy-start | bytes 928
  1625.1 138.1 %copy-start.101 = (f32[77]{0:T(128)S(1)}, f32[77]{0:T(128)}, u32[]{:S(2)}) copy-start(f32[77]{0:T(128)} %copy-done.100) | copy-start | bytes 928
  1685.1 82.1 %copy-start.82 = (f32[512]{0:T(512)S(1)}, f32[512]{0:T(512)}, u32[]{:S(2)}) copy-start(f32[512]{0:T(512)} %copy-done.81) | copy-start | bytes 6148
  1685.1 82.2 %copy-start.78 = (f32[512]{0:T(512)S(1)}, f32[512]{0:T(512)}, u32[]{:S(2)}) copy-start(f32[512]{0:T(512)} %copy-done.76) | copy-start | bytes 6148
  1767.3 41.3 %copy-start.83 = (bf16[4,192]{1,0:T(4,128)(2,1)S(1)}, bf16[4,192]{1,0:T(4,128)(2,1)}, u32[]{:S(2)}) copy-start(bf16[4,192]{1,0:T(4,128)(2,1)} %param.18) | copy-start | bytes 4612
  1769.1 42.6 %copy-start.103 = (f32[77]{0:T(128)S(1)}, f32[77]{0:T(128)}, u32[]{:S(2)}) copy-start(f32[77]{0:T(128)} %copy-done.102) | copy-start | bytes 928
  (87 other events, 345.4 us)
Sparse Core Ops, SparseCore 0:
  12.0 71.1 all-reduce.12
  85.4 108.7 all-gather.6
  196.4 54.0 all-gather.8
  307.1 74.7 all-reduce.18
  384.2 138.1 all-gather.10
  524.7 136.2 all-gather.12
  688.5 134.3 all-reduce.16
  1554.2 64.1 reduce-scatter.18
  1622.0 61.4 reduce-scatter.20
  1685.9 75.5 all-reduce.14
  1766.2 96.4 reduce-scatter.12
  1867.2 228.9 reduce-scatter.10
  2101.2 312.3 reduce-scatter.14
  2418.4 312.4 reduce-scatter.16
where the time goes:
time: 2740 us
  waiting for transfers between devices  1600 us (58%)
  blocking collectives  820 us (30%)
  matrix products  131 us (5%)
  other arithmetic  98.8 us (4%)
  local copies, waits for them, and re-layouts  70.1 us (3%)
    unnamed x1, blocking collectives  654 us
    reduce_scatter x1, waiting for transfers between devices, on_device(): lax.psum_scatter(jnp.stack(up_weight_grads), ('dp', 'ctx'), scatter_dimen...  317 us
    reduce_scatter x1, waiting for transfers between devices, on_device(): lax.psum_scatter(jnp.stack(down_weight_grads), ('dp', 'ctx'), scatter_dim...  317 us
    reduce_scatter x1, waiting for transfers between devices, on_device(): lax.psum_scatter(jnp.stack(qkv_weight_grads), ('dp', 'ctx'), scatter_dime...  233 us
    psum x2, waiting for transfers between devices, branch_total(): return lax.psum(parts, 'tp')  162 us
    all_gather x1, waiting for transfers between devices, on_device(): lax.all_gather(up_weight, ('dp', 'ctx'), axis=1, tiled=True)  134 us
    all_gather x1, waiting for transfers between devices, on_device(): lax.all_gather(down_weight, ('dp', 'ctx'), axis=1, tiled=True)  131 us
    all_gather x1, waiting for transfers between devices, on_device(): lax.all_gather(qkv_weight, ('dp', 'ctx'), axis=1, tiled=True)  104 us
  transfers between devices with their start and end apart: 14, of which 12 were waited for; matrix products, arithmetic and copies ran while one was open for 7% of the time, Pallas kernels for 0%

commit v1 on v0

v1 whole, which is shorter than its diff:
```python
import functools

import jax
import jax.numpy as jnp
from jax import lax
from jax.experimental import pallas as pl
from jax.experimental.pallas import tpu as pltpu
from jax.sharding import PartitionSpec as P

HEAD_DIM = 64
F32 = jnp.float32
BF16 = jnp.bfloat16
VMEM_LIMIT = 60 * 1024 * 1024
PLANE = ("ctx", "tp")
TEXT_SLOTS = 128
QUERY_BLOCK = 256


def dot(left, right, dims=((1,), (0,))):
    return lax.dot_general(left, right, (dims, ((), ())), preferred_element_type=F32)


def key_bias(rows, image_rows, text_rows):
    slot = lax.broadcasted_iota(jnp.int32, (rows, 1), 0)
    masked = jnp.logical_and(slot >= image_rows, lax.rem(slot - image_rows, TEXT_SLOTS) >= text_rows)
    return jnp.where(masked, -1e30, 0.0).astype(F32)


def attend_forward_kernel(heads, image_rows, text_rows, q_ref, k_ref, v_ref, o_ref, lse_ref, vt_ref):
    @pl.when(pl.program_id(0) == 0)
    def _():
        vt_ref[...] = v_ref[...].T

    rows = k_ref.shape[0]
    bias = key_bias(rows, image_rows, text_rows)
    queries_t = (q_ref[...] * HEAD_DIM ** (-0.5)).T
    outs = []
    for head in range(heads):
        span = slice(head * HEAD_DIM, (head + 1) * HEAD_DIM)
        scores = dot(k_ref[:, span], queries_t[span]) + bias
        top = jnp.max(scores, axis=0, keepdims=True)
        grown = jnp.exp(scores - top)
        total = jnp.sum(grown, axis=0, keepdims=True)
        lse_ref[head : head + 1] = top + jnp.log(total)
        outs.append(dot(vt_ref[span], grown.astype(BF16)) * (1.0 / total))
    o_ref[...] = jnp.concatenate(outs, 0).T.astype(BF16)


def attend_forward(q, k, v, image_rows, text_rows):
    rows, wide = q.shape
    heads = wide // HEAD_DIM
    whole = pl.BlockSpec((rows, wide), lambda i: (0, 0))
    block = pl.BlockSpec((QUERY_BLOCK, wide), lambda i: (i, 0))
    return pl.pallas_call(
        functools.partial(attend_forward_kernel, heads, image_rows, text_rows),
        grid=(rows // QUERY_BLOCK,),
        in_specs=[block, whole, whole],
        out_specs=[block, pl.BlockSpec((heads, QUERY_BLOCK), lambda i: (0, i))],
        out_shape=[
            jax.ShapeDtypeStruct((rows, wide), BF16),
            jax.ShapeDtypeStruct((heads, rows), F32),
        ],
        scratch_shapes=[pltpu.VMEM((wide, rows), BF16)],
        compiler_params=pltpu.CompilerParams(vmem_limit_bytes=VMEM_LIMIT),
        cost_estimate=pl.CostEstimate(
            flops=4 * rows * rows * wide, bytes_accessed=8 * rows * wide, transcendentals=heads * rows * rows
        ),
        name="attend_forward",
    )(q, k, v)


def attend_backward_kernel(
    heads, image_rows, text_rows, q_ref, k_ref, v_ref, g_ref, lse_ref, dq_ref, dk_ref, dv_ref, kt_ref, dk_sum, dv_sum
):
    step = pl.program_id(0)

    @pl.when(step == 0)
    def _():
        kt_ref[...] = k_ref[...].T
        dk_sum[...] = jnp.zeros_like(dk_sum)
        dv_sum[...] = jnp.zeros_like(dv_sum)

    rows = k_ref.shape[0]
    bias = key_bias(rows, image_rows, text_rows)
    queries = q_ref[...] * HEAD_DIM ** (-0.5)
    queries_t = queries.T
    grads = g_ref[...]
    grads_t = grads.T
    outs = []
    for head in range(heads):
        span = slice(head * HEAD_DIM, (head + 1) * HEAD_DIM)
        scores = dot(k_ref[:, span], queries_t[span]) + bias
        prob = jnp.exp(scores - lse_ref[head : head + 1])
        grad_prob = dot(v_ref[:, span], grads_t[span])
        weighted = prob * grad_prob
        inner = jnp.sum(weighted, axis=0, keepdims=True)
        grad_score = (weighted - prob * inner).astype(BF16)
        dv_sum[head] += dot(prob.astype(BF16), grads[:, span])
        dk_sum[head] += dot(grad_score, queries[:, span])
        outs.append(dot(kt_ref[span], grad_score) * HEAD_DIM ** (-0.5))
    dq_ref[...] = jnp.concatenate(outs, 0).T.astype(BF16)

    @pl.when(step == pl.num_programs(0) - 1)
    def _():
        dk_ref[...] = jnp.concatenate([dk_sum[head] for head in range(heads)], 1).astype(BF16)
        dv_ref[...] = jnp.concatenate([dv_sum[head] for head in range(heads)], 1).astype(BF16)


def attend_backward(q, k, v, grad, lse, image_rows, text_rows):
    rows, wide = q.shape
    heads = wide // HEAD_DIM
    whole = pl.BlockSpec((rows, wide), lambda i: (0, 0))
    block = pl.BlockSpec((QUERY_BLOCK, wide), lambda i: (i, 0))
    return pl.pallas_call(
        functools.partial(attend_backward_kernel, heads, image_rows, text_rows),
        grid=(rows // QUERY_BLOCK,),
        in_specs=[block, whole, whole, block, pl.BlockSpec((heads, QUERY_BLOCK), lambda i: (0, i))],
        out_specs=[block, whole, whole],
        out_shape=[jax.ShapeDtypeStruct((rows, wide), BF16)] * 3,
        scratch_shapes=[
            pltpu.VMEM((wide, rows), BF16),
            pltpu.VMEM((heads, rows, HEAD_DIM), F32),
            pltpu.VMEM((heads, rows, HEAD_DIM), F32),
        ],
        compiler_params=pltpu.CompilerParams(vmem_limit_bytes=VMEM_LIMIT),
        cost_estimate=pl.CostEstimate(
            flops=10 * rows * rows * wide, bytes_accessed=14 * rows * wide, transcendentals=heads * rows * rows
        ),
        name="attend_backward",
    )(q, k, v, grad, lse)


def normalise(inputs):
    centred = inputs - jnp.mean(inputs, axis=-1, keepdims=True)
    spread = lax.rsqrt(jnp.mean(centred * centred, axis=-1, keepdims=True) + 1e-06)
    return centred * spread, spread


def normalise_back(grad_norm, norm, spread):
    return spread * (
        grad_norm
        - jnp.mean(grad_norm, axis=-1, keepdims=True)
        - norm * jnp.mean(grad_norm * norm, axis=-1, keepdims=True)
    )


def gelu_parts(hidden):
    root = 0.7978845608028654
    square = hidden * hidden
    bent = jnp.tanh(hidden * (root + root * 0.044715 * square))
    half = 0.5 * (1.0 + bent)
    slope = half + 0.5 * hidden * (1.0 - bent * bent) * (root + 3.0 * root * 0.044715 * square)
    return hidden * half, slope


def plane_scatter(partial_image, partial_text):
    return tuple(
        lax.psum_scatter(part, PLANE, scatter_dimension=0, tiled=True).astype(F32)
        for part in (partial_image, partial_text)
    )


def plane_gather(own_image, own_text):
    return tuple(lax.all_gather(part, PLANE, axis=0, tiled=True) for part in (own_image, own_text))


def gather_rows(shard):
    mixed = lax.all_to_all(shard, "ctx", split_axis=2, concat_axis=1, tiled=True)[:, :, 0]
    return lax.all_gather(mixed, "dp", axis=1, tiled=True)


def scatter_rows(grad):
    mine = lax.psum_scatter(grad.astype(BF16), "dp", scatter_dimension=1, tiled=True)
    streams, rows, half = mine.shape
    ctx_n = lax.axis_size("ctx")
    split = mine.reshape(streams, ctx_n, rows // ctx_n, 1, half)
    both = lax.all_to_all(split, "ctx", split_axis=1, concat_axis=3, tiled=True)[:, 0]
    return both.astype(F32)


def on_device(
    image_tokens,
    text_tokens,
    conditioning,
    ada_weight,
    ada_bias,
    qkv_weight,
    qv_bias,
    out_weight,
    out_bias,
    up_weight,
    up_bias,
    down_weight,
    down_bias,
    image_cotangent,
    text_cotangent,
):
    ctx_n, tp_n, dp_n = lax.axis_size("ctx"), lax.axis_size("tp"), lax.axis_size("dp")
    dp, ctx, tp = lax.axis_index("dp"), lax.axis_index("ctx"), lax.axis_index("tp")
    image_length, text_length, width = image_tokens.shape[1], text_tokens.shape[1], image_tokens.shape[2]
    slice_width = qkv_weight.shape[3]
    shard_rows = qkv_weight.shape[1]
    half = slice_width // ctx_n
    up_half = up_weight.shape[2] // ctx_n
    image_own, text_own = image_length // tp_n, TEXT_SLOTS // tp_n
    image_all = image_length * ctx_n
    pad = ((0, TEXT_SLOTS - text_length), (0, 0))

    cond_float = conditioning.astype(F32)
    activated_low = jax.nn.silu(cond_float).astype(BF16)
    partial_mod = jnp.einsum("nd,adkf->nakf", activated_low, ada_weight, preferred_element_type=F32)
    mod_slices = lax.psum(partial_mod, ("dp", "ctx")) + ada_bias.astype(F32)
    own_slices = lax.dynamic_slice_in_dim(mod_slices, dp, 1, 0)[0]
    modulation = lax.all_gather(own_slices, "tp", axis=2, tiled=True)

    qkv_full = gather_rows(
        qkv_weight.reshape(2, shard_rows, 3, ctx_n, half)
        .transpose(0, 1, 3, 2, 4)
        .reshape(2, shard_rows, ctx_n, 3 * half)
    )
    out_full = gather_rows(out_weight.reshape(2, shard_rows, ctx_n, half))
    up_full = gather_rows(up_weight.reshape(2, shard_rows, ctx_n, up_half))
    down_full = gather_rows(down_weight.reshape(2, shard_rows, ctx_n, up_half))
    biases = lax.all_gather(
        jnp.concatenate([out_bias, down_bias], 0).astype(F32), ("dp", "ctx"), axis=1, tiled=True
    )
    out_bias_full, down_bias_full = biases[:2], biases[2:]
    qv_own = lax.dynamic_slice_in_dim(qv_bias, ctx * half, half, 2).astype(F32)
    up_bias_own = lax.dynamic_slice_in_dim(up_bias, ctx * up_half, up_half, 1).astype(F32)

    tokens = (image_tokens[0], jnp.pad(text_tokens[0], pad))
    cotangents = (image_cotangent[0], jnp.pad(text_cotangent[0], pad))
    tokens_all = [lax.all_gather(part, "ctx", axis=0, tiled=True) for part in tokens]
    cotangents_all = [lax.all_gather(part, "ctx", axis=0, tiled=True) for part in cotangents]
    own_rows = (image_own, text_own)

    def own(parts):
        return [
            lax.dynamic_slice_in_dim(part, tp * rows, rows, 0).astype(F32)
            for part, rows in zip(parts, own_rows)
        ]

    tokens_own, cotangents_own = own(tokens), own(cotangents)
    text_valid = (tp * text_own + lax.broadcasted_iota(jnp.int32, (text_own, 1), 0)) < text_length
    valid = (jnp.ones((image_own, 1), F32), text_valid.astype(F32))

    normed_low, qkv_parts = [], []
    for stream in range(2):
        norm, _ = normalise(tokens_all[stream].astype(F32))
        normed = (norm * (1.0 + modulation[stream, 1]) + modulation[stream, 0]).astype(BF16)
        normed_low.append(normed)
        bias = jnp.concatenate([qv_own[stream, 0], jnp.zeros((half,), F32), qv_own[stream, 1]])
        qkv_parts.append((dot(normed, qkv_full[stream]) + bias).astype(BF16))
    joint = jnp.concatenate(qkv_parts, 0)
    queries, keys, values = joint[:, :half], joint[:, half : 2 * half], joint[:, 2 * half :]
    blended, lse = attend_forward(queries, keys, values, image_all, text_length)
    blended_parts = (blended[:image_all], blended[image_all:])
    attention_own = plane_scatter(
        *[dot(blended_parts[s], out_full[s], ((1,), (1,))).astype(BF16) for s in range(2)]
    )
    attention, middles, norms2, spreads2, second_own = [], [], [], [], []
    for stream in range(2):
        branch = attention_own[stream] + out_bias_full[stream]
        middle = tokens_own[stream] + modulation[stream, 2] * branch
        norm, spread = normalise(middle)
        attention.append(branch)
        middles.append(middle)
        norms2.append(norm)
        spreads2.append(spread)
        second_own.append((norm * (1.0 + modulation[stream, 4]) + modulation[stream, 3]).astype(BF16))
    second_low = plane_gather(*second_own)

    feed_parts, second_parts = [], []
    down_weight_grads, up_weight_grads, down_bias_grads, up_bias_grads = [], [], [], []
    for stream in range(2):
        hidden = dot(second_low[stream], up_full[stream]) + up_bias_own[stream]
        gelu_out, slope = gelu_parts(hidden)
        gelu_low = gelu_out.astype(BF16)
        feed_parts.append(dot(gelu_low, down_full[stream], ((1,), (1,))).astype(BF16))
        grad_feed = (cotangents_all[stream].astype(F32) * modulation[stream, 5]).astype(BF16)
        down_weight_grads.append(dot(grad_feed, gelu_low, ((0,), (0,))))
        grad_hidden = (dot(grad_feed, down_full[stream]) * slope).astype(BF16)
        up_bias_grads.append(jnp.sum(grad_hidden.astype(F32), axis=0))
        up_weight_grads.append(dot(second_low[stream], grad_hidden, ((0,), (0,))))
        second_parts.append(dot(grad_hidden, up_full[stream], ((1,), (1,))).astype(BF16))
        own_feed = (cotangents[stream].astype(F32) * modulation[stream, 5]).astype(BF16)
        down_bias_grads.append(jnp.sum(own_feed.astype(F32), axis=0))
    feed_own = plane_scatter(*feed_parts)
    grad_second = plane_scatter(*second_parts)
    down_weight_grad = scatter_rows(jnp.stack(down_weight_grads)).reshape(2, shard_rows, -1)
    up_weight_grad = scatter_rows(jnp.stack(up_weight_grads)).reshape(2, shard_rows, -1)

    outputs, squares, mod_grads, grad_middles, attention_grads, out_bias_grads = [], [], [], [], [], []
    for stream in range(2):
        feed = feed_own[stream] + down_bias_full[stream]
        gated_attention = modulation[stream, 2] * attention[stream]
        gated_feed = modulation[stream, 5] * feed
        result = middles[stream] + gated_feed
        outputs.append(result.astype(BF16))
        squares.append(
            [jnp.sum(part * part * valid[stream]) for part in (result, gated_attention, gated_feed)]
        )
        grad_scaled = grad_second[stream] * (1.0 + modulation[stream, 4])
        grad_middle = cotangents_own[stream] + normalise_back(grad_scaled, norms2[stream], spreads2[stream])
        grad_attention = (grad_middle * modulation[stream, 2]).astype(BF16)
        grad_middles.append(grad_middle)
        attention_grads.append(grad_attention)
        out_bias_grads.append(jnp.sum(grad_attention.astype(F32), axis=0))
        mod_grads.append(
            [
                jnp.sum(grad_middle * attention[stream], axis=0),
                jnp.sum(grad_second[stream], axis=0),
                jnp.sum(grad_second[stream] * norms2[stream], axis=0),
                jnp.sum(cotangents_own[stream] * feed, axis=0),
            ]
        )
    attention_grad_all = plane_gather(*attention_grads)

    out_weight_grads, blended_grads = [], []
    for stream in range(2):
        out_weight_grads.append(dot(attention_grad_all[stream], blended_parts[stream], ((0,), (0,))))
        blended_grads.append(dot(attention_grad_all[stream], out_full[stream]).astype(BF16))
    grad_queries, grad_keys, grad_values = attend_backward(
        queries, keys, values, jnp.concatenate(blended_grads, 0), lse, image_all, text_length
    )
    grad_joint = jnp.concatenate([grad_queries, grad_keys, grad_values], 1)
    grad_parts = (grad_joint[:image_all], grad_joint[image_all:])
    qkv_weight_grads, qv_bias_grads, normed_parts = [], [], []
    for stream in range(2):
        sums = jnp.sum(grad_parts[stream].astype(F32), axis=0)
        qv_bias_grads.append(jnp.stack([sums[:half], sums[2 * half :]]))
        qkv_weight_grads.append(dot(normed_low[stream], grad_parts[stream], ((0,), (0,))))
        normed_parts.append(dot(grad_parts[stream], qkv_full[stream], ((1,), (1,))).astype(BF16))
    grad_normed = plane_scatter(*normed_parts)
    out_weight_grad = scatter_rows(jnp.stack(out_weight_grads)).reshape(2, shard_rows, -1)
    qkv_weight_grad = (
        scatter_rows(jnp.stack(qkv_weight_grads))
        .reshape(2, shard_rows, ctx_n, 3, half)
        .transpose(0, 1, 3, 2, 4)
        .reshape(2, shard_rows, 3, slice_width)
    )

    token_grads, mod_streams = [], []
    for stream in range(2):
        norm, spread = normalise(tokens_own[stream])
        grad_scaled = grad_normed[stream] * (1.0 + modulation[stream, 1])
        grad_tokens = grad_middles[stream] + normalise_back(grad_scaled, norm, spread)
        token_grads.append(grad_tokens.astype(BF16))
        mod_streams.append(
            jnp.stack(
                [jnp.sum(grad_normed[stream], axis=0), jnp.sum(grad_normed[stream] * norm, axis=0)]
                + mod_grads[stream]
            )
        )
    finals = [
        lax.all_gather(part, "tp", axis=0, tiled=True) for part in (*outputs, *token_grads)
    ]
    grad_mod = lax.psum_scatter(jnp.stack(mod_streams), "tp", scatter_dimension=2, tiled=True)
    grad_mod = lax.psum(grad_mod, "ctx")
    grad_mod_low = lax.all_gather(grad_mod, "dp", axis=0).astype(BF16)
    ada_bias_grad = jnp.sum(grad_mod_low.astype(F32), axis=0)
    ada_weight_grad = jnp.einsum("nd,nakf->adkf", activated_low, grad_mod_low, preferred_element_type=F32)
    cond_partial = jnp.einsum("nakf,adkf->nd", grad_mod_low, ada_weight, preferred_element_type=F32)
    cond_total = lax.psum(cond_partial, "tp")
    cond_grad = jax.vjp(jax.nn.silu, cond_float)[1](cond_total)[0]

    bias_rows = lax.psum_scatter(
        jnp.concatenate(
            [jnp.stack(down_bias_grads) * (tp == 0).astype(F32), jnp.stack(out_bias_grads)], 0
        ),
        ("dp", "ctx"),
        scatter_dimension=1,
        tiled=True,
    )
    bias_rows = lax.psum(bias_rows, "tp")
    qv_local = lax.dynamic_update_slice_in_dim(
        jnp.zeros((2, 2, slice_width), F32), jnp.stack(qv_bias_grads), ctx * half, 2
    )
    up_local = lax.dynamic_update_slice_in_dim(
        jnp.zeros((2, up_bias.shape[1]), F32), jnp.stack(up_bias_grads), ctx * up_half, 1
    )
    qv_bias_grad, up_bias_grad = lax.psum((qv_local, up_local), ("dp", "ctx"))
    squares_local = jnp.stack([squares[s][term] for term in range(3) for s in range(2)])
    squares_total = lax.psum(squares_local, ("dp", "ctx", "tp"))
    counts = jnp.array([image_length, text_length] * 3, F32) * (dp_n * ctx_n * width)
    root_means = jnp.sqrt(squares_total / counts)
    return (
        finals[0][None],
        finals[1][None, :text_length],
        finals[2][None],
        finals[3][None, :text_length],
        cond_grad,
        ada_weight_grad,
        ada_bias_grad,
        qkv_weight_grad,
        qv_bias_grad,
        out_weight_grad,
        bias_rows[2:],
        up_weight_grad,
        up_bias_grad,
        down_weight_grad,
        bias_rows[:2],
        root_means,
    )


def solution(mesh):
    rows = P(None, ("dp", "ctx"))
    tokens = P("dp", "ctx", None)
    stacked = P(None, ("dp", "ctx"), None, "tp")
    matrix = P(None, ("dp", "ctx"), "tp")
    return jax.shard_map(
        on_device,
        mesh=mesh,
        in_specs=(
            tokens,
            tokens,
            rows,
            stacked,
            P(None, None, "tp"),
            stacked,
            P(None, None, "tp"),
            matrix,
            rows,
            matrix,
            P(None, "tp"),
            matrix,
            rows,
            tokens,
            tokens,
        ),
        out_specs=(
            tokens,
            tokens,
            tokens,
            tokens,
            rows,
            stacked,
            P(None, None, "tp"),
            stacked,
            P(None, None, "tp"),
            matrix,
            rows,
            matrix,
            P(None, "tp"),
            matrix,
            rows,
            P(),
        ),
        check_vma=False,
    )
```

time: 2740 us -> 1260 us (0.46)
  waiting for transfers between devices: 1600 us -> 607 us
  blocking collectives: 820 us -> 285 us
  local copies, waits for them, and re-layouts: 70.1 us -> 131 us
  matrix products: 131 us -> 96.4 us
  Pallas kernels: 0 us -> 33.4 us
  other arithmetic: 98.8 us -> 65.7 us
    reduce_scatter x4 -> x10, waiting for transfers between devices: 913 us -> 254 us  [the longest x8 133 us: plane_scatter(): lax.psum_scatter(part, PLANE, scatter_dimension=0, tiled=True).astype(F32)]
    unnamed x1 -> x0, blocking collectives: 654 us -> none
    psum x4 -> x1, waiting for transfers between devices: 303 us -> 99 us  [on_device(): mod_slices = lax.psum(partial_mod, ('dp', 'ctx')) + ada_bias.astype(F32)]
    all_gather x4 -> x10, waiting for transfers between devices: 369 us -> 214 us  [the longest x4 126 us: gather_rows(): return lax.all_gather(mixed, 'dp', axis=1, tiled=True)]
    psum x0 -> x2, blocking collectives: none -> 57.8 us  [the longest x1 50.7 us: on_device(): squares_total = lax.psum(squares_local, ('dp', 'ctx', 'tp'))]
    all_to_all x0 -> x3, blocking collectives: none -> 57.6 us  [gather_rows(): lax.all_to_all(shard, 'ctx', split_axis=2, concat_axis=1, tiled=True)]
    unnamed x260 -> x168, local copies, waits for them, and re-layouts: 24.1 us -> 62.1 us
    dot_general x30 -> x24, matrix products: 127 us -> 91.7 us  [dot(): lax.dot_general(left, right, (dims, ((), ())), preferred_element_type=F32)]
  transfers between devices with their start and end apart: 14 -> 30, of which waited for: 12 -> 17; matrix products, arithmetic and copies ran while one was open for 7% -> 20% of each run, Pallas kernels for 0% -> 1%
where the time goes in v1:
time: 1260 us
  waiting for transfers between devices  607 us (48%)
  blocking collectives  285 us (23%)
  local copies, waits for them, and re-layouts  131 us (10%)
  matrix products  96.4 us (8%)
  other arithmetic  65.7 us (5%)
  Pallas kernels  33.4 us (3%)
  starting transfers between devices  21.6 us (2%)
  between operations  17.5 us (1%)
    reduce_scatter x8, waiting for transfers between devices, plane_scatter(): lax.psum_scatter(part, PLANE, scatter_dimension=0, tiled=True).astype(F32)  133 us
    all_gather x4, waiting for transfers between devices, gather_rows(): return lax.all_gather(mixed, 'dp', axis=1, tiled=True)  126 us
    reduce_scatter x2, waiting for transfers between devices, scatter_rows(): lax.psum_scatter(grad.astype(BF16), 'dp', scatter_dimension=1, tiled=True)  121 us
    psum x1, waiting for transfers between devices, on_device(): mod_slices = lax.psum(partial_mod, ('dp', 'ctx')) + ada_bias.astype(F32)  99 us
    dot_general x24, matrix products, dot(): lax.dot_general(left, right, (dims, ((), ())), preferred_element_type=F32)  91.7 us
    unnamed x168, local copies, waits for them, and re-layouts  62.1 us
    all_to_all x3, blocking collectives, gather_rows(): lax.all_to_all(shard, 'ctx', split_axis=2, concat_axis=1, tiled=True)  57.6 us
    psum x1, blocking collectives, on_device(): squares_total = lax.psum(squares_local, ('dp', 'ctx', 'tp'))  50.7 us
  transfers between devices with their start and end apart: 30, of which 17 were waited for; matrix products, arithmetic and copies ran while one was open for 20% of the time, Pallas kernels for 1%

profile of v1, /device:TPU:0, one launch (start us, length us, event | category | flops | bytes accessed | tf_op | source)
XLA Modules:
  0.0 1257.3 jit_solution(14620419210907155854)
XLA Ops:
  17.5 27.7 %all_to_all.96 = bf16[2,192,2,576]{3,1,0,2:T(8,128)(2,1)S(1)} all-to-all(bf16[2,192,2,576]{3,1,0,2:T(8,128)(2,1)} %copy.149), channel_id=1, replica_groups=mesh['dp'=4,'ctx'=2,'tp'=4] {'ctx'}, dimensions={2} | all-to-all | bytes 1769472 | tf_op jit(solution)/shard_map/all_to_all | solution.py:168
  51.4 27.6 %all_gather.63 = bf16[256,1536]{1,0:T(8,128)(2,1)S(1)} all-gather(bf16[128,1536]{1,0:T(8,128)(2,1)S(1)} %pad.7), channel_id=1, replica_groups=mesh['dp'=4,'ctx'=2,'tp'=4] {'ctx'}, dimensions={0}, use_global_device_ids=true | all-gather | bytes 1179648 | tf_op jit(solution)/shard_map/all_gather | solution.py:233
  79.6 99.0 %all-reduce.6.cloned.1.call-done = f32[4,2,6,384]{3,0,2,1:T(4,128)} async-done(((f32[4,2,6,384]{3,0,2,1:T(4,128)}), f32[4,2,6,384]{3,0,2,1:T(4,128)}) %all-reduce.6.cloned.1.call-update) | async-done | bytes 73744 | tf_op jit(solution)/shard_map/psum | solution.py:212
  179.5 5.3 all-gather
  201.3 14.7 %attend_forward.1 = (bf16[1280,192]{1,0:T(8,128)(2,1)}, f32[3,1280]{1,0:T(4,128)}) custom-call(bf16[1280,192]{1,0:T(8,128)(2,1)} %get-tuple-element.135.q_ref, bf16[1280,192]{1,0:T(8,128)(2,1)} %get-tuple-element.136.k_ref, bf16[1280,192]{1,0:T(8,128)(2,1)} %get-tuple-element.134.v_ref), custom_call_target="tpu_custom_call" | custom-call | flops 1258291200 | bytes 1966080 | tf_op jit(solution)/shard_map/attend_forward/pallas_call | solution.py:54
  224.2 17.3 %all_to_all.97 = bf16[2,192,2,768]{3,1,0,2:T(8,128)(2,1)S(1)} all-to-all(bf16[2,192,2,768]{3,1,0,2:T(8,128)(2,1)S(1)} %bitcast.310), channel_id=1, replica_groups=mesh['dp'=4,'ctx'=2,'tp'=4] {'ctx'}, dimensions={2} | all-to-all | bytes 2359296 | tf_op jit(solution)/shard_map/all_to_all | solution.py:168
  242.7 30.8 %all-gather.3 = f32[8,192,4]{1,2,0:T(4,128)S(1)} all-gather(f32[1,192,4]{1,2,0:T(4,128)S(1)} %convert_bitcast_fusion.5), channel_id=1, replica_groups=mesh['dp'=4,'ctx'=2,'tp'=4] {'dp','ctx'}, dimensions={0}, use_global_device_ids=true | all-gather | bytes 27648 | tf_op jit(solution)/shard_map/all_gather | solution.py:224
  282.1 12.6 all_to_all.98
  299.2 31.9 %all-gather.21.cloned.1.call-done = bf16[2,1536,768]{2,1,0:T(8,128)(2,1)} async-done(((bf16[2,384,768]{2,1,0:T(8,128)(2,1)}), bf16[2,1536,768]{2,1,0:T(8,128)(2,1)}) %all-gather.21.cloned.1.call-update) | async-done | bytes 4718608 | tf_op jit(solution)/shard_map/all_gather | solution.py:169
  331.0 33.4 %all-gather.19.cloned.1.call-done = bf16[1024,1536]{1,0:T(8,128)(2,1)} async-done(((bf16[128,1536]{1,0:T(8,128)(2,1)}), bf16[1024,1536]{1,0:T(8,128)(2,1)}) %all-gather.19.cloned.1.call-update) | async-done | bytes 3145744 | tf_op jit(solution)/shard_map/all_gather | solution.py:164
  364.5 6.9 fusion.20
  371.4 39.6 %all-gather.33.cloned.1.call-done = bf16[1,1024,1536]{2,1,0:T(8,128)(2,1)} async-done(((bf16[1,512,1536]{2,1,0:T(8,128)(2,1)}), bf16[1,1024,1536]{2,1,0:T(8,128)(2,1)}) %all-gather.33.cloned.1.call-update) | async-done | bytes 3145744 | tf_op jit(solution)/shard_map/all_gather | solution.py:234
  410.9 91.4 %all-gather.23.cloned.1.call-done = bf16[2,1536,768]{2,1,0:T(8,128)(2,1)} async-done(((bf16[2,384,768]{2,1,0:T(8,128)(2,1)}), bf16[2,1536,768]{2,1,0:T(8,128)(2,1)}) %all-gather.23.cloned.1.call-update) | async-done | bytes 4718608 | tf_op jit(solution)/shard_map/all_gather | solution.py:169
  502.3 8.1 convert_reduce_fusion.1
  515.7 7.2 convolution_convert_fusion.3
  523.9 11.7 all_gather.74
  539.6 11.6 all_gather.70
  566.9 46.1 %reduce-scatter.25.cloned.1.call-done = bf16[128,1536]{1,0:T(8,128)(2,1)} async-done(((bf16[1024,1536]{1,0:T(8,128)(2,1)}), bf16[128,1536]{1,0:T(8,128)(2,1)}) %reduce-scatter.25.cloned.1.call-update) | async-done | bytes 393232 | tf_op jit(solution)/shard_map/reduce_scatter | solution.py:158
  621.8 30.0 %reduce-scatter.33.cloned.1.call-done = bf16[32,1536]{1,0:T(8,128)(2,1)} async-done(((bf16[256,1536]{1,0:T(8,128)(2,1)}), bf16[32,1536]{1,0:T(8,128)(2,1)}) %reduce-scatter.33.cloned.1.call-update) | async-done | bytes 98320 | tf_op jit(solution)/shard_map/reduce_scatter | solution.py:158
  651.8 39.0 %reduce-scatter.29.cloned.1.call-done = bf16[32,1536]{1,0:T(8,128)(2,1)} async-done(((bf16[256,1536]{1,0:T(8,128)(2,1)}), bf16[32,1536]{1,0:T(8,128)(2,1)}) %reduce-scatter.29.cloned.1.call-update) | async-done | bytes 98320 | tf_op jit(solution)/shard_map/reduce_scatter | solution.py:158
  696.1 12.1 all_gather.75
  711.7 15.2 %all-gather.27.cloned.1.call-done = bf16[1024,1536]{1,0:T(8,128)(2,1)} async-done(((bf16[128,1536]{1,0:T(8,128)(2,1)}), bf16[1024,1536]{1,0:T(8,128)(2,1)}) %all-gather.27.cloned.1.call-update) | async-done | bytes 3145744 | tf_op jit(solution)/shard_map/all_gather | solution.py:164
  734.9 18.6 %attend_backward.1 = (bf16[1280,192]{1,0:T(8,128)(2,1)}, bf16[1280,192]{1,0:T(8,128)(2,1)}, bf16[1280,192]{1,0:T(8,128)(2,1)}) custom-call(bf16[1280,192]{1,0:T(8,128)(2,1)} %get-tuple-element.135.q_ref, bf16[1280,192]{1,0:T(8,128)(2,1)} %get-tuple-element.136.k_ref, bf16[1280,192]{1,0:T(8,128)(2,1)} %get-tuple-element.134.v_ref, ...), custom_call_target="tpu_custom_call" | custom-call | flops 3145728000 | bytes 3440640 | tf_op jit(solution)/shard_map/attend_backward/pallas_call | solution.py:114
  762.7 5.6 convolution_convert_fusion
  780.5 5.5 fusion.10
  803.7 5.0 copy.184
  808.7 4.6 reshape.294
  813.7 6.0 fusion.14
  826.1 18.2 %reduce-scatter.35.cloned.1.call-done = bf16[128,1536]{1,0:T(8,128)(2,1)} async-done(((bf16[1024,1536]{1,0:T(8,128)(2,1)}), bf16[128,1536]{1,0:T(8,128)(2,1)}) %reduce-scatter.35.cloned.1.call-update) | async-done | bytes 393232 | tf_op jit(solution)/shard_map/reduce_scatter | solution.py:158
  853.2 4.9 reshape.290
  862.3 10.6 copy.182
  873.0 8.6 reshape.292
  882.3 49.6 %reduce-scatter.39.cloned.1.call-done = bf16[2,384,768]{2,1,0:T(8,128)(2,1)} async-done(((bf16[2,1536,768]{2,1,0:T(8,128)(2,1)}), bf16[2,384,768]{2,1,0:T(8,128)(2,1)}) %reduce-scatter.39.cloned.1.call-update) | async-done | bytes 1179664 | tf_op jit(solution)/shard_map/reduce_scatter | solution.py:173
  937.9 6.4 all_gather.71
  948.8 71.1 %reduce-scatter.41.cloned.1.call-done = bf16[2,384,768]{2,1,0:T(8,128)(2,1)} async-done(((bf16[2,1536,768]{2,1,0:T(8,128)(2,1)}), bf16[2,384,768]{2,1,0:T(8,128)(2,1)}) %reduce-scatter.41.cloned.1.call-update) | async-done | bytes 1179664 | tf_op jit(solution)/shard_map/reduce_scatter | solution.py:173
  1022.2 4.5 all-to-all-start.7
  1026.8 50.7 %psum.55 = f32[6]{0:T(128)S(1)} all-reduce(f32[6]{0:T(128)S(1)} %stack.223), channel_id=1, replica_groups=mesh['dp'=4,'ctx'=2,'tp'=4] {'dp','ctx','tp'}, use_global_device_ids=true, to_apply=%region_67.68 | all-reduce | flops 6 | bytes 48 | tf_op jit(solution)/shard_map/psum | solution.py:384
  1078.0 8.1 reduce-scatter.49.cloned.1.call-done
  1105.4 36.5 %all-reduce.2 = (f32[2,2,384]{2,1,0:T(2,128)}, f32[2,1536]{1,0:T(2,128)}) all-reduce(f32[2,2,384]{2,1,0:T(2,128)S(1)} %dynamic_update_slice.6, f32[2,1536]{1,0:T(2,128)S(1)} %maximum_dynamic-update-slice_fusion), channel_id=1, replica_groups=mesh['dp'=4,'ctx'=2,'tp'=4] {'dp','ctx'}, use_global_device_ids=true, to_apply=%region_48.49 | all-reduce | flops 4608 | bytes 36864 | tf_op jit(solution)/shard_map/psum | solution.py:382
  1141.9 6.3 all_gather.77
  1154.7 6.6 all-to-all-done.5
  1169.4 7.1 psum.50
  1176.5 15.1 %all_gather.79 = bf16[4,2,6,384]{3,1,2,0:T(2,128)(2,1)S(1)} all-gather(bf16[1,2,6,384]{3,1,2,0:T(2,128)(2,1)S(1)} %psum.50), channel_id=1, replica_groups=mesh['dp'=4,'ctx'=2,'tp'=4] {'dp'}, dimensions={0}, use_global_device_ids=true | all-gather | bytes 46080 | tf_op jit(solution)/shard_map/all_gather | solution.py:360
  1192.8 6.5 all-reduce.3
  1199.9 12.6 %reduce-scatter.45.cloned.1.call-done = bf16[384,1152]{1,0:T(8,128)(2,1)} async-done(((bf16[1536,1152]{1,0:T(8,128)(2,1)}), bf16[384,1152]{1,0:T(8,128)(2,1)}) %reduce-scatter.45.cloned.1.call-update) | async-done | bytes 884752
  1216.4 4.4 all-to-all-start.4
  1223.9 10.0 all-to-all-done.4
  1237.1 4.4 copy.168
  (388 shorter events, 232.9 us)
Async XLA Ops:
  8.0 170.5 %all-reduce.6.cloned.1.call-start = ((), (), s32[]{:S(2)}) async-start(), calls=%async_computation.22 | async-start | bytes 147456 | tf_op jit(solution)/shard_map/psum | solution.py:212
  11.2 177.8 %all-gather.31.cloned.1.call-start = ((), (), s32[]{:S(2)}) async-start(), calls=%async_computation.41 | async-start | bytes 4718592 | tf_op jit(solution)/shard_map/all_gather | solution.py:233
  11.8 181.1 %all-gather.15.cloned.1.call-start = ((), (), s32[]{:S(2)}) async-start(), calls=%async_computation.23 | async-start | bytes 4915200 | tf_op jit(solution)/shard_map/all_gather | solution.py:169
  17.5 28.8 %copy-start.24 = (bf16[2,192,384]{2,1,0:T(8,128)(2,1)S(1)}, bf16[2,192,384]{2,1,0:T(8,128)(2,1)}, u32[]{:S(2)}) copy-start(bf16[2,192,384]{2,1,0:T(8,128)(2,1)} %param.23) | copy-start | bytes 884740
  47.6 137.9 %all-to-all-start.1 = ((bf16[2,192,2,192]{1,3,0,2:T(8,128)(2,1)}), bf16[2,192,2,192]{1,3,0,2:T(8,128)(2,1)S(1)}, u32[]{:S(2)}, u32[]{:S(2)}) async-start(bf16[2,192,2,192]{1,3,0,2:T(8,128)(2,1)} %copy.155), calls=%async_computation.1 | async-start | bytes 786432 | tf_op jit(solution)/shard_map/all_to_all | solution.py:168
  51.1 167.8 %all-gather.17.cloned.1.call-start = ((), (), s32[]{:S(2)}) async-start(), calls=%async_computation.24 | async-start | bytes 1474560 | tf_op jit(solution)/shard_map/all_gather | solution.py:169
  79.2 113.6 %copy-start.53 = (f32[256]{0:T(256)}, f32[256]{0:T(256)S(1)}, u32[]{:S(2)}) copy-start(f32[256]{0:T(256)S(1)} %broadcast_multiply_fusion.1) | copy-start | bytes 3076
  79.6 113.3 %copy-start.63 = (f32[256]{0:T(256)}, f32[256]{0:T(256)S(1)}, u32[]{:S(2)}) copy-start(f32[256]{0:T(256)S(1)} %add_rsqrt_fusion.1) | copy-start | bytes 3076
  185.5 92.2 %copy-start.22 = (f32[1536]{0:T(1024)}, f32[1536]{0:T(1024)S(1)}, u32[]{:S(2)}) copy-start(f32[1536]{0:T(1024)S(1)} %get-tuple-element.114) | copy-start | bytes 18436
  185.5 92.2 %copy-start.28 = (f32[1536]{0:T(1024)}, f32[1536]{0:T(1024)S(1)}, u32[]{:S(2)}) copy-start(f32[1536]{0:T(1024)S(1)} %get-tuple-element.108) | copy-start | bytes 18436
  185.5 316.8 %copy-start.26 = (f32[1536]{0:T(1024)}, f32[1536]{0:T(1024)S(1)}, u32[]{:S(2)}) copy-start(f32[1536]{0:T(1024)S(1)} %get-tuple-element.109) | copy-start | bytes 18436
  185.6 351.2 %copy-start.23 = (f32[1536]{0:T(1024)}, f32[1536]{0:T(1024)S(1)}, u32[]{:S(2)}) copy-start(f32[1536]{0:T(1024)S(1)} %get-tuple-element.106) | copy-start | bytes 18436
  188.7 85.6 %reduce-scatter.23.cloned.1.call-start = ((), (), s32[]{:S(2)}) async-start(), calls=%async_computation.25 | async-start | bytes 3538944 | tf_op jit(solution)/shard_map/reduce_scatter | solution.py:158
  222.7 108.3 %all-gather.21.cloned.1.call-start = ((), (), s32[]{:S(2)}) async-start(), calls=%async_computation.27 | async-start | bytes 5898240 | tf_op jit(solution)/shard_map/all_gather | solution.py:169
  224.1 18.5 %copy-start.65 = (bf16[2,192]{1,0:T(2,128)(2,1)S(1)}, bf16[2,192]{1,0:T(2,128)(2,1)}, u32[]{:S(2)}) copy-start(bf16[2,192]{1,0:T(2,128)(2,1)} %param.28) | copy-start | bytes 2308
  224.2 18.5 %copy-start.66 = (bf16[2,192]{1,0:T(2,128)(2,1)S(1)}, bf16[2,192]{1,0:T(2,128)(2,1)}, u32[]{:S(2)}) copy-start(bf16[2,192]{1,0:T(2,128)(2,1)} %param.24) | copy-start | bytes 2308
  242.6 121.9 %all-gather.19.cloned.1.call-start = ((), (), s32[]{:S(2)}) async-start(), calls=%async_computation.26 | async-start | bytes 3538944 | tf_op jit(solution)/shard_map/all_gather | solution.py:164
  279.9 131.0 %all-gather.33.cloned.1.call-start = ((), (), s32[]{:S(2)}) async-start(), calls=%async_computation.42 | async-start | bytes 4718592 | tf_op jit(solution)/shard_map/all_gather | solution.py:234
  280.7 221.6 %all-gather.23.cloned.1.call-start = ((), (), s32[]{:S(2)}) async-start(), calls=%async_computation.28 | async-start | bytes 5898240 | tf_op jit(solution)/shard_map/all_gather | solution.py:169
  295.8 239.9 %reduce-scatter.27.cloned.1.call-start = ((), (), s32[]{:S(2)}) async-start(), calls=%async_computation.31 | async-start | bytes 884736 | tf_op jit(solution)/shard_map/reduce_scatter | solution.py:158
  296.5 219.2 %copy-start.55 = (f32[768]{0:T(1024)}, f32[768]{0:T(1024)S(1)}, u32[]{:S(2)}) copy-start(f32[768]{0:T(1024)S(1)} %get-tuple-element.120) | copy-start | bytes 9220
  298.9 268.0 %reduce-scatter.31.cloned.1.call-start = ((), (), s32[]{:S(2)}) async-start(), calls=%async_computation.33 | async-start | bytes 3538944 | tf_op jit(solution)/shard_map/reduce_scatter | solution.py:158
  515.6 97.3 %reduce-scatter.25.cloned.1.call-start = ((), (), s32[]{:S(2)}) async-start(), calls=%async_computation.29 | async-start | bytes 3538944 | tf_op jit(solution)/shard_map/reduce_scatter | solution.py:158
  522.9 128.9 %reduce-scatter.33.cloned.1.call-start = ((), (), s32[]{:S(2)}) async-start(), calls=%async_computation.35 | async-start | bytes 884736 | tf_op jit(solution)/shard_map/reduce_scatter | solution.py:158
  561.0 51.9 %copy-start.2 = (bf16[128,1536]{1,0:T(8,128)(2,1)S(1)}, bf16[128,1536]{1,0:T(8,128)(2,1)}, u32[]{:S(2)}) copy-start(bf16[128,1536]{1,0:T(8,128)(2,1)} %reduce-scatter.23.cloned.1.call-done) | copy-start | bytes 1179652
  561.0 129.8 %reduce-scatter.29.cloned.1.call-start = ((), (), s32[]{:S(2)}) async-start(), calls=%async_computation.32 | async-start | bytes 884736 | tf_op jit(solution)/shard_map/reduce_scatter | solution.py:158
  565.1 161.8 %all-gather.27.cloned.1.call-start = ((), (), s32[]{:S(2)}) async-start(), calls=%async_computation.34 | async-start | bytes 3538944 | tf_op jit(solution)/shard_map/all_gather | solution.py:164
  612.9 77.9 %copy-start.6 = (bf16[32,1536]{1,0:T(8,128)(2,1)S(1)}, bf16[32,1536]{1,0:T(8,128)(2,1)}, u32[]{:S(2)}) copy-start(bf16[32,1536]{1,0:T(8,128)(2,1)} %reduce-scatter.27.cloned.1.call-done) | copy-start | bytes 294916
  620.5 201.3 %reduce-scatter.37.cloned.1.call-start = ((), (), s32[]{:S(2)}) async-start(), calls=%async_computation.38 | async-start | bytes 884736 | tf_op jit(solution)/shard_map/reduce_scatter | solution.py:158
  690.8 18.2 %copy-start.13 = (bf16[2,1536,192]{1,2,0:T(8,128)(2,1)S(1)}, bf16[2,1536,192]{1,2,0:T(8,128)(2,1)}, u32[]{:S(2)}) copy-start(bf16[2,1536,192]{1,2,0:T(8,128)(2,1)} %all-gather.17.cloned.1.call-done) | copy-start | bytes 3538948
  759.3 85.0 %reduce-scatter.35.cloned.1.call-start = ((), (), s32[]{:S(2)}) async-start(), calls=%async_computation.36 | async-start | bytes 3538944 | tf_op jit(solution)/shard_map/reduce_scatter | solution.py:158
  768.3 163.5 %reduce-scatter.39.cloned.1.call-start = ((), (), s32[]{:S(2)}) async-start(), calls=%async_computation.39 | async-start | bytes 5898240 | tf_op jit(solution)/shard_map/reduce_scatter | solution.py:173
  777.9 242.0 %reduce-scatter.41.cloned.1.call-start = ((), (), s32[]{:S(2)}) async-start(), calls=%async_computation.40 | async-start | bytes 5898240 | tf_op jit(solution)/shard_map/reduce_scatter | solution.py:173
  788.6 297.5 %reduce-scatter.49.cloned.1.call-start = ((), (), s32[]{:S(2)}) async-start(), calls=%async_computation.46 | async-start | bytes 884736
  794.0 293.1 %all-gather.25.cloned.1.call-start = ((), (), s32[]{:S(2)}) async-start(), calls=%async_computation.30 | async-start | bytes 1966080 | tf_op jit(solution)/shard_map/all_gather | solution.py:356
  794.6 353.7 %reduce-scatter.47.cloned.1.call-start = ((), (), s32[]{:S(2)}) async-start(), calls=%async_computation.45 | async-start | bytes 1474560
  813.4 351.9 %reduce-scatter.43.cloned.1.call-start = ((), (), s32[]{:S(2)}) async-start(), calls=%async_computation.43 | async-start | bytes 983040
  821.7 24.1 %copy-start.9 = (f32[128,1536]{1,0:T(8,128)S(1)}, f32[128,1536]{1,0:T(8,128)}, u32[]{:S(2)}) copy-start(f32[128,1536]{1,0:T(8,128)} %get-tuple-element.139) | copy-start | bytes 2359300
  858.1 354.4 %reduce-scatter.45.cloned.1.call-start = ((), (), s32[]{:S(2)}) async-start(), calls=%async_computation.44 | async-start | bytes 4423680
  881.6 56.2 %copy-start.18 = (bf16[32,1536]{1,0:T(8,128)(2,1)S(1)}, bf16[32,1536]{1,0:T(8,128)(2,1)}, u32[]{:S(2)}) copy-start(bf16[32,1536]{1,0:T(8,128)(2,1)} %get-tuple-element.142) | copy-start | bytes 294916
  934.2 88.0 %all-to-all-start.6 = ((bf16[2,2,192,1,768]{4,2,0,3,1:T(8,128)(2,1)}), bf16[2,2,192,1,768]{4,2,0,3,1:T(8,128)(2,1)S(1)}, u32[]{:S(2)}, u32[]{:S(2)}) async-start(bf16[2,2,192,1,768]{4,2,0,3,1:T(8,128)(2,1)} %copy.171), calls=%async_computation.15 | async-start | bytes 2359296 | tf_op jit(solution)/shard_map/all_to_all | solution.py:177
  944.3 133.1 %copy-start.72 = (f32[6]{0:T(128)S(1)}, f32[6]{0:T(128)}, u32[]{:S(2)}) copy-start(f32[6]{0:T(128)} %constant.105) | copy-start | bytes 76
  1022.2 72.4 %all-to-all-start.7 = ((bf16[2,2,192,1,768]{4,2,0,3,1:T(8,128)(2,1)}), bf16[2,2,192,1,768]{4,2,0,3,1:T(8,128)(2,1)}, u32[]{:S(2)}, u32[]{:S(2)}) async-start(bf16[2,2,192,1,768]{4,2,0,3,1:T(8,128)(2,1)} %copy.173), calls=%async_computation.17 | async-start | bytes 2359296 | tf_op jit(solution)/shard_map/all_to_all | solution.py:177
  1026.7 197.2 %all-gather.29.cloned.1.call-start = ((), (), s32[]{:S(2)}) async-start(), calls=%async_computation.37 | async-start | bytes 1966080 | tf_op jit(solution)/shard_map/all_gather | solution.py:356
  1099.3 42.6 %copy-start.19 = (bf16[32,1536]{1,0:T(8,128)(2,1)S(1)}, bf16[32,1536]{1,0:T(8,128)(2,1)}, u32[]{:S(2)}) copy-start(bf16[32,1536]{1,0:T(8,128)(2,1)} %get-tuple-element.147) | copy-start | bytes 294916
  1150.5 10.8 all-to-all-start.5
  1165.2 34.1 %copy-start.39 = (bf16[4,192]{1,0:T(4,128)(2,1)S(1)}, bf16[4,192]{1,0:T(4,128)(2,1)}, u32[]{:S(2)}) copy-start(bf16[4,192]{1,0:T(4,128)(2,1)} %param.18) | copy-start | bytes 4612
  1216.4 17.5 %all-to-all-start.4 = ((bf16[2,2,192,1,576]{4,2,0,3,1:T(8,128)(2,1)}), bf16[2,2,192,1,576]{4,2,0,3,1:T(8,128)(2,1)}, u32[]{:S(2)}, u32[]{:S(2)}) async-start(bf16[2,2,192,1,576]{4,2,0,3,1:T(8,128)(2,1)} %copy.166), calls=%async_computation.12 | async-start | bytes 1966080 | tf_op jit(solution)/shard_map/all_to_all | solution.py:177
  (58 other events, 323.4 us)
Sparse Core Ops, SparseCore 0:
  12.9 165.6 all-reduce.5
  222.9 45.8 reduce-scatter.22
  300.7 34.6 reduce-scatter.26
  515.8 47.6 reduce-scatter.30
  566.7 46.1 reduce-scatter.24
  616.8 34.9 reduce-scatter.32
  655.9 34.9 reduce-scatter.28
  693.5 33.4 all-gather.26
  759.4 34.9 reduce-scatter.36
  798.0 46.2 reduce-scatter.34
  846.6 85.2 reduce-scatter.38
  934.0 85.7 reduce-scatter.40
  1023.1 62.8 reduce-scatter.48
  1088.9 28.4 reduce-scatter.46
  1120.0 21.9 reduce-scatter.42
  1144.7 67.7 reduce-scatter.44
Sparse Core Ops, SparseCore 1:
  13.2 68.9 all-gather.30
  84.2 77.2 all-gather.14
  188.8 30.0 all-gather.16
  242.7 88.3 all-gather.20
  333.7 30.7 all-gather.18
  366.1 44.7 all-gather.32
  413.0 89.2 all-gather.22
  796.1 19.5 all-gather.24
  1105.2 18.7 all-gather.28

commit v2 on v1

v2 whole, which is shorter than its diff:
```python
import functools

import jax
import jax.numpy as jnp
from jax import lax
from jax.experimental import pallas as pl
from jax.experimental.pallas import tpu as pltpu
from jax.sharding import PartitionSpec as P

HEAD_DIM = 64
F32 = jnp.float32
BF16 = jnp.bfloat16
VMEM_LIMIT = 60 * 1024 * 1024
PLANE = ("ctx", "tp")
TEXT_SLOTS = 96
JOINT_STEP = 256
QUERY_BLOCK = 256


def dot(left, right, dims=((1,), (0,))):
    return lax.dot_general(left, right, (dims, ((), ())), preferred_element_type=F32)


def key_bias(rows, image_rows, text_rows):
    slot = lax.broadcasted_iota(jnp.int32, (rows, 1), 0)
    text_slot = slot - image_rows
    unused = jnp.logical_or(lax.rem(text_slot, TEXT_SLOTS) >= text_rows, text_slot >= 2 * TEXT_SLOTS)
    masked = jnp.logical_and(text_slot >= 0, unused)
    return jnp.where(masked, -1e30, 0.0).astype(F32)


def attend_forward_kernel(heads, image_rows, text_rows, q_ref, k_ref, v_ref, o_ref, lse_ref, vt_ref):
    @pl.when(pl.program_id(0) == 0)
    def _():
        vt_ref[...] = v_ref[...].T

    rows = k_ref.shape[0]
    bias = key_bias(rows, image_rows, text_rows)
    queries_t = (q_ref[...] * HEAD_DIM ** (-0.5)).T
    outs = []
    for head in range(heads):
        span = slice(head * HEAD_DIM, (head + 1) * HEAD_DIM)
        scores = dot(k_ref[:, span], queries_t[span]) + bias
        top = jnp.max(scores, axis=0, keepdims=True)
        grown = jnp.exp(scores - top)
        total = jnp.sum(grown, axis=0, keepdims=True)
        lse_ref[head : head + 1] = top + jnp.log(total)
        outs.append(dot(vt_ref[span], grown.astype(BF16)) * (1.0 / total))
    o_ref[...] = jnp.concatenate(outs, 0).T.astype(BF16)


def attend_forward(q, k, v, image_rows, text_rows):
    rows, wide = q.shape
    heads = wide // HEAD_DIM
    whole = pl.BlockSpec((rows, wide), lambda i: (0, 0))
    block = pl.BlockSpec((QUERY_BLOCK, wide), lambda i: (i, 0))
    return pl.pallas_call(
        functools.partial(attend_forward_kernel, heads, image_rows, text_rows),
        grid=(rows // QUERY_BLOCK,),
        in_specs=[block, whole, whole],
        out_specs=[block, pl.BlockSpec((heads, QUERY_BLOCK), lambda i: (0, i))],
        out_shape=[
            jax.ShapeDtypeStruct((rows, wide), BF16),
            jax.ShapeDtypeStruct((heads, rows), F32),
        ],
        scratch_shapes=[pltpu.VMEM((wide, rows), BF16)],
        compiler_params=pltpu.CompilerParams(vmem_limit_bytes=VMEM_LIMIT),
        cost_estimate=pl.CostEstimate(
            flops=4 * rows * rows * wide, bytes_accessed=8 * rows * wide, transcendentals=heads * rows * rows
        ),
        name="attend_forward",
    )(q, k, v)


def attend_backward_kernel(
    heads, image_rows, text_rows, q_ref, k_ref, v_ref, g_ref, lse_ref, dq_ref, dk_ref, dv_ref, kt_ref, dk_sum, dv_sum
):
    step = pl.program_id(0)

    @pl.when(step == 0)
    def _():
        kt_ref[...] = k_ref[...].T
        dk_sum[...] = jnp.zeros_like(dk_sum)
        dv_sum[...] = jnp.zeros_like(dv_sum)

    rows = k_ref.shape[0]
    bias = key_bias(rows, image_rows, text_rows)
    queries = q_ref[...] * HEAD_DIM ** (-0.5)
    queries_t = queries.T
    grads = g_ref[...]
    grads_t = grads.T
    outs = []
    for head in range(heads):
        span = slice(head * HEAD_DIM, (head + 1) * HEAD_DIM)
        scores = dot(k_ref[:, span], queries_t[span]) + bias
        prob = jnp.exp(scores - lse_ref[head : head + 1])
        grad_prob = dot(v_ref[:, span], grads_t[span])
        weighted = prob * grad_prob
        inner = jnp.sum(weighted, axis=0, keepdims=True)
        grad_score = (weighted - prob * inner).astype(BF16)
        dv_sum[head] += dot(prob.astype(BF16), grads[:, span])
        dk_sum[head] += dot(grad_score, queries[:, span])
        outs.append(dot(kt_ref[span], grad_score) * HEAD_DIM ** (-0.5))
    dq_ref[...] = jnp.concatenate(outs, 0).T.astype(BF16)

    @pl.when(step == pl.num_programs(0) - 1)
    def _():
        dk_ref[...] = jnp.concatenate([dk_sum[head] for head in range(heads)], 1).astype(BF16)
        dv_ref[...] = jnp.concatenate([dv_sum[head] for head in range(heads)], 1).astype(BF16)


def attend_backward(q, k, v, grad, lse, image_rows, text_rows):
    rows, wide = q.shape
    heads = wide // HEAD_DIM
    whole = pl.BlockSpec((rows, wide), lambda i: (0, 0))
    block = pl.BlockSpec((QUERY_BLOCK, wide), lambda i: (i, 0))
    return pl.pallas_call(
        functools.partial(attend_backward_kernel, heads, image_rows, text_rows),
        grid=(rows // QUERY_BLOCK,),
        in_specs=[block, whole, whole, block, pl.BlockSpec((heads, QUERY_BLOCK), lambda i: (0, i))],
        out_specs=[block, whole, whole],
        out_shape=[jax.ShapeDtypeStruct((rows, wide), BF16)] * 3,
        scratch_shapes=[
            pltpu.VMEM((wide, rows), BF16),
            pltpu.VMEM((heads, rows, HEAD_DIM), F32),
            pltpu.VMEM((heads, rows, HEAD_DIM), F32),
        ],
        compiler_params=pltpu.CompilerParams(vmem_limit_bytes=VMEM_LIMIT),
        cost_estimate=pl.CostEstimate(
            flops=10 * rows * rows * wide, bytes_accessed=14 * rows * wide, transcendentals=heads * rows * rows
        ),
        name="attend_backward",
    )(q, k, v, grad, lse)


def normalise(inputs):
    centred = inputs - jnp.mean(inputs, axis=-1, keepdims=True)
    spread = lax.rsqrt(jnp.mean(centred * centred, axis=-1, keepdims=True) + 1e-06)
    return centred * spread, spread


def normalise_back(grad_norm, norm, spread):
    return spread * (
        grad_norm
        - jnp.mean(grad_norm, axis=-1, keepdims=True)
        - norm * jnp.mean(grad_norm * norm, axis=-1, keepdims=True)
    )


def gelu_parts(hidden):
    root = 0.7978845608028654
    square = hidden * hidden
    bent = jnp.tanh(hidden * (root + root * 0.044715 * square))
    half = 0.5 * (1.0 + bent)
    slope = half + 0.5 * hidden * (1.0 - bent * bent) * (root + 3.0 * root * 0.044715 * square)
    return hidden * half, slope


MESH = pl.DeviceIdType.MESH
VMEM_SPEC = pl.BlockSpec(memory_space=pltpu.VMEM)
ANY_SPEC = pl.BlockSpec(memory_space=pl.ANY)


class Wires:
    def __init__(self, send_sems, recv_sems):
        self.dp, self.x, self.tp = lax.axis_index("dp"), lax.axis_index("ctx"), lax.axis_index("tp")
        self.y, self.k = self.tp // 2, self.tp % 2
        self.x_next = (self.dp, 1 - self.x, self.tp)
        self.y_next = (self.dp, self.x, (1 - self.y) * 2 + self.k)
        self.k_next = (self.dp, self.x, self.y * 2 + 1 - self.k)
        self.send_sems, self.recv_sems, self.used = send_sems, recv_sems, 0
        self.started = []

    def copy(self, source, target, device):
        wire = pltpu.make_async_remote_copy(
            src_ref=source,
            dst_ref=target,
            send_sem=self.send_sems.at[self.used],
            recv_sem=self.recv_sems.at[self.used],
            device_id=device,
            device_id_type=MESH,
        )
        self.used += 1
        wire.start()
        self.started.append(wire)
        return wire

    def meet(self, devices):
        barrier = pltpu.get_barrier_semaphore()
        for device in devices:
            pl.semaphore_signal(barrier, inc=1, device_id=device, device_id_type=MESH)
        pl.semaphore_wait(barrier, len(devices))

    def finish(self):
        for wire in self.started:
            wire.wait_send()


def row_step(rows):
    return 32 if rows % 32 == 0 else rows


def over_rows(rows, body):
    step = row_step(rows)
    if step == rows:
        body(slice(0, rows))
        return

    def one(index, carry):
        body(pl.ds(pl.multiple_of(index * step, step), step))
        return carry

    lax.fori_loop(0, rows // step, one, 0)


def reduce_plane(wires, streams):
    x, y, k = wires.x, wires.y, wires.k
    first = [wires.copy(s["part"].at[:, :, 1 - k], s["core"], wires.k_next) for s in streams]
    second = []
    for s, arrived in zip(streams, first):
        part, core, held = s["part"], s["core"], s["held"]
        rows, width = part.shape[3], part.shape[4]
        cut = width // 2
        arrived.wait_recv()
        for i in range(2):
            for j in range(2):

                def add(span, i=i, j=j):
                    held[i, j, span] = (part[i, j, k, span].astype(F32) + core[i, j, span].astype(F32)).astype(BF16)

                over_rows(rows, add)
        second.append(
            (
                wires.copy(held.at[:, 1 - y, :, pl.ds(0, cut)], s["along_y"], wires.y_next),
                wires.copy(held.at[1 - x, :, :, pl.ds(cut, cut)], s["along_x"], wires.x_next),
            )
        )
    third = []
    for s, (from_y, from_x) in zip(streams, second):
        held, along_y, along_x, out_x, out_y = s["held"], s["along_y"], s["along_x"], s["out_x"], s["out_y"]
        rows, width = held.shape[2], held.shape[3]
        cut = width // 2
        from_y.wait_recv()
        from_x.wait_recv()

        def add(span):
            out_x[span] = (
                held[1 - x, y, span, :cut].astype(F32) + along_y[1 - x, span].astype(F32)
            ).astype(BF16)
            out_y[span] = (
                held[x, 1 - y, span, cut:].astype(F32) + along_x[1 - y, span].astype(F32)
            ).astype(BF16)

        over_rows(rows, add)
        third.append(
            (
                wires.copy(out_x, s["last_x"], wires.x_next),
                wires.copy(out_y, s["last_y"], wires.y_next),
            )
        )
    for s, (from_x, from_y) in zip(streams, third):
        held, along_y, along_x, last_x, last_y, total = (
            s["held"],
            s["along_y"],
            s["along_x"],
            s["last_x"],
            s["last_y"],
            s["total"],
        )
        rows, width = held.shape[2], held.shape[3]
        cut = width // 2
        from_x.wait_recv()
        from_y.wait_recv()

        def add(span):
            total[span, :cut] = (
                held[x, y, span, :cut].astype(F32) + along_y[x, span].astype(F32) + last_x[span].astype(F32)
            )
            total[span, cut:] = (
                held[x, y, span, cut:].astype(F32) + along_x[y, span].astype(F32) + last_y[span].astype(F32)
            )

        over_rows(rows, add)


REDUCE_KEYS = ("core", "held", "along_y", "along_x", "out_x", "out_y", "last_x", "last_y", "total")


def reduce_scratch(rows, width):
    half = width // 2
    return [
        pltpu.VMEM((2, 2, rows, width), BF16),
        pltpu.VMEM((2, 2, rows, width), BF16),
        pltpu.VMEM((2, rows, half), BF16),
        pltpu.VMEM((2, rows, half), BF16),
        pltpu.VMEM((rows, half), BF16),
        pltpu.VMEM((rows, half), BF16),
        pltpu.VMEM((rows, half), BF16),
        pltpu.VMEM((rows, half), BF16),
        pltpu.VMEM((rows, width), F32),
    ]


def spread_plane(wires, blocks):
    x, y, k = wires.x, wires.y, wires.k
    first = []
    for block in blocks:
        cut = block.shape[4] // 2
        low, high = pl.ds(0, cut), pl.ds(cut, cut)
        mine = block.at[x, y, k, :, low], block.at[x, y, k, :, high]
        first.append((wires.copy(mine[0], mine[0], wires.x_next), wires.copy(mine[1], mine[1], wires.y_next)))
    second = []
    for block, (from_x, from_y) in zip(blocks, first):
        cut = block.shape[4] // 2
        low, high = pl.ds(0, cut), pl.ds(cut, cut)
        from_x.wait_recv()
        from_y.wait_recv()
        lows, highs = block.at[:, y, k, :, low], block.at[x, :, k, :, high]
        second.append((wires.copy(lows, lows, wires.y_next), wires.copy(highs, highs, wires.x_next)))
    third = []
    for block, (from_y, from_x) in zip(blocks, second):
        from_y.wait_recv()
        from_x.wait_recv()
        gathered = block.at[:, :, k]
        third.append(wires.copy(gathered, gathered, wires.k_next))
    for arrived in third:
        arrived.wait_recv()


def comm_call(kernel, outs, scratch, wires, collective_id, name, in_specs, out_specs):
    return pl.pallas_call(
        kernel,
        out_shape=outs,
        in_specs=in_specs,
        out_specs=out_specs,
        scratch_shapes=scratch + [pltpu.SemaphoreType.DMA((wires,)), pltpu.SemaphoreType.DMA((wires,))],
        compiler_params=pltpu.CompilerParams(
            collective_id=collective_id, has_side_effects=True, vmem_limit_bytes=VMEM_LIMIT
        ),
        name=name,
    )


def enter_kernel(
    n_dp,
    part_ref,
    bias_ref,
    rows_ref,
    image_ref,
    text_ref,
    mod_ref,
    rows_out,
    image_out,
    text_out,
    mod_in,
    local_sems,
    send_sems,
    recv_sems,
):
    wires = Wires(send_sems, recv_sems)
    dp, x, y, k, tp = wires.dp, wires.x, wires.y, wires.k, wires.tp
    count = n_dp * 2
    me = dp * 2 + x
    peers = [lax.rem(me + offset, count) for offset in range(1, count)]
    others = [(peer // 2, peer % 2, tp) for peer in peers]
    lanes = [lax.rem(tp + offset, 4) for offset in range(1, 4)]
    wires.meet(others + [(dp, x, lane) for lane in lanes])

    keep = [
        pltpu.make_async_copy(image_ref, image_out.at[x], local_sems.at[0]),
        pltpu.make_async_copy(text_ref, text_out.at[x], local_sems.at[1]),
    ]
    streams = ((image_ref, image_out), (text_ref, text_out))
    sums = [wires.copy(part_ref.at[peer // 2], mod_in.at[me], other) for peer, other in zip(peers, others)]
    rows = [wires.copy(rows_ref, rows_out.at[me], other) for other in others]
    along_x = [wires.copy(ref.at[tp], out.at[x, tp], wires.x_next) for ref, out in streams]
    for local in keep:
        local.start()
    mod_in[me] = part_ref[dp]
    rows_out[me] = rows_ref[...]
    for arrived in sums:
        arrived.wait_recv()
    total = bias_ref[...]
    for source in range(count):
        total = total + mod_in[source]
    mod_ref[tp] = total
    mods = [wires.copy(mod_ref.at[tp], mod_ref.at[tp], (dp, x, lane)) for lane in lanes]
    along_y = []
    for (_, out), arrived in zip(streams, along_x):
        arrived.wait_recv()
        block = out.at[1 - x, tp]
        along_y.append(wires.copy(block, block, wires.y_next))
    across = []
    for _, out in streams:
        block = out.at[1 - x, tp]
        across.append(wires.copy(block, block, wires.k_next))
    far = (1 - y) * 2 + k
    for (_, out), arrived in zip(streams, along_y):
        arrived.wait_recv()
        block = out.at[1 - x, far]
        across.append(wires.copy(block, block, wires.k_next))
    for arrived in mods + rows + across:
        arrived.wait_recv()
    for local in keep:
        local.wait()
    wires.finish()


def enter(partial_mod, ada_bias, bias_rows, image, text):
    n_dp, kinds, wide = partial_mod.shape
    count = 2 * n_dp
    tp_n = image.shape[0]
    return comm_call(
        functools.partial(enter_kernel, n_dp),
        [
            jax.ShapeDtypeStruct((tp_n, kinds, wide), F32),
            jax.ShapeDtypeStruct((count,) + bias_rows.shape, F32),
            jax.ShapeDtypeStruct((2,) + image.shape, BF16),
            jax.ShapeDtypeStruct((2,) + text.shape, BF16),
        ],
        [pltpu.VMEM((count, kinds, wide), F32), pltpu.SemaphoreType.DMA((2,))],
        2 * (count - 1) + 3 + 8,
        0,
        "enter",
        [VMEM_SPEC] * 3 + [ANY_SPEC] * 2,
        [VMEM_SPEC] * 2 + [ANY_SPEC] * 2,
    )(partial_mod, ada_bias, bias_rows, image, text)


def middle_kernel(
    image_part,
    text_part,
    image_x,
    text_x,
    mod_ref,
    bias_ref,
    image_attention,
    text_attention,
    image_middle,
    text_middle,
    image_all,
    text_all,
    *scratch,
):
    send_sems, recv_sems = scratch[-2:]
    wires = Wires(send_sems, recv_sems)
    x, y, k = wires.x, wires.y, wires.k
    wires.meet([wires.x_next, wires.y_next, wires.k_next])
    size = len(REDUCE_KEYS)
    streams = [
        dict(zip(("part",) + REDUCE_KEYS, (part,) + scratch[i * size : (i + 1) * size]))
        for i, part in enumerate((image_part, text_part))
    ]
    reduce_plane(wires, streams)
    for i, (tokens, attention, middle, gathered) in enumerate(
        ((image_x, image_attention, image_middle, image_all), (text_x, text_attention, text_middle, text_all))
    ):
        total = streams[i]["total"]

        def finish(span, i=i, tokens=tokens, attention=attention, middle=middle, gathered=gathered, total=total):
            branch = total[span] + bias_ref[i]
            attention[span] = branch
            value = tokens[span].astype(F32) + mod_ref[i, 2] * branch
            middle[span] = value
            norm, _ = normalise(value)
            gathered[x, y, k, span] = (norm * (1.0 + mod_ref[i, 4]) + mod_ref[i, 3]).astype(BF16)

        over_rows(total.shape[0], finish)
    spread_plane(wires, [image_all, text_all])
    wires.finish()


def middle_step(image_part, text_part, image_x, text_x, mod, bias):
    (image_rows, width), text_rows = image_x.shape, text_x.shape[0]
    outs = []
    for _ in range(2):
        outs += [jax.ShapeDtypeStruct((rows, width), F32) for rows in (image_rows, text_rows)]
    outs += [jax.ShapeDtypeStruct(part.shape, BF16) for part in (image_part, text_part)]
    return comm_call(
        middle_kernel,
        outs,
        reduce_scratch(image_rows, width) + reduce_scratch(text_rows, width),
        20,
        1,
        "middle",
        [VMEM_SPEC] * 6,
        [VMEM_SPEC] * 6,
    )(image_part, text_part, image_x, text_x, mod, bias)


def turn_kernel(
    valid_ref,
    image_feed,
    text_feed,
    image_second,
    text_second,
    image_attention,
    text_attention,
    image_middle,
    text_middle,
    image_cot,
    text_cot,
    mod_ref,
    bias_ref,
    image_out,
    text_out,
    image_grad,
    text_grad,
    sums_ref,
    image_all,
    text_all,
    *scratch,
):
    send_sems, recv_sems = scratch[-2:]
    wires = Wires(send_sems, recv_sems)
    x, y, k = wires.x, wires.y, wires.k
    wires.meet([wires.x_next, wires.y_next, wires.k_next])
    size = len(REDUCE_KEYS)
    streams = [
        dict(zip(("part",) + REDUCE_KEYS, (part,) + scratch[i * size : (i + 1) * size]))
        for i, part in enumerate((image_second, text_second, image_feed, text_feed))
    ]
    reduce_plane(wires, streams)
    sums_ref[...] = jnp.zeros_like(sums_ref)
    groups = (
        (image_attention, image_middle, image_cot, image_out, image_grad, image_all),
        (text_attention, text_middle, text_cot, text_out, text_grad, text_all),
    )
    for i, (attention, middle, cot, out, grad, gathered) in enumerate(groups):
        second, feed = streams[i]["total"], streams[2 + i]["total"]

        def finish(span, i=i, attention=attention, middle=middle, cot=cot, out=out, grad=grad, gathered=gathered, second=second, feed=feed):
            branch, value, arriving, pulled = attention[span], middle[span], cot[span].astype(F32), second[span]
            fed = feed[span] + bias_ref[i]
            gated_branch = mod_ref[i, 2] * branch
            gated_feed = mod_ref[i, 5] * fed
            result = value + gated_feed
            out[span] = result.astype(BF16)
            norm, spread = normalise(value)
            grad_middle = arriving + normalise_back(pulled * (1.0 + mod_ref[i, 4]), norm, spread)
            grad[span] = grad_middle
            low = (grad_middle * mod_ref[i, 2]).astype(BF16)
            gathered[x, y, k, span] = low
            if i == 1:
                kept = valid_ref[span]
                result, gated_branch, gated_feed = result * kept, gated_branch * kept, gated_feed * kept
            own_feed = (arriving * mod_ref[i, 5]).astype(BF16).astype(F32)
            terms = (
                grad_middle * branch,
                pulled,
                pulled * norm,
                arriving * fed,
                own_feed,
                low.astype(F32),
                result * result,
                gated_branch * gated_branch,
                gated_feed * gated_feed,
            )
            for t, term in enumerate(terms):
                sums_ref[i, t : t + 1] += jnp.sum(term, axis=0, keepdims=True)

        over_rows(second.shape[0], finish)
    spread_plane(wires, [image_all, text_all])
    wires.finish()


def turn_step(valid, feeds, seconds, attentions, middles, cots, mod, bias):
    width = middles[0].shape[1]
    rows = [part.shape[0] for part in middles]
    outs = [jax.ShapeDtypeStruct((r, width), BF16) for r in rows]
    outs += [jax.ShapeDtypeStruct((r, width), F32) for r in rows]
    outs += [jax.ShapeDtypeStruct((2, 16, width), F32)]
    outs += [jax.ShapeDtypeStruct(part.shape, BF16) for part in feeds]
    scratch = []
    for _ in range(2):
        for r in rows:
            scratch += reduce_scratch(r, width)
    return comm_call(
        turn_kernel, outs, scratch, 30, 2, "turn", [VMEM_SPEC] * 13, [VMEM_SPEC] * 7
    )(valid, *feeds, *seconds, *attentions, *middles, *cots, mod, bias)


PACKED = 24


def leave_kernel(
    n_dp,
    image_part,
    text_part,
    image_x,
    text_x,
    image_grad,
    text_grad,
    image_out,
    text_out,
    sums_ref,
    mod_ref,
    halves_ref,
    image_outs,
    text_outs,
    image_grads,
    text_grads,
    packed_out,
    halves_out,
    *scratch,
):
    send_sems, recv_sems = scratch[-2:]
    packed, packed_in, own_sums, both_halves, local_sums = scratch[-7:-2]
    wires = Wires(send_sems, recv_sems)
    dp, x, y, k, tp = wires.dp, wires.x, wires.y, wires.k, wires.tp
    me = x * 4 + tp
    peers = [lax.rem(me + offset, 8) for offset in range(1, 8)]
    planes = [lax.rem(dp + offset, n_dp) for offset in range(1, n_dp)]
    wires.meet([(dp, peer // 4, peer % 4) for peer in peers] + [(plane, x, tp) for plane in planes])

    image_outs[tp] = image_out[...]
    text_outs[tp] = text_out[...]
    both_halves[x] = halves_ref[...]
    halves = wires.copy(both_halves.at[x], both_halves.at[x], wires.x_next)
    size = len(REDUCE_KEYS)
    streams = [
        dict(zip(("part",) + REDUCE_KEYS, (part,) + scratch[i * size : (i + 1) * size]))
        for i, part in enumerate((image_part, text_part))
    ]
    reduce_plane(wires, streams)
    local_sums[...] = jnp.zeros_like(local_sums)
    for i, (tokens, grad, all_grads) in enumerate(
        ((image_x, image_grad, image_grads), (text_x, text_grad, text_grads))
    ):
        total = streams[i]["total"]

        def finish(span, i=i, tokens=tokens, grad=grad, all_grads=all_grads, total=total):
            pulled = total[span]
            norm, spread = normalise(tokens[span].astype(F32))
            grad_tokens = grad[span] + normalise_back(pulled * (1.0 + mod_ref[i, 1]), norm, spread)
            all_grads[tp, span] = grad_tokens.astype(BF16)
            local_sums[2 * i : 2 * i + 1] += jnp.sum(pulled, axis=0, keepdims=True)
            local_sums[2 * i + 1 : 2 * i + 2] += jnp.sum(pulled * norm, axis=0, keepdims=True)

        over_rows(total.shape[0], finish)
    wide = packed.shape[2]
    for t in range(4):
        cols = slice(t * wide, (t + 1) * wide)
        for i in range(2):
            packed[t, 6 * i : 6 * i + 2] = local_sums[2 * i : 2 * i + 2, cols]
            packed[t, 6 * i + 2 : 6 * i + 6] = sums_ref[i, 0:4, cols]
            packed[t, 12 + 5 * i : 12 + 5 * i + 5] = sums_ref[i, 4:9, cols]
        packed[t, 22:24] = jnp.zeros((2, wide), F32)
    packed_in[me] = packed[tp]
    gathers = [wires.copy(packed.at[peer % 4], packed_in.at[me], (dp, peer // 4, peer % 4)) for peer in peers]
    finals = (image_outs, text_outs, image_grads, text_grads)
    along_y = [wires.copy(final.at[tp], final.at[tp], wires.y_next) for final in finals]
    across = [wires.copy(final.at[tp], final.at[tp], wires.k_next) for final in finals]
    for arrived in gathers:
        arrived.wait_recv()
    total = packed_in[0]
    for source in range(1, 8):
        total = total + packed_in[source]
    own_sums[...] = total
    halves.wait_recv()
    for plane in planes:
        across.append(wires.copy(own_sums, packed_out.at[dp], (plane, x, tp)))
        across.append(wires.copy(both_halves, halves_out.at[dp], (plane, x, tp)))
    packed_out[dp] = total
    halves_out[dp] = both_halves[...]
    far = (1 - y) * 2 + k
    for final, arrived in zip(finals, along_y):
        arrived.wait_recv()
        across.append(wires.copy(final.at[far], final.at[far], wires.k_next))
    for arrived in across:
        arrived.wait_recv()
    wires.finish()


def leave_step(n_dp, parts, tokens, grads, outs_own, sums, mod, halves):
    width = tokens[0].shape[1]
    rows = [part.shape[0] for part in tokens]
    wide = width // 4
    outs = [jax.ShapeDtypeStruct((4, r, width), BF16) for r in rows] * 2
    outs += [
        jax.ShapeDtypeStruct((n_dp, PACKED, wide), F32),
        jax.ShapeDtypeStruct((n_dp, 2) + halves.shape, F32),
    ]
    scratch = []
    for r in rows:
        scratch += reduce_scratch(r, width)
    scratch += [
        pltpu.VMEM((4, PACKED, wide), F32),
        pltpu.VMEM((8, PACKED, wide), F32),
        pltpu.VMEM((PACKED, wide), F32),
        pltpu.VMEM((2,) + halves.shape, F32),
        pltpu.VMEM((8, width), F32),
    ]
    return comm_call(
        functools.partial(leave_kernel, n_dp),
        outs,
        scratch,
        1 + 10 + 7 + 8 + 2 * (n_dp - 1) + 4,
        3,
        "leave",
        [VMEM_SPEC] * 11,
        [VMEM_SPEC] * 6,
    )(*parts, *tokens, *grads, *outs_own, sums, mod, halves)


def share_kernel(part_ref, out_ref, send_sems, recv_sems):
    wires = Wires(send_sems, recv_sems)
    dp, x, tp = wires.dp, wires.x, wires.tp
    lanes = [(dp, x, lax.rem(tp + offset, 4)) for offset in range(1, 4)]
    wires.meet(lanes)
    copies = [wires.copy(part_ref, out_ref.at[tp], lane) for lane in lanes]
    out_ref[tp] = part_ref[...]
    for arrived in copies:
        arrived.wait_recv()
    wires.finish()


def share(part):
    return comm_call(
        share_kernel,
        jax.ShapeDtypeStruct((4,) + part.shape, F32),
        [],
        3,
        4,
        "share",
        [VMEM_SPEC],
        VMEM_SPEC,
    )(part)


def gather_rows(shard, ctx):
    pairs = [(0, 1), (1, 0)]
    kept = lax.dynamic_index_in_dim(shard, ctx, 2, keepdims=False)
    given = lax.dynamic_index_in_dim(shard, 1 - ctx, 2, keepdims=False)
    other = lax.ppermute(given, "ctx", pairs)
    first, last = jnp.where(ctx == 0, kept, other), jnp.where(ctx == 0, other, kept)
    return lax.all_gather(jnp.concatenate([first, last], 1), "dp", axis=1, tiled=True)


def scatter_rows(grad, ctx):
    mine = lax.psum_scatter(grad.astype(BF16), "dp", scatter_dimension=1, tiled=True)
    rows = mine.shape[1] // 2
    kept = lax.dynamic_slice_in_dim(mine, ctx * rows, rows, 1)
    given = lax.dynamic_slice_in_dim(mine, (1 - ctx) * rows, rows, 1)
    other = lax.ppermute(given, "ctx", [(0, 1), (1, 0)])
    first, last = jnp.where(ctx == 0, kept, other), jnp.where(ctx == 0, other, kept)
    return first.astype(F32), last.astype(F32)


def on_device(
    image_tokens,
    text_tokens,
    conditioning,
    ada_weight,
    ada_bias,
    qkv_weight,
    qv_bias,
    out_weight,
    out_bias,
    up_weight,
    up_bias,
    down_weight,
    down_bias,
    image_cotangent,
    text_cotangent,
):
    ctx_n, tp_n, dp_n = lax.axis_size("ctx"), lax.axis_size("tp"), lax.axis_size("dp")
    dp, ctx, tp = lax.axis_index("dp"), lax.axis_index("ctx"), lax.axis_index("tp")
    image_length, text_length, width = image_tokens.shape[1], text_tokens.shape[1], image_tokens.shape[2]
    slice_width = qkv_weight.shape[3]
    shard_rows = qkv_weight.shape[1]
    half = slice_width // ctx_n
    up_half = up_weight.shape[2] // ctx_n
    own_rows = (image_length // tp_n, TEXT_SLOTS // tp_n)
    image_all = image_length * ctx_n
    text_all = TEXT_SLOTS * ctx_n
    joint_pad = -(image_all + text_all) % JOINT_STEP
    pad = ((0, TEXT_SLOTS - text_length), (0, 0))

    qkv_full = gather_rows(
        qkv_weight.reshape(2, shard_rows, 3, ctx_n, half)
        .transpose(0, 1, 3, 2, 4)
        .reshape(2, shard_rows, ctx_n, 3 * half),
        ctx,
    )
    out_full = gather_rows(out_weight.reshape(2, shard_rows, ctx_n, half), ctx)
    up_full = gather_rows(up_weight.reshape(2, shard_rows, ctx_n, up_half), ctx)
    down_full = gather_rows(down_weight.reshape(2, shard_rows, ctx_n, up_half), ctx)
    qv_own = lax.dynamic_slice_in_dim(qv_bias, ctx * half, half, 2).astype(F32)
    up_bias_own = lax.dynamic_slice_in_dim(up_bias, ctx * up_half, up_half, 1).astype(F32)

    tokens = (image_tokens[0], jnp.pad(text_tokens[0], pad))
    cotangents = (image_cotangent[0], jnp.pad(text_cotangent[0], pad))
    cond_float = conditioning.astype(F32)
    activated_low = jax.nn.silu(cond_float).astype(BF16)
    partial_mod = jnp.einsum("nd,adkf->nakf", activated_low, ada_weight, preferred_element_type=F32)
    mod_blocks, bias_blocks, image_blocks, text_blocks = enter(
        partial_mod.reshape(dp_n, 12, slice_width),
        ada_bias.astype(F32).reshape(12, slice_width),
        jnp.concatenate([out_bias, down_bias], 0).astype(F32),
        *[part.reshape(tp_n, rows, width) for part, rows in zip(tokens, own_rows)],
    )
    modulation = mod_blocks.transpose(1, 0, 2).reshape(2, 6, width)
    biases = bias_blocks.transpose(1, 0, 2).reshape(4, width)
    mod_rows = modulation[:, :, None]
    out_bias_rows, down_bias_rows = biases[:2, None], biases[2:, None]
    tokens_all = (image_blocks.reshape(image_all, width), text_blocks.reshape(text_all, width))
    cotangents_all = []
    for part in cotangents:
        other = lax.ppermute(part, "ctx", [(0, 1), (1, 0)])
        first, last = jnp.where(ctx == 0, part, other), jnp.where(ctx == 0, other, part)
        cotangents_all.append(jnp.concatenate([first, last], 0))

    def own(parts):
        return [lax.dynamic_slice_in_dim(part, tp * rows, rows, 0) for part, rows in zip(parts, own_rows)]

    tokens_own, cotangents_own = own(tokens), own(cotangents)
    slots = tp * own_rows[1] + lax.broadcasted_iota(jnp.int32, (own_rows[1], 1), 0)
    valid = jnp.broadcast_to((slots < text_length).astype(F32), (own_rows[1], width))

    def blocks(part):
        return part.reshape(2, 2, 2, part.shape[0] // 8, width)

    normed_low, qkv_parts = [], []
    for stream in range(2):
        norm, _ = normalise(tokens_all[stream].astype(F32))
        normed = (norm * (1.0 + modulation[stream, 1]) + modulation[stream, 0]).astype(BF16)
        normed_low.append(normed)
        bias = jnp.concatenate([qv_own[stream, 0], jnp.zeros((half,), F32), qv_own[stream, 1]])
        qkv_parts.append((dot(normed, qkv_full[stream]) + bias).astype(BF16))
    joint = jnp.concatenate(qkv_parts + [jnp.zeros((joint_pad, 3 * half), BF16)], 0)
    queries, keys, values = joint[:, :half], joint[:, half : 2 * half], joint[:, 2 * half :]
    blended, lse = attend_forward(queries, keys, values, image_all, text_length)
    blended_parts = (blended[:image_all], blended[image_all : image_all + text_all])
    out_parts = [
        blocks(dot(blended_parts[s], out_full[s], ((1,), (1,))).astype(BF16)) for s in range(2)
    ]
    *attentions_middles, image_second, text_second = middle_step(
        *out_parts, *tokens_own, mod_rows, out_bias_rows
    )
    attentions, middles = attentions_middles[:2], attentions_middles[2:]
    second_low = (image_second.reshape(image_all, width), text_second.reshape(text_all, width))

    feed_parts, second_parts = [], []
    down_weight_grads, up_weight_grads, up_bias_grads = [], [], []
    for stream in range(2):
        hidden = dot(second_low[stream], up_full[stream]) + up_bias_own[stream]
        gelu_out, slope = gelu_parts(hidden)
        gelu_low = gelu_out.astype(BF16)
        feed_parts.append(blocks(dot(gelu_low, down_full[stream], ((1,), (1,))).astype(BF16)))
        grad_feed = (cotangents_all[stream].astype(F32) * modulation[stream, 5]).astype(BF16)
        down_weight_grads.append(dot(grad_feed, gelu_low, ((0,), (0,))))
        grad_hidden = (dot(grad_feed, down_full[stream]) * slope).astype(BF16)
        up_bias_grads.append(jnp.sum(grad_hidden.astype(F32), axis=0))
        up_weight_grads.append(dot(second_low[stream], grad_hidden, ((0,), (0,))))
        second_parts.append(blocks(dot(grad_hidden, up_full[stream], ((1,), (1,))).astype(BF16)))
    down_weight_grad = jnp.concatenate(scatter_rows(jnp.stack(down_weight_grads), ctx), 2)
    up_weight_grad = jnp.concatenate(scatter_rows(jnp.stack(up_weight_grads), ctx), 2)
    image_out, text_out, image_middle_grad, text_middle_grad, sums, image_attn, text_attn = turn_step(
        valid, feed_parts, second_parts, attentions, middles, cotangents_own, mod_rows, down_bias_rows
    )
    attention_grad_all = (image_attn.reshape(image_all, width), text_attn.reshape(text_all, width))

    out_weight_grads, blended_grads = [], []
    for stream in range(2):
        out_weight_grads.append(dot(attention_grad_all[stream], blended_parts[stream], ((0,), (0,))))
        blended_grads.append(dot(attention_grad_all[stream], out_full[stream]).astype(BF16))
    grad_queries, grad_keys, grad_values = attend_backward(
        queries,
        keys,
        values,
        jnp.concatenate(blended_grads + [jnp.zeros((joint_pad, half), BF16)], 0),
        lse,
        image_all,
        text_length,
    )
    grad_joint = jnp.concatenate([grad_queries, grad_keys, grad_values], 1)
    grad_parts = (grad_joint[:image_all], grad_joint[image_all : image_all + text_all])
    qkv_weight_grads, qv_bias_grads, normed_parts = [], [], []
    for stream in range(2):
        sums_joint = jnp.sum(grad_parts[stream].astype(F32), axis=0)
        qv_bias_grads.append(jnp.concatenate([sums_joint[:half], sums_joint[2 * half :]]))
        qkv_weight_grads.append(dot(normed_low[stream], grad_parts[stream], ((0,), (0,))))
        normed_parts.append(blocks(dot(grad_parts[stream], qkv_full[stream], ((1,), (1,))).astype(BF16)))
    out_weight_grad = jnp.concatenate(scatter_rows(jnp.stack(out_weight_grads), ctx), 2)
    qkv_weight_grad = jnp.concatenate(
        [part.reshape(2, shard_rows, 3, half) for part in scatter_rows(jnp.stack(qkv_weight_grads), ctx)], 3
    )

    halves = jnp.concatenate(
        [part.reshape(-1, slice_width) for part in (*qv_bias_grads, *up_bias_grads)]
        + [jnp.zeros((2, slice_width), F32)],
        0,
    )
    image_outs, text_outs, image_grads, text_grads, packed, halves_all = leave_step(
        dp_n,
        normed_parts,
        tokens_own,
        (image_middle_grad, text_middle_grad),
        (image_out, text_out),
        sums,
        mod_rows,
        halves,
    )
    grad_mod_low = packed[:, :12].astype(BF16)
    ada_bias_grad = jnp.sum(grad_mod_low.astype(F32), axis=0).reshape(2, 6, slice_width)
    grad_mod_low = grad_mod_low.reshape(dp_n, 2, 6, slice_width)
    ada_weight_grad = jnp.einsum("nd,nakf->adkf", activated_low, grad_mod_low, preferred_element_type=F32)
    cond_partial = jnp.einsum("nakf,adkf->nd", grad_mod_low, ada_weight, preferred_element_type=F32)
    totals = jnp.sum(packed[:, 12:22], axis=0)
    cond_rows = jnp.pad(cond_partial, ((0, -dp_n % 2), (0, slice_width - shard_rows)))
    shared = share(jnp.concatenate([totals, cond_rows], 0))
    cond_total = jnp.sum(shared[:, 10 : 10 + dp_n, :shard_rows], axis=0)
    cond_grad = jax.vjp(jax.nn.silu, cond_float)[1](cond_total)[0]
    full = shared[:, :10].transpose(1, 0, 2).reshape(2, 5, width)
    bias_grads = lax.dynamic_slice_in_dim(full[:, :2], (dp * ctx_n + ctx) * shard_rows, shard_rows, 2)
    squares_total = jnp.sum(full[:, 2:], axis=2).T.reshape(6)
    counts = jnp.array([image_length, text_length] * 3, F32) * (dp_n * ctx_n * width)
    root_means = jnp.sqrt(squares_total / counts)
    half_sums = jnp.sum(halves_all, axis=0)
    qv_rows = half * 2 // slice_width
    up_rows = up_half // slice_width
    qv_bias_grad = (
        half_sums[:, : 2 * qv_rows].reshape(ctx_n, 2, 2, half).transpose(1, 2, 0, 3).reshape(2, 2, slice_width)
    )
    up_bias_grad = (
        half_sums[:, 2 * qv_rows : 2 * (qv_rows + up_rows)]
        .reshape(ctx_n, 2, up_half)
        .transpose(1, 0, 2)
        .reshape(2, ctx_n * up_half)
    )
    return (
        image_outs.reshape(1, image_length, width),
        text_outs.reshape(1, TEXT_SLOTS, width)[:, :text_length],
        image_grads.reshape(1, image_length, width),
        text_grads.reshape(1, TEXT_SLOTS, width)[:, :text_length],
        cond_grad,
        ada_weight_grad,
        ada_bias_grad,
        qkv_weight_grad,
        qv_bias_grad,
        out_weight_grad,
        bias_grads[:, 1],
        up_weight_grad,
        up_bias_grad,
        down_weight_grad,
        bias_grads[:, 0],
        root_means,
    )


def solution(mesh):
    rows = P(None, ("dp", "ctx"))
    tokens = P("dp", "ctx", None)
    stacked = P(None, ("dp", "ctx"), None, "tp")
    matrix = P(None, ("dp", "ctx"), "tp")
    return jax.shard_map(
        on_device,
        mesh=mesh,
        in_specs=(
            tokens,
            tokens,
            rows,
            stacked,
            P(None, None, "tp"),
            stacked,
            P(None, None, "tp"),
            matrix,
            rows,
            matrix,
            P(None, "tp"),
            matrix,
            rows,
            tokens,
            tokens,
        ),
        out_specs=(
            tokens,
            tokens,
            tokens,
            tokens,
            rows,
            stacked,
            P(None, None, "tp"),
            stacked,
            P(None, None, "tp"),
            matrix,
            rows,
            matrix,
            P(None, "tp"),
            matrix,
            rows,
            P(),
        ),
        check_vma=False,
    )
```

time: 1260 us -> 756 us (0.60)
  waiting for transfers between devices: 607 us -> 208 us
  blocking collectives: 285 us -> 0 us
  Pallas kernels: 33.4 us -> 275 us
  local copies, waits for them, and re-layouts: 131 us -> 96.2 us
  matrix products: 96.4 us -> 82.2 us
    pallas_call x0 -> x5, Pallas kernels: none -> 242 us  [the longest x1 67.6 us: turn_step(): comm_call(turn_kernel, outs, scratch, 30, 2, 'turn', [VMEM_SPEC] * 13, [V...]
    all_gather x10 -> x4, waiting for transfers between devices: 214 us -> 57.1 us  [gather_rows(): lax.all_gather(jnp.concatenate([first, last], 1), 'dp', axis=1, tiled=True)]
    reduce_scatter x8 -> x0, waiting for transfers between devices: 133 us -> none  [plane_scatter(): lax.psum_scatter(part, PLANE, scatter_dimension=0, tiled=True).astype(F32)]
    all_gather x9 -> x0, blocking collectives: 127 us -> none  [the longest x2 39.3 us: on_device(): lax.all_gather(part, 'ctx', axis=0, tiled=True)]
    psum x4 -> x0, blocking collectives: 101 us -> none  [the longest x1 50.7 us: on_device(): squares_total = lax.psum(squares_local, ('dp', 'ctx', 'tp'))]
    psum x1 -> x0, waiting for transfers between devices: 99 us -> none  [on_device(): mod_slices = lax.psum(partial_mod, ('dp', 'ctx')) + ada_bias.astype(F32)]
    all_to_all x3 -> x0, blocking collectives: 57.6 us -> none  [gather_rows(): lax.all_to_all(shard, 'ctx', split_axis=2, concat_axis=1, tiled=True)]
    ppermute x0 -> x10, waiting for transfers between devices: none -> 33.9 us  [the longest x4 27.7 us: gather_rows(): other = lax.ppermute(given, 'ctx', pairs)]
  transfers between devices with their start and end apart: 30 -> 18, of which waited for: 17 -> 7; matrix products, arithmetic and copies ran while one was open for 20% -> 24% of each run, Pallas kernels for 1% -> 28%
where the time goes in v2:
time: 756 us; the launch traced here: 746 us
  Pallas kernels  275 us (36%)
  waiting for transfers between devices  208 us (28%)
  local copies, waits for them, and re-layouts  96.2 us (13%)
  matrix products  82.2 us (11%)
  other arithmetic  53.2 us (7%)
  between operations  15.4 us (2%)
  starting transfers between devices  15.3 us (2%)
    reduce_scatter x2, waiting for transfers between devices, scatter_rows(): lax.psum_scatter(grad.astype(BF16), 'dp', scatter_dimension=1, tiled=True)  117 us
    dot_general x24, matrix products, dot(): lax.dot_general(left, right, (dims, ((), ())), preferred_element_type=F32)  78.8 us
    pallas_call x1, Pallas kernels, turn_step(): comm_call(turn_kernel, outs, scratch, 30, 2, 'turn', [VMEM_SPEC] * 13, [V...  67.6 us
    pallas_call x1, Pallas kernels, enter(): comm_call(functools.partial(enter_kernel, n_dp), [jax.ShapeDtypeStruct((t...  67.1 us
    all_gather x4, waiting for transfers between devices, gather_rows(): lax.all_gather(jnp.concatenate([first, last], 1), 'dp', axis=1, tiled=True)  57.1 us
    pallas_call x1, Pallas kernels, leave_step(): comm_call(functools.partial(leave_kernel, n_dp), outs, scratch, 1 + 10 +...  54.4 us
    pallas_call x1, Pallas kernels, middle_step(): comm_call(middle_kernel, outs, reduce_scratch(image_rows, width) + reduce...  47.7 us
    unnamed x114, local copies, waits for them, and re-layouts  43.1 us
  transfers between devices with their start and end apart: 18, of which 7 were waited for; matrix products, arithmetic and copies ran while one was open for 24% of the time, Pallas kernels for 28%

profile of v2, /device:TPU:0, one launch (start us, length us, event | category | flops | bytes accessed | tf_op | source)
XLA Modules:
  0.0 746.0 jit_solution(1796509811129400039)
XLA Ops:
  7.2 4.2 reshape.306
  11.5 2.7 copy.183
  15.3 2.9 collective-permute-start
  18.2 11.5 %collective-permute-done = bf16[2,192,576]{2,1,0:T(8,128)(2,1)} collective-permute-done((bf16[2,192,576]{2,1,0:T(8,128)(2,1)}, bf16[2,192,576]{2,1,0:T(8,128)(2,1)}, u32[]{:S(2)}, u32[]{:S(2)}) %collective-permute-start) | collective-permute-done | bytes 442400 | tf_op jit(solution)/shard_map/ppermute | solution.py:735
  36.0 4.0 collective-permute-done.1
  41.0 3.0 reshape.312
  44.0 3.7 reshape.313
  47.7 7.5 %constant_dynamic-slice_fusion.10 = (bf16[2,192,1,768]{3,2,1,0:T(2,128)(2,1)}, bf16[2,192,1,768]{3,2,1,0:T(2,128)(2,1)}, bf16[2,192,1,768]{3,2,1,0:T(2,128)(2,1)S(1)}, bf16[2,192,1,768]{3,2,1,0:T(2,128)(2,1)S(1)}) fusion(bf16[2,192,2,768]{3,2,1,0:T(2,128)(2,1)} %reshape.313, s32[]{:T(128)S(6)} %select_n.143, s32[]{:T(128)S(6)} %select_n.144, ...), kind=kLoop, calls=%fused_computation.153 | loop fusion | bytes 4718600 | tf_op jit(solution)/shard_map/jit(dynamic_index_in_dim)/dynamic_slice | solution.py:733
  56.7 12.1 %collective-permute-done.2 = bf16[2,192,768]{2,1,0:T(8,128)(2,1)S(1)} collective-permute-done((bf16[2,192,768]{2,1,0:T(8,128)(2,1)S(1)}, bf16[2,192,768]{2,1,0:T(8,128)(2,1)S(1)}, u32[]{:S(2)}, u32[]{:S(2)}) %collective-permute-start.2) | collective-permute-done | bytes 589856 | tf_op jit(solution)/shard_map/ppermute | solution.py:735
  78.2 67.1 %enter.1 = (f32[4,12,384]{2,1,0:T(8,128)}, f32[8,4,192]{2,1,0:T(4,128)}, bf16[2,4,128,1536]{3,2,1,0:T(8,128)(2,1)}, bf16[2,4,24,1536]{3,2,1,0:T(8,128)(2,1)}) custom-call(f32[4,12,384]{2,1,0:T(8,128)} %copy.181.part_ref, f32[12,384]{1,0:T(8,128)} %reshape.342.bias_ref, f32[4,192]{1,0:T(4,128)} %maximum_convert_fusion.4.rows_ref, ...), custom_call_target="tpu_custom_call" | custom-call | tf_op jit(solution)/shard_map/enter/pallas_call | solution.py:413
  149.4 2.8 convert_reduce_fusion
  163.6 4.0 add_convert_fusion
  167.7 2.6 fusion.3
  173.0 2.8 broadcast_select_fusion.1
  175.8 3.1 fusion.21
  179.0 4.1 add_convert_fusion.1
  185.0 14.6 %attend_forward.1 = (bf16[1280,192]{1,0:T(8,128)(2,1)}, f32[3,1280]{1,0:T(4,128)}) custom-call(bf16[1280,192]{1,0:T(8,128)(2,1)} %get-tuple-element.210.q_ref, bf16[1280,192]{1,0:T(8,128)(2,1)} %get-tuple-element.209.k_ref, bf16[1280,192]{1,0:T(8,128)(2,1)} %get-tuple-element.208.v_ref), custom_call_target="tpu_custom_call" | custom-call | flops 1258291200 | bytes 1966080 | tf_op jit(solution)/shard_map/attend_forward/pallas_call | solution.py:57
  201.9 3.9 convolution_convert_fusion.1
  205.8 47.7 %middle.1 = (f32[128,1536]{1,0:T(8,128)}, f32[24,1536]{1,0:T(8,128)}, f32[128,1536]{1,0:T(8,128)}, f32[24,1536]{1,0:T(8,128)}, bf16[2,2,2,128,1536]{4,3,2,1,0:T(...) custom-call(bf16[2,2,2,128,1536]{4,3,2,1,0:T(8,128)(2,1)} %bitcast.213, bf16[2,2,2,24,1536]{4,3,2,1,0:T(8,128)(2,1)} %bitcast.224, ...), custom_call_target="tpu_custom_call" | custom-call | tf_op jit(solution)/shard_map/middle/pallas_call | solution.py:479
  253.6 3.4 fusion.18
  257.0 5.9 fusion.12
  263.0 57.0 %all-gather.11.cloned.1.call-done = bf16[2,1536,768]{2,1,0:T(8,128)(2,1)} async-done(((bf16[2,384,768]{2,1,0:T(8,128)(2,1)}), bf16[2,1536,768]{2,1,0:T(8,128)(2,1)}) %all-gather.11.cloned.1.call-update) | async-done | bytes 4718608 | tf_op jit(solution)/shard_map/all_gather | solution.py:737
  320.0 3.7 convolution_convert_fusion.13
  323.8 2.6 convert_reduce_fusion.4
  328.6 5.2 convolution_convert_fusion.3
  333.7 3.9 convert_reduce_fusion.1
  337.6 4.1 convolution_convert_fusion.2
  342.4 67.6 %turn.1 = (bf16[128,1536]{1,0:T(8,128)(2,1)}, bf16[24,1536]{1,0:T(8,128)(2,1)}, f32[128,1536]{1,0:T(8,128)}, f32[24,1536]{1,0:T(8,128)}, f32[2,16,1536]{2,1,0:T(...) custom-call(f32[24,1536]{1,0:T(8,128)} %broadcast_in_dim.13.valid_ref, ...), custom_call_target="tpu_custom_call" | custom-call | tf_op jit(solution)/shard_map/turn/pallas_call | solution.py:578
  411.5 2.7 fusion.11
  415.4 3.6 copy.216
  420.7 4.0 convolution_convert_fusion.16
  428.4 18.5 %attend_backward.1 = (bf16[1280,192]{1,0:T(8,128)(2,1)}, bf16[1280,192]{1,0:T(8,128)(2,1)}, bf16[1280,192]{1,0:T(8,128)(2,1)}) custom-call(bf16[1280,192]{1,0:T(8,128)(2,1)} %get-tuple-element.210.q_ref, bf16[1280,192]{1,0:T(8,128)(2,1)} %get-tuple-element.209.k_ref, bf16[1280,192]{1,0:T(8,128)(2,1)} %get-tuple-element.208.v_ref, ...), custom_call_target="tpu_custom_call" | custom-call | flops 3145728000 | bytes 3440640 | tf_op jit(solution)/shard_map/attend_backward/pallas_call | solution.py:117
  455.1 10.6 %copy.214 = bf16[2,1536,576]{2,0,1:T(2,128)(2,1)} copy(bf16[2,1536,576]{1,2,0:T(8,128)(2,1)} %pad_maximum_fusion.2) | data formatting | bytes 7077888
  465.7 8.6 %reshape.350 = bf16[1536,1152]{1,0:T(8,128)(2,1)} reshape(bf16[1536,2,576]{2,1,0:T(2,128)(2,1)} %bitcast.212) | data formatting | bytes 7077888
  476.9 5.4 fusion.5
  482.3 2.5 pad_maximum_fusion.1
  487.1 4.3 fusion.4
  491.5 2.5 pad_maximum_fusion
  495.1 3.1 convolution_convert_fusion.15
  498.2 5.4 convolution_convert_fusion
  503.6 54.4 %leave.1 = (bf16[4,128,1536]{2,1,0:T(8,128)(2,1)}, bf16[4,24,1536]{2,1,0:T(8,128)(2,1)}, bf16[4,128,1536]{2,1,0:T(8,128)(2,1)}, bf16[4,24,1536]{2,1,0:T(8,128)(2...) custom-call(bf16[2,2,2,128,1536]{4,3,2,1,0:T(8,128)(2,1)} %bitcast.219, bf16[2,2,2,24,1536]{4,3,2,1,0:T(8,128)(2,1)} %bitcast.236, ...), custom_call_target="tpu_custom_call" | custom-call | tf_op jit(solution)/shard_map/leave/pallas_call | solution.py:694
  561.7 5.3 share.1
  570.2 2.5 convolution_bitcast_fusion
  583.5 2.7 reshape.351
  589.5 38.7 %reduce-scatter.11.cloned.1.call-done = bf16[2,384,768]{2,1,0:T(8,128)(2,1)} async-done(((bf16[2,1536,768]{2,1,0:T(8,128)(2,1)}), bf16[2,384,768]{2,1,0:T(8,128)(2,1)}) %reduce-scatter.11.cloned.1.call-update) | async-done | bytes 1179664 | tf_op jit(solution)/shard_map/reduce_scatter | solution.py:741
  637.7 78.5 %reduce-scatter.9.cloned.1.call-done = bf16[2,384,768]{2,1,0:T(8,128)(2,1)} async-done(((bf16[2,1536,768]{2,1,0:T(8,128)(2,1)}), bf16[2,384,768]{2,1,0:T(8,128)(2,1)}) %reduce-scatter.9.cloned.1.call-update) | async-done | bytes 1179664 | tf_op jit(solution)/shard_map/reduce_scatter | solution.py:741
  720.5 3.0 copy.208
  726.5 6.2 collective-permute-done.8
  (267 shorter events, 109.9 us)
Async XLA Ops:
  7.2 68.8 %copy-start = (bf16[2,192,6,384]{3,1,2,0:T(8,128)(2,1)S(1)}, bf16[2,192,6,384]{3,1,2,0:T(8,128)(2,1)}, u32[]{:S(2)}) copy-start(bf16[2,192,6,384]{3,1,2,0:T(8,128)(2,1)} %param.19) | copy-start | bytes 5308420
  7.2 168.6 %all-gather.5.cloned.1.call-start = ((), (), s32[]{:S(2)}) async-start(), calls=%async_computation.4 | async-start | bytes 4423680 | tf_op jit(solution)/shard_map/all_gather | solution.py:737
  15.3 14.5 %collective-permute-start = (bf16[2,192,576]{2,1,0:T(8,128)(2,1)}, bf16[2,192,576]{2,1,0:T(8,128)(2,1)}, u32[]{:S(2)}, u32[]{:S(2)}) collective-permute-start(bf16[2,192,576]{2,1,0:T(8,128)(2,1)} %bitcast.245), channel_id=1, source_target_pairs={{0,4},{4,0},{1,5},{5,1},{2,6},{6,2},{3,7},{7,3},{8,12},{12,8},{9,1... | collective-permute-start | bytes 1327112 | tf_op jit(solution)/shard_map/ppermute | solution.py:735
  32.4 167.3 %all-gather.7.cloned.1.call-start = ((), (), s32[]{:S(2)}) async-start(), calls=%async_computation.5 | async-start | bytes 1474560 | tf_op jit(solution)/shard_map/all_gather | solution.py:737
  33.9 6.2 collective-permute-start.1
  40.9 212.6 %all-gather.9.cloned.1.call-start = ((), (), s32[]{:S(2)}) async-start(), calls=%async_computation.6 | async-start | bytes 5898240 | tf_op jit(solution)/shard_map/all_gather | solution.py:737
  55.2 13.6 %collective-permute-start.2 = (bf16[2,192,768]{2,1,0:T(8,128)(2,1)S(1)}, bf16[2,192,768]{2,1,0:T(8,128)(2,1)S(1)}, u32[]{:S(2)}, u32[]{:S(2)}) collective-permute-start(bf16[2,192,768]{2,1,0:T(8,128)(2,1)S(1)} %bitcast.239), channel_id=1, source_target_pairs={{0,4},{4,0},{1,5},{5,1},{2,6},{6,2},{3,7},{7,3},{8,12},{12,8},{9,1... | collective-permute-start | bytes 1769480 | tf_op jit(solution)/shard_map/ppermute | solution.py:735
  69.0 4.3 copy-start.5
  69.0 6.3 copy-start.23
  70.1 5.9 copy-start.33
  70.1 249.9 %all-gather.11.cloned.1.call-start = ((), (), s32[]{:S(2)}) async-start(), calls=%async_computation.7 | async-start | bytes 5898240 | tf_op jit(solution)/shard_map/all_gather | solution.py:737
  70.4 102.6 %collective-permute-start.4 = (bf16[512,1536]{1,0:T(8,128)(2,1)}, bf16[512,1536]{1,0:T(8,128)(2,1)}, u32[]{:S(2)}, u32[]{:S(2)}) collective-permute-start(bf16[512,1536]{1,0:T(8,128)(2,1)} %bitcast.223), channel_id=1, source_target_pairs={{0,4},{4,0},{1,5},{5,1},{2,6},{6,2},{3,7},{7,3},{8,12},{12,8},{9,1... | collective-permute-start | bytes 4718600 | tf_op jit(solution)/shard_map/ppermute | solution.py:810
  71.6 5.4 copy-start.34
  71.6 6.0 copy-start.38
  71.6 6.0 copy-start.39
  72.3 98.8 %collective-permute-start.5 = (bf16[96,1536]{1,0:T(8,128)(2,1)}, bf16[96,1536]{1,0:T(8,128)(2,1)}, u32[]{:S(2)}, u32[]{:S(2)}) collective-permute-start(bf16[96,1536]{1,0:T(8,128)(2,1)} %pad.12), channel_id=1, source_target_pairs={{0,4},{4,0},{1,5},{5,1},{2,6},{6,2},{3,7},{7,3},{8,12},{12,8},{9,1... | collective-permute-start | bytes 884744 | tf_op jit(solution)/shard_map/ppermute | solution.py:810
  74.1 83.7 %collective-permute-start.3 = (bf16[2,192,768]{2,1,0:T(8,128)(2,1)}, bf16[2,192,768]{2,1,0:T(8,128)(2,1)}, u32[]{:S(2)}, u32[]{:S(2)}) collective-permute-start(bf16[2,192,768]{2,1,0:T(8,128)(2,1)} %bitcast.208), channel_id=1, source_target_pairs={{0,4},{4,0},{1,5},{5,1},{2,6},{6,2},{3,7},{7,3},{8,12},{12,8},{9,1... | collective-permute-start | bytes 1769480 | tf_op jit(solution)/shard_map/ppermute | solution.py:735
  76.3 72.9 %copy-start.36 = (bf16[2,2,384]{2,1,0:T(2,128)(2,1)S(1)}, bf16[2,2,384]{2,1,0:T(2,128)(2,1)}, u32[]{:S(2)}) copy-start(bf16[2,2,384]{2,1,0:T(2,128)(2,1)} %param.22) | copy-start | bytes 9220
  149.2 3.3 copy-start.1
  152.2 4.3 copy-start.35
  152.2 4.3 copy-start.3
  152.5 5.4 copy-start.4
  160.1 412.5 %reduce-scatter.15.cloned.1.call-start = ((), (), s32[]{:S(2)}) async-start(), calls=%async_computation.11 | async-start | bytes 1474560
  163.6 4.1 copy-start.2
  175.8 158.0 %copy-start.16 = (bf16[512,1536]{1,0:T(8,128)(2,1)}, bf16[512,1536]{1,0:T(8,128)(2,1)S(1)}, u32[]{:S(2)}) copy-start(bf16[512,1536]{1,0:T(8,128)(2,1)S(1)} %get-tuple-element.196) | copy-start | bytes 4718596
  175.8 3.2 copy-start.7
  253.6 3.5 copy-start.42
  320.0 3.8 copy-start.28
  320.0 3.8 copy-start.29
  320.0 3.8 copy-start.44
  320.0 8.5 %copy-start.45 = (f32[1024,768]{1,0:T(8,128)S(1)}, f32[1024,768]{1,0:T(8,128)}, u32[]{:S(2)}) copy-start(f32[1024,768]{1,0:T(8,128)} %fusion.12) | copy-start | bytes 9437188
  323.8 3.0 copy-start.40
  323.8 4.8 copy-start.41
  328.6 5.2 copy-start.18
  337.6 4.1 copy-start.46
  342.4 67.7 %copy-start.25 = (bf16[1280,192]{1,0:T(8,128)(2,1)S(1)}, bf16[1280,192]{1,0:T(8,128)(2,1)}, u32[]{:S(2)}) copy-start(bf16[1280,192]{1,0:T(8,128)(2,1)} %get-tuple-element.47) | copy-start | bytes 1474564
  420.7 5.3 copy-start.20
  420.7 162.8 %reduce-scatter.13.cloned.1.call-start = ((), (), s32[]{:S(2)}) async-start(), calls=%async_computation.10 | async-start | bytes 4423680
  474.4 153.7 %reduce-scatter.11.cloned.1.call-start = ((), (), s32[]{:S(2)}) async-start(), calls=%async_computation.9 | async-start | bytes 5898240 | tf_op jit(solution)/shard_map/reduce_scatter | solution.py:741
  484.9 231.4 %reduce-scatter.9.cloned.1.call-start = ((), (), s32[]{:S(2)}) async-start(), calls=%async_computation.8 | async-start | bytes 5898240 | tf_op jit(solution)/shard_map/reduce_scatter | solution.py:741
  558.1 11.4 %copy-start.37 = (f32[2,3]{1,0:T(2,128)S(1)}, f32[2,3]{1,0:T(2,128)}, u32[]{:S(2)}) copy-start(f32[2,3]{1,0:T(2,128)} %constant.119) | copy-start | bytes 76
  570.1 9.0 %copy-start.31 = (bf16[4,24,1536]{2,1,0:T(8,128)(2,1)S(1)}, bf16[4,24,1536]{2,1,0:T(8,128)(2,1)}, u32[]{:S(2)}) copy-start(bf16[4,24,1536]{2,1,0:T(8,128)(2,1)} %get-tuple-element.67) | copy-start | bytes 884740
  570.2 9.7 %copy-start.30 = (bf16[4,24,1536]{2,1,0:T(8,128)(2,1)S(1)}, bf16[4,24,1536]{2,1,0:T(8,128)(2,1)}, u32[]{:S(2)}) copy-start(bf16[4,24,1536]{2,1,0:T(8,128)(2,1)} %get-tuple-element.69) | copy-start | bytes 884740
  574.3 15.1 %collective-permute-start.7 = (bf16[2,192,192]{1,2,0:T(8,128)(2,1)S(1)}, bf16[2,192,192]{1,2,0:T(8,128)(2,1)S(1)}, u32[]{:S(2)}, u32[]{:S(2)}) collective-permute-start(bf16[2,192,192]{1,2,0:T(8,128)(2,1)S(1)} %copy.229), channel_id=1, source_target_pairs={{0,4},{4,0},{1,5},{5,1},{2,6},{6,2},{3,7},{7,3},{8,12},{12,8},{9,1... | collective-permute-start | bytes 442376 | tf_op jit(solution)/shard_map/ppermute | solution.py:745
  588.5 45.7 %collective-permute-start.6 = (bf16[2,192,576]{2,1,0:T(8,128)(2,1)}, bf16[2,192,576]{2,1,0:T(8,128)(2,1)}, u32[]{:S(2)}, u32[]{:S(2)}) collective-permute-start(bf16[2,192,576]{2,1,0:T(8,128)(2,1)} %copy.201), channel_id=1, source_target_pairs={{0,4},{4,0},{1,5},{5,1},{2,6},{6,2},{3,7},{7,3},{8,12},{12,8},{9,1... | collective-permute-start | bytes 1327112 | tf_op jit(solution)/shard_map/ppermute | solution.py:745
  630.0 93.5 %collective-permute-start.9 = (bf16[2,192,768]{2,1,0:T(8,128)(2,1)}, bf16[2,192,768]{2,1,0:T(8,128)(2,1)}, u32[]{:S(2)}, u32[]{:S(2)}) collective-permute-start(bf16[2,192,768]{2,1,0:T(8,128)(2,1)} %constant_dynamic-slice_fusion.1), channel_id=1, source_target_pairs={{0,4},{4,0},{1,5},{5,1},{2,6},{6,2},{3,7},{7,3},{8,12},{12,8},{9,1... | collective-permute-start | bytes 1769480 | tf_op jit(solution)/shard_map/ppermute | solution.py:745
  717.3 15.3 %collective-permute-start.8 = (bf16[2,192,768]{2,1,0:T(8,128)(2,1)S(1)}, bf16[2,192,768]{2,1,0:T(8,128)(2,1)}, u32[]{:S(2)}, u32[]{:S(2)}) collective-permute-start(bf16[2,192,768]{2,1,0:T(8,128)(2,1)S(1)} %constant_dynamic-slice_fusion.2), channel_id=1, source_target_pairs={{0,4},{4,0},{1,5},{5,1},{2,6},{6,2},{3,7},{7,3},{8,12},{12,8},{9,1... | collective-permute-start | bytes 1769480 | tf_op jit(solution)/shard_map/ppermute | solution.py:745
  724.8 7.9 %copy-start.22 = (bf16[2,384,768]{2,1,0:T(8,128)(2,1)S(1)}, bf16[2,384,768]{2,1,0:T(8,128)(2,1)}, u32[]{:S(2)}) copy-start(bf16[2,384,768]{2,1,0:T(8,128)(2,1)} %reduce-scatter.9.cloned.1.call-done) | copy-start | bytes 3538948
  (17 other events, 34.2 us)
Sparse Core Ops, SparseCore 0:
  32.5 76.2 all-gather.4
  110.4 28.5 all-gather.6
  141.2 88.8 all-gather.8
  232.1 87.8 all-gather.10
  420.8 26.9 reduce-scatter.14
  474.5 64.1 reduce-scatter.12
  541.0 87.1 reduce-scatter.10
  630.4 85.7 reduce-scatter.8

commit v3 on v2

--- a/solution.py
+++ b/solution.py
@@ -13,12 +13,101 @@
 VMEM_LIMIT = 60 * 1024 * 1024
 PLANE = ("ctx", "tp")
 TEXT_SLOTS = 96
-JOINT_STEP = 256
+MOST_GROUPS = 4
 QUERY_BLOCK = 256
 
 
 def dot(left, right, dims=((1,), (0,))):
     return lax.dot_general(left, right, (dims, ((), ())), preferred_element_type=F32)
+
+
+def local_call(kernel, steps, in_specs, outs, scratch, flops, name):
+    return pl.pallas_call(
+        kernel,
+        grid=(steps,),
+        in_specs=in_specs,
+        out_specs=[spec for spec, _ in outs],
+        out_shape=[shape for _, shape in outs],
+        scratch_shapes=scratch,
+        compiler_params=pltpu.CompilerParams(vmem_limit_bytes=VMEM_LIMIT),
+        cost_estimate=pl.CostEstimate(flops=flops, bytes_accessed=flops // 256, transcendentals=0),
+        name=name,
+    )
+
+
+def fixed(shape):
+    return pl.BlockSpec(shape, lambda i: (0,) * len(shape), pipeline_mode=pl.Buffered(1))
+
+
+def stepped(shape):
+    return pl.BlockSpec(shape, lambda i: (i,) + (0,) * (len(shape) - 1))
+
+
+def image_block(shape, last):
+    return pl.BlockSpec(shape, lambda i: (jnp.minimum(i, last),) + (0,) * (len(shape) - 1))
+
+
+def stream_block(shape, steps):
+    return pl.BlockSpec(shape, lambda i: (i // steps,) + (0,) * (len(shape) - 1))
+
+
+def padded(text):
+    return jnp.concatenate([text, jnp.zeros((QUERY_BLOCK - text.shape[0], text.shape[1]), text.dtype)], 0)
+
+
+def by_stream(steps, image_ref, text_ref, body):
+    step = pl.program_id(0)
+
+    @pl.when(step < steps)
+    def _():
+        body(image_ref[...], 0)
+
+    @pl.when(step >= steps)
+    def _():
+        body(padded(text_ref[...]), 1)
+
+
+def project_kernel(steps, image_ref, text_ref, mod_ref, weight_ref, bias_ref, normed_ref, q_ref, k_ref, v_ref, out_ref):
+    half = q_ref.shape[1]
+
+    def body(tokens, stream):
+        norm, _ = normalise(tokens.astype(F32))
+        normed = (norm * (1.0 + mod_ref[0, 1]) + mod_ref[0, 0]).astype(BF16)
+        normed_ref[...] = normed
+        joint = dot(normed, weight_ref[0, :, : 3 * half]) + bias_ref[0]
+        q_ref[...] = joint[:, :half].astype(BF16)
+        k_ref[...] = joint[:, half : 2 * half].astype(BF16)
+        v_ref[...] = joint[:, 2 * half :].astype(BF16)
+
+    by_stream(steps, image_ref, text_ref, body)
+
+    @pl.when(lax.rem(pl.program_id(0), steps) == 0)
+    def _():
+        out_ref[0] = weight_ref[0, :, 3 * half :]
+
+
+def project(image, text, mod, weight, bias):
+    (rows, width), wide = image.shape, weight.shape[2]
+    steps, half = rows // QUERY_BLOCK, wide // 4
+    joint = rows + QUERY_BLOCK
+    heads = [(stepped((QUERY_BLOCK, half)), jax.ShapeDtypeStruct((joint, half), BF16))] * 3
+    return local_call(
+        functools.partial(project_kernel, steps),
+        steps + 1,
+        [
+            image_block((QUERY_BLOCK, width), steps - 1),
+            fixed(text.shape),
+            stream_block((1,) + mod.shape[1:], steps),
+            stream_block((1,) + weight.shape[1:], steps),
+            stream_block((1,) + bias.shape[1:], steps),
+        ],
+        [(stepped((QUERY_BLOCK, width)), jax.ShapeDtypeStruct((joint, width), BF16))]
+        + heads
+        + [(stream_block((1, width, half), steps), jax.ShapeDtypeStruct((2, width, half), BF16))],
+        [],
+        6 * joint * width * half,
+        "project",
+    )(image, text, mod, weight, bias)
 
 
 def key_bias(rows, image_rows, text_rows):
@@ -29,13 +118,17 @@
     return jnp.where(masked, -1e30, 0.0).astype(F32)
 
 
-def attend_forward_kernel(heads, image_rows, text_rows, q_ref, k_ref, v_ref, o_ref, lse_ref, vt_ref):
-    @pl.when(pl.program_id(0) == 0)
+def attend_forward_kernel(
+    steps, heads, text_rows, q_ref, k_ref, v_ref, weight_ref, o_ref, lse_ref, image_ref, text_ref, vt_ref
+):
+    step = pl.program_id(0)
+
+    @pl.when(step == 0)
     def _():
         vt_ref[...] = v_ref[...].T
 
     rows = k_ref.shape[0]
-    bias = key_bias(rows, image_rows, text_rows)
+    bias = key_bias(rows, steps * QUERY_BLOCK, text_rows)
     queries_t = (q_ref[...] * HEAD_DIM ** (-0.5)).T
     outs = []
     for head in range(heads):
@@ -46,45 +139,84 @@
         total = jnp.sum(grown, axis=0, keepdims=True)
         lse_ref[head : head + 1] = top + jnp.log(total)
         outs.append(dot(vt_ref[span], grown.astype(BF16)) * (1.0 / total))
-    o_ref[...] = jnp.concatenate(outs, 0).T.astype(BF16)
-
-
-def attend_forward(q, k, v, image_rows, text_rows):
+    blended = jnp.concatenate(outs, 0).T.astype(BF16)
+    o_ref[...] = blended
+    branch = dot(blended, weight_ref[0], ((1,), (1,))).astype(BF16)
+
+    @pl.when(step < steps)
+    def _():
+        image_ref[...] = branch
+
+    @pl.when(step >= steps)
+    def _():
+        text_ref[...] = branch[: text_ref.shape[0]]
+
+
+def attend_forward(q, k, v, weight, text_all, text_rows):
     rows, wide = q.shape
+    width = weight.shape[1]
     heads = wide // HEAD_DIM
-    whole = pl.BlockSpec((rows, wide), lambda i: (0, 0))
-    block = pl.BlockSpec((QUERY_BLOCK, wide), lambda i: (i, 0))
-    return pl.pallas_call(
-        functools.partial(attend_forward_kernel, heads, image_rows, text_rows),
-        grid=(rows // QUERY_BLOCK,),
-        in_specs=[block, whole, whole],
-        out_specs=[block, pl.BlockSpec((heads, QUERY_BLOCK), lambda i: (0, i))],
-        out_shape=[
-            jax.ShapeDtypeStruct((rows, wide), BF16),
-            jax.ShapeDtypeStruct((heads, rows), F32),
+    steps = rows // QUERY_BLOCK - 1
+    return local_call(
+        functools.partial(attend_forward_kernel, steps, heads, text_rows),
+        steps + 1,
+        [
+            stepped((QUERY_BLOCK, wide)),
+            fixed((rows, wide)),
+            fixed((rows, wide)),
+            stream_block((1, width, wide), steps),
         ],
-        scratch_shapes=[pltpu.VMEM((wide, rows), BF16)],
-        compiler_params=pltpu.CompilerParams(vmem_limit_bytes=VMEM_LIMIT),
-        cost_estimate=pl.CostEstimate(
-            flops=4 * rows * rows * wide, bytes_accessed=8 * rows * wide, transcendentals=heads * rows * rows
-        ),
-        name="attend_forward",
-    )(q, k, v)
+        [
+            (stepped((QUERY_BLOCK, wide)), jax.ShapeDtypeStruct((rows, wide), BF16)),
+            (pl.BlockSpec((heads, QUERY_BLOCK), lambda i: (0, i)), jax.ShapeDtypeStruct((heads, rows), F32)),
+            (image_block((QUERY_BLOCK, width), steps - 1), jax.ShapeDtypeStruct((steps * QUERY_BLOCK, width), BF16)),
+            (pl.BlockSpec((text_all, width), lambda i: (0, 0)), jax.ShapeDtypeStruct((text_all, width), BF16)),
+        ],
+        [pltpu.VMEM((wide, rows), BF16)],
+        4 * rows * rows * wide,
+        "attend_forward",
+    )(q, k, v, weight)
 
 
 def attend_backward_kernel(
-    heads, image_rows, text_rows, q_ref, k_ref, v_ref, g_ref, lse_ref, dq_ref, dk_ref, dv_ref, kt_ref, dk_sum, dv_sum
+    steps,
+    heads,
+    text_rows,
+    q_ref,
+    k_ref,
+    v_ref,
+    o_ref,
+    lse_ref,
+    image_ref,
+    text_ref,
+    weight_ref,
+    dq_ref,
+    dk_ref,
+    dv_ref,
+    dw_ref,
+    kt_ref,
+    g_ref,
+    dk_sum,
+    dv_sum,
+    dw_sum,
 ):
     step = pl.program_id(0)
+    wide = q_ref.shape[1]
 
     @pl.when(step == 0)
     def _():
         kt_ref[...] = k_ref[...].T
         dk_sum[...] = jnp.zeros_like(dk_sum)
         dv_sum[...] = jnp.zeros_like(dv_sum)
-
+        dw_sum[...] = jnp.zeros_like(dw_sum)
+
+    def bring(arriving, stream):
+        g_ref[...] = dot(arriving, weight_ref[0]).astype(BF16)
+        dw_sum[stream] += dot(arriving, o_ref[...], ((0,), (0,)))
+
+    by_stream(steps, image_ref, text_ref, bring)
     rows = k_ref.shape[0]
-    bias = key_bias(rows, image_rows, text_rows)
+    bias = key_bias(rows, steps * QUERY_BLOCK, text_rows)
     queries = q_ref[...] * HEAD_DIM ** (-0.5)
     queries_t = queries.T
     grads = g_ref[...]
@@ -103,34 +235,146 @@
         outs.append(dot(kt_ref[span], grad_score) * HEAD_DIM ** (-0.5))
     dq_ref[...] = jnp.concatenate(outs, 0).T.astype(BF16)
 
-    @pl.when(step == pl.num_programs(0) - 1)
+    @pl.when(step == steps)
     def _():
         dk_ref[...] = jnp.concatenate([dk_sum[head] for head in range(heads)], 1).astype(BF16)
         dv_ref[...] = jnp.concatenate([dv_sum[head] for head in range(heads)], 1).astype(BF16)
-
-
-def attend_backward(q, k, v, grad, lse, image_rows, text_rows):
+        for stream in range(2):
+            dw_ref[:, stream * wide : (stream + 1) * wide] = dw_sum[stream].astype(BF16)
+
+
+def attend_backward(q, k, v, blended, lse, image, text, weight, text_rows):
     rows, wide = q.shape
+    width = weight.shape[1]
     heads = wide // HEAD_DIM
+    steps = rows // QUERY_BLOCK - 1
+    block = stepped((QUERY_BLOCK, wide))
     whole = pl.BlockSpec((rows, wide), lambda i: (0, 0))
-    block = pl.BlockSpec((QUERY_BLOCK, wide), lambda i: (i, 0))
-    return pl.pallas_call(
-        functools.partial(attend_backward_kernel, heads, image_rows, text_rows),
-        grid=(rows // QUERY_BLOCK,),
-        in_specs=[block, whole, whole, block, pl.BlockSpec((heads, QUERY_BLOCK), lambda i: (0, i))],
-        out_specs=[block, whole, whole],
-        out_shape=[jax.ShapeDtypeStruct((rows, wide), BF16)] * 3,
-        scratch_shapes=[
+    return local_call(
+        functools.partial(attend_backward_kernel, steps, heads, text_rows),
+        steps + 1,
+        [
+            block,
+            fixed((rows, wide)),
+            fixed((rows, wide)),
+            block,
+            pl.BlockSpec((heads, QUERY_BLOCK), lambda i: (0, i)),
+            image_block((QUERY_BLOCK, width), steps - 1),
+            fixed(text.shape),
+            stream_block((1, width, wide), steps),
+        ],
+        [
+            (block, jax.ShapeDtypeStruct((rows, wide), BF16)),
+            (whole, jax.ShapeDtypeStruct((rows, wide), BF16)),
+            (whole, jax.ShapeDtypeStruct((rows, wide), BF16)),
+            (pl.BlockSpec((width, 2 * wide), lambda i: (0, 0)), jax.ShapeDtypeStruct((width, 2 * wide), BF16)),
+        ],
+        [
             pltpu.VMEM((wide, rows), BF16),
+            pltpu.VMEM((QUERY_BLOCK, wide), BF16),
             pltpu.VMEM((heads, rows, HEAD_DIM), F32),
             pltpu.VMEM((heads, rows, HEAD_DIM), F32),
+            pltpu.VMEM((2, width, wide), F32),
         ],
-        compiler_params=pltpu.CompilerParams(vmem_limit_bytes=VMEM_LIMIT),
-        cost_estimate=pl.CostEstimate(
-            flops=10 * rows * rows * wide, bytes_accessed=14 * rows * wide, transcendentals=heads * rows * rows
-        ),
-        name="attend_backward",
-    )(q, k, v, grad, lse)
+        10 * rows * rows * wide,
+        "attend_backward",
+    )(q, k, v, blended, lse, image, text, weight)
+
+
+def unproject_kernel(
+    steps, dq_ref, dk_ref, dv_ref, normed_ref, weight_ref, image_ref, text_ref, dw_ref, sums_ref, dw_sum
+):
+    step = pl.program_id(0)
+    half = dq_ref.shape[1]
+    stream = step // steps
+
+    @pl.when(step == 0)
+    def _():
+        dw_sum[...] = jnp.zeros_like(dw_sum)
+        sums_ref[...] = jnp.zeros_like(sums_ref)
+
+    grads = jnp.concatenate([dq_ref[...], dk_ref[...], dv_ref[...]], 1)
+    part = dot(grads, weight_ref[0, :, : 3 * half], ((1,), (1,))).astype(BF16)
+    dw_sum[stream] += dot(normed_ref[...], grads, ((0,), (0,)))
+    sums_ref[stream] += jnp.sum(grads.astype(F32), axis=0, keepdims=True)
+
+    @pl.when(step < steps)
+    def _():
+        image_ref[...] = part
+
+    @pl.when(step == steps)
+    def _():
+        text_ref[...] = part[: text_ref.shape[0]]
+        for s in range(2):
+            dw_ref[:, s * 3 * half : (s + 1) * 3 * half] = dw_sum[s].astype(BF16)
+
+
+def unproject(dq, dk, dv, normed, weight, text_all):
+    rows, half = dq.shape
+    width = normed.shape[1]
+    steps = rows // QUERY_BLOCK - 1
+    block = stepped((QUERY_BLOCK, half))
+    return local_call(
+        functools.partial(unproject_kernel, steps),
+        steps + 1,
+        [block, block, block, stepped((QUERY_BLOCK, width)), stream_block((1,) + weight.shape[1:], steps)],
+        [
+            (image_block((QUERY_BLOCK, width), steps - 1), jax.ShapeDtypeStruct((steps * QUERY_BLOCK, width), BF16)),
+            (pl.BlockSpec((text_all, width), lambda i: (0, 0)), jax.ShapeDtypeStruct((text_all, width), BF16)),
+            (pl.BlockSpec((width, 6 * half), lambda i: (0, 0)), jax.ShapeDtypeStruct((width, 6 * half), BF16)),
+            (pl.BlockSpec((2, 1, 3 * half), lambda i: (0, 0, 0)), jax.ShapeDtypeStruct((2, 1, 3 * half), F32)),
+        ],
+        [pltpu.VMEM((2, width, 3 * half), F32)],
+        12 * rows * width * half,
+        "unproject",
+    )(dq, dk, dv, normed, weight)
+
+
+def feed_kernel(second_ref, cot_ref, up_ref, down_ref, bias_ref, feed_ref, pull_ref, dw_ref, sums_ref, up_sum, down_sum):
+    step = pl.program_id(0)
+    wide = up_ref.shape[1]
+
+    @pl.when(step == 0)
+    def _():
+        up_sum[...] = jnp.zeros_like(up_sum)
+        down_sum[...] = jnp.zeros_like(down_sum)
+        sums_ref[...] = jnp.zeros_like(sums_ref)
+
+    second, arriving = second_ref[...], cot_ref[...]
+    hidden = dot(second, up_ref[...]) + bias_ref[...]
+    gelu_out, slope = gelu_parts(hidden)
+    gelu_low = gelu_out.astype(BF16)
+    feed_ref[...] = dot(gelu_low, down_ref[...], ((1,), (1,))).astype(BF16)
+    down_sum[...] += dot(arriving, gelu_low, ((0,), (0,)))
+    pulled = (dot(arriving, down_ref[...]) * slope).astype(BF16)
+    sums_ref[...] += jnp.sum(pulled.astype(F32), axis=0, keepdims=True)
+    up_sum[...] += dot(second, pulled, ((0,), (0,)))
+    pull_ref[...] = dot(pulled, up_ref[...], ((1,), (1,))).astype(BF16)
+
+    @pl.when(step == pl.num_programs(0) - 1)
+    def _():
+        dw_ref[:, :wide] = up_sum[...].astype(BF16)
+        dw_ref[:, wide:] = down_sum[...].astype(BF16)
+
+
+def feed_forward(second, arriving, up, down, bias):
+    (rows, width), wide = second.shape, up.shape[1]
+    block_rows = QUERY_BLOCK if rows % QUERY_BLOCK == 0 else rows
+    block = stepped((block_rows, width))
+    return local_call(
+        feed_kernel,
+        rows // block_rows,
+        [block, block, fixed(up.shape), fixed(down.shape), fixed((1, wide))],
+        [
+            (block, jax.ShapeDtypeStruct((rows, width), BF16)),
+            (block, jax.ShapeDtypeStruct((rows, width), BF16)),
+            (pl.BlockSpec((width, 2 * wide), lambda i: (0, 0)), jax.ShapeDtypeStruct((width, 2 * wide), BF16)),
+            (pl.BlockSpec((1, wide), lambda i: (0, 0)), jax.ShapeDtypeStruct((1, wide), F32)),
+        ],
+        [pltpu.VMEM((width, wide), F32)] * 2,
+        12 * rows * width * wide,
+        "feed_forward",
+    )(second, arriving, up, down, bias.reshape(1, wide))
 
 
 def normalise(inputs):
@@ -301,28 +545,39 @@
     ]
 
 
-def spread_plane(wires, blocks):
+def block_halves(block):
+    cut = block.shape[-1] // 2
+    inner = (slice(None),) * (len(block.shape) - 4)
+    return inner + (pl.ds(0, cut),), inner + (pl.ds(cut, cut),)
+
+
+def spread_first(wires, block):
     x, y, k = wires.x, wires.y, wires.k
-    first = []
-    for block in blocks:
-        cut = block.shape[4] // 2
-        low, high = pl.ds(0, cut), pl.ds(cut, cut)
-        mine = block.at[x, y, k, :, low], block.at[x, y, k, :, high]
-        first.append((wires.copy(mine[0], mine[0], wires.x_next), wires.copy(mine[1], mine[1], wires.y_next)))
-    second = []
-    for block, (from_x, from_y) in zip(blocks, first):
-        cut = block.shape[4] // 2
-        low, high = pl.ds(0, cut), pl.ds(cut, cut)
-        from_x.wait_recv()
-        from_y.wait_recv()
-        lows, highs = block.at[:, y, k, :, low], block.at[x, :, k, :, high]
-        second.append((wires.copy(lows, lows, wires.y_next), wires.copy(highs, highs, wires.x_next)))
-    third = []
-    for block, (from_y, from_x) in zip(blocks, second):
-        from_y.wait_recv()
-        from_x.wait_recv()
-        gathered = block.at[:, :, k]
-        third.append(wires.copy(gathered, gathered, wires.k_next))
+    low, high = block_halves(block)
+    mine = block.at[(x, y, k) + low], block.at[(x, y, k) + high]
+    return wires.copy(mine[0], mine[0], wires.x_next), wires.copy(mine[1], mine[1], wires.y_next)
+
+
+def spread_second(wires, block, first):
+    x, y, k = wires.x, wires.y, wires.k
+    low, high = block_halves(block)
+    for arrived in first:
+        arrived.wait_recv()
+    lows, highs = block.at[(slice(None), y, k) + low], block.at[(x, slice(None), k) + high]
+    return wires.copy(lows, lows, wires.y_next), wires.copy(highs, highs, wires.x_next)
+
+
+def spread_third(wires, block, second):
+    for arrived in second:
+        arrived.wait_recv()
+    gathered = block.at[:, :, wires.k]
+    return wires.copy(gathered, gathered, wires.k_next)
+
+
+def spread_plane(wires, blocks, started=()):
+    first = list(started) + [spread_first(wires, block) for block in blocks[len(started) :]]
+    second = [spread_second(wires, block, arrived) for block, arrived in zip(blocks, first)]
+    third = [spread_third(wires, block, arrived) for block, arrived in zip(blocks, second)]
     for arrived in third:
         arrived.wait_recv()
 
@@ -343,17 +598,23 @@
 
 def enter_kernel(
     n_dp,
+    groups,
     part_ref,
     bias_ref,
     rows_ref,
     image_ref,
     text_ref,
+    attn_ref,
+    up_ref,
+    down_ref,
     mod_ref,
     rows_out,
     image_out,
     text_out,
+    gates_out,
+    attn_out,
+    ffn_out,
     mod_in,
-    local_sems,
     send_sems,
     recv_sems,
 ):
@@ -364,18 +625,12 @@
     peers = [lax.rem(me + offset, count) for offset in range(1, count)]
     others = [(peer // 2, peer % 2, tp) for peer in peers]
     lanes = [lax.rem(tp + offset, 4) for offset in range(1, 4)]
+    z_next = (lax.rem(dp + 1, n_dp), x, tp)
     wires.meet(others + [(dp, x, lane) for lane in lanes])
 
-    keep = [
-        pltpu.make_async_copy(image_ref, image_out.at[x], local_sems.at[0]),
-        pltpu.make_async_copy(text_ref, text_out.at[x], local_sems.at[1]),
-    ]
-    streams = ((image_ref, image_out), (text_ref, text_out))
     sums = [wires.copy(part_ref.at[peer // 2], mod_in.at[me], other) for peer, other in zip(peers, others)]
     rows = [wires.copy(rows_ref, rows_out.at[me], other) for other in others]
-    along_x = [wires.copy(ref.at[tp], out.at[x, tp], wires.x_next) for ref, out in streams]
-    for local in keep:
-        local.start()
+    swaps = [wires.copy(attn_ref.at[1 - x, s], attn_out.at[s, dp, x], wires.x_next) for s in range(2)]
     mod_in[me] = part_ref[dp]
     rows_out[me] = rows_ref[...]
     for arrived in sums:
@@ -385,6 +640,41 @@
         total = total + mod_in[source]
     mod_ref[tp] = total
     mods = [wires.copy(mod_ref.at[tp], mod_ref.at[tp], (dp, x, lane)) for lane in lanes]
+    for arrived in mods:
+        arrived.wait_recv()
+    gates = []
+    if groups > 1:
+        gates = [
+            wires.copy(mod_ref.at[:, 11], gates_out.at[dp], (lax.rem(dp + offset, groups), x, tp))
+            for offset in range(1, groups)
+        ]
+        for lane in range(4):
+            gates_out[dp, lane] = mod_ref[lane, 11]
+
+    ring = {(s, 0): wires.copy(attn_ref.at[x, s], attn_out.at[s, dp, x], z_next) for s in range(2)}
+
+    def pass_on(turn, side):
+        for s in range(2):
+            ring[s, side].wait_recv()
+            if turn < n_dp - 1:
+                origin = lax.rem(dp + n_dp - turn, n_dp)
+                block = attn_out.at[s, origin, x if side == 0 else 1 - x]
+                ring[s, side] = wires.copy(block, block, z_next)
+
+    streams = ((image_ref, image_out), (text_ref, text_out))
+    cols = ffn_out.shape[3]
+    wide = ffn_out.shape[0] // 2
+    held = []
+    for i, weight in enumerate((up_ref, down_ref)):
+        for s in range(wide):
+            given = weight.at[s, :, pl.ds(pl.multiple_of((1 - x) * cols, cols), cols)]
+            held.append((given, ffn_out.at[i * wide + s, x]))
+    for s, arrived in enumerate(swaps):
+        arrived.wait_recv()
+        block = attn_out.at[s, dp, 1 - x]
+        ring[s, 1] = wires.copy(block, block, z_next)
+    along_x = [wires.copy(ref.at[tp], out.at[x, tp], wires.x_next) for ref, out in streams]
+    pass_on(1, 0)
     along_y = []
     for (_, out), arrived in zip(streams, along_x):
         arrived.wait_recv()
@@ -394,66 +684,157 @@
     for _, out in streams:
         block = out.at[1 - x, tp]
         across.append(wires.copy(block, block, wires.k_next))
+    later = [wires.copy(given, place, wires.x_next) for given, place in held]
+
+    def keep_tokens(span):
+        for block in range(4):
+            image_out[x, block, span] = image_ref[block, span]
+
+    def keep_weights(span):
+        for s in range(2):
+            attn_out[s, dp, x, span] = attn_ref[x, s, span]
+        for i, weight in enumerate((up_ref, down_ref)):
+            for s in range(wide):
+                first, last = weight[s, span, :cols], weight[s, span, cols:]
+                ffn_out[i * wide + s, x, span] = jnp.where(x == 0, first, last)
+
+    over_rows(image_ref.shape[1], keep_tokens)
+    over_rows(attn_ref.shape[2], keep_weights)
+    for block in range(4):
+        text_out[x, block] = text_ref[block]
+    pass_on(1, 1)
     far = (1 - y) * 2 + k
     for (_, out), arrived in zip(streams, along_y):
         arrived.wait_recv()
         block = out.at[1 - x, far]
         across.append(wires.copy(block, block, wires.k_next))
-    for arrived in mods + rows + across:
-        arrived.wait_recv()
-    for local in keep:
-        local.wait()
+    for turn in range(2, n_dp - 1):
+        pass_on(turn, 0)
+        pass_on(turn, 1)
+    if n_dp > 2:
+        pass_on(n_dp - 1, 0)
+        pass_on(n_dp - 1, 1)
+    for arrived in rows + across + later + gates:
+        arrived.wait_recv()
     wires.finish()
 
 
-def enter(partial_mod, ada_bias, bias_rows, image, text):
-    n_dp, kinds, wide = partial_mod.shape
+def enter(groups, partial_mod, ada_bias, bias_rows, image, text, attn, up, down, wide):
+    n_dp, kinds, slice_width = partial_mod.shape
     count = 2 * n_dp
-    tp_n = image.shape[0]
+    rows, cols = up.shape[1], up.shape[2] // 2
+    width = image.shape[2]
     return comm_call(
-        functools.partial(enter_kernel, n_dp),
+        functools.partial(enter_kernel, n_dp, groups),
         [
-            jax.ShapeDtypeStruct((tp_n, kinds, wide), F32),
+            jax.ShapeDtypeStruct((4, kinds, slice_width), F32),
             jax.ShapeDtypeStruct((count,) + bias_rows.shape, F32),
             jax.ShapeDtypeStruct((2,) + image.shape, BF16),
             jax.ShapeDtypeStruct((2,) + text.shape, BF16),
+            jax.ShapeDtypeStruct((groups, 4, slice_width), F32),
+            jax.ShapeDtypeStruct((2, n_dp, 2) + attn.shape[2:], BF16),
+            jax.ShapeDtypeStruct((2 * wide, 2, rows, cols), BF16),
         ],
-        [pltpu.VMEM((count, kinds, wide), F32), pltpu.SemaphoreType.DMA((2,))],
-        2 * (count - 1) + 3 + 8,
+        [pltpu.VMEM((count, kinds, slice_width), F32)],
+        2 * (count - 1) + 2 + 4 * n_dp + 16 + groups + 5,
         0,
         "enter",
-        [VMEM_SPEC] * 3 + [ANY_SPEC] * 2,
-        [VMEM_SPEC] * 2 + [ANY_SPEC] * 2,
-    )(partial_mod, ada_bias, bias_rows, image, text)
+        [VMEM_SPEC] * 8,
+        [VMEM_SPEC] * 7,
+    )(partial_mod, ada_bias, bias_rows, image, text, attn, up, down)
+
+
+def meet_groups(wires, groups, more=()):
+    dp, x, tp = wires.dp, wires.x, wires.tp
+    count = groups * 2
+    if groups == 1:
+        others = [wires.x_next]
+    else:
+        peers = [lax.rem(dp * 2 + x + offset, count) for offset in range(1, count)]
+        others = [(peer // 2, peer % 2, tp) for peer in peers]
+    wires.meet(others + [wires.y_next, wires.k_next, *more])
+
+
+def start_moves(wires, groups, moved_ref, moved_out, local_sem):
+    if groups == 1:
+        return []
+    dp, x, tp = wires.dp, wires.x, wires.tp
+    count = groups * 2
+    me = dp * 2 + x
+    peers = [lax.rem(me + offset, count) for offset in range(1, count)]
+    local = pltpu.make_async_copy(moved_ref.at[me], moved_out.at[me], local_sem)
+    local.start()
+    return [local] + [
+        wires.copy(moved_ref.at[peer], moved_out.at[me], (peer // 2, peer % 2, tp)) for peer in peers
+    ]
+
+
+def end_moves(moves):
+    if moves:
+        moves[0].wait()
+    for arrived in moves[1:]:
+        arrived.wait_recv()
 
 
 def middle_kernel(
+    n_dp,
+    groups,
     image_part,
     text_part,
     image_x,
     text_x,
     mod_ref,
     bias_ref,
-    image_attention,
-    text_attention,
-    image_middle,
-    text_middle,
-    image_all,
-    text_all,
-    *scratch,
+    moved_ref,
+    *rest,
 ):
-    send_sems, recv_sems = scratch[-2:]
+    ffn_refs = rest[: n_dp - 1]
+    (
+        cot_ref,
+        image_attention,
+        text_attention,
+        image_middle,
+        text_middle,
+        image_all,
+        text_all,
+        cots_all,
+        moved_out,
+        ffn_out,
+    ) = rest[n_dp - 1 : n_dp + 9]
+    scratch = rest[n_dp + 9 :]
+    local_sem, send_sems, recv_sems = scratch[-3:]
     wires = Wires(send_sems, recv_sems)
-    x, y, k = wires.x, wires.y, wires.k
-    wires.meet([wires.x_next, wires.y_next, wires.k_next])
+    dp, x, y, k, tp = wires.dp, wires.x, wires.y, wires.k, wires.tp
+    z_next = (lax.rem(dp + 1, n_dp), x, tp)
+    meet_groups(wires, groups, [z_next] if groups == 1 else [])
+    cots = []
+    if groups > 1:
+        cots_all[x, y, k, dp] = cot_ref[...]
+        for offset in range(1, groups):
+            block = cots_all.at[x, y, k, dp]
+            cots.append(wires.copy(block, block, (lax.rem(dp + offset, groups), x, tp)))
+    last = wires.copy(ffn_refs[n_dp - 2], ffn_out.at[:, lax.rem(dp + 2, n_dp)], z_next)
     size = len(REDUCE_KEYS)
     streams = [
         dict(zip(("part",) + REDUCE_KEYS, (part,) + scratch[i * size : (i + 1) * size]))
         for i, part in enumerate((image_part, text_part))
     ]
+
+    def keep(span):
+        for turn, block in enumerate(ffn_refs):
+            for i in range(block.shape[0]):
+                ffn_out[i, lax.rem(dp + n_dp - turn, n_dp), span] = block[i, span]
+
     reduce_plane(wires, streams)
-    for i, (tokens, attention, middle, gathered) in enumerate(
-        ((image_x, image_attention, image_middle, image_all), (text_x, text_attention, text_middle, text_all))
+    for arrived in cots:
+        arrived.wait_recv()
+    gathers, started = [image_all, text_all], []
+    if groups > 1:
+        gathers, started = [cots_all] + gathers, [spread_first(wires, cots_all)]
+    zs = []
+    for i, tokens, attention, middle, gathered in (
+        (1, text_x, text_attention, text_middle, text_all.at[:, :, :, dp if groups > 1 else 0]),
+        (0, image_x, image_attention, image_middle, image_all),
     ):
         total = streams[i]["total"]
 
@@ -466,29 +847,44 @@
             gathered[x, y, k, span] = (norm * (1.0 + mod_ref[i, 4]) + mod_ref[i, 3]).astype(BF16)
 
         over_rows(total.shape[0], finish)
-    spread_plane(wires, [image_all, text_all])
+        if i == 1:
+            for offset in range(1, groups):
+                block = text_all.at[x, y, k, dp]
+                zs.append(wires.copy(block, block, (lax.rem(dp + offset, groups), x, tp)))
+    for arrived in zs:
+        arrived.wait_recv()
+    moves = start_moves(wires, groups, moved_ref, moved_out, local_sem)
+    over_rows(ffn_out.shape[2], keep)
+    spread_plane(wires, gathers, started)
+    end_moves(moves)
+    last.wait_recv()
     wires.finish()
 
 
-def middle_step(image_part, text_part, image_x, text_x, mod, bias):
+def middle_step(groups, image_part, text_part, image_x, text_x, mod, bias, moved, ffn, cot):
     (image_rows, width), text_rows = image_x.shape, text_x.shape[0]
     outs = []
     for _ in range(2):
         outs += [jax.ShapeDtypeStruct((rows, width), F32) for rows in (image_rows, text_rows)]
-    outs += [jax.ShapeDtypeStruct(part.shape, BF16) for part in (image_part, text_part)]
+    outs += [jax.ShapeDtypeStruct(image_part.shape, BF16)]
+    outs += [jax.ShapeDtypeStruct((2, 2, 2, groups, text_rows, width), BF16)] * 2
+    outs += [jax.ShapeDtypeStruct(moved.shape, BF16)]
+    n_dp = len(ffn) + 1
+    outs += [jax.ShapeDtypeStruct((ffn[0].shape[0], n_dp) + ffn[0].shape[1:], BF16)]
     return comm_call(
-        middle_kernel,
+        functools.partial(middle_kernel, n_dp, groups),
         outs,
-        reduce_scratch(image_rows, width) + reduce_scratch(text_rows, width),
-        20,
+        reduce_scratch(image_rows, width) + reduce_scratch(text_rows, width) + [pltpu.SemaphoreType.DMA(())],
+        30 + 4 * groups,
         1,
         "middle",
-        [VMEM_SPEC] * 6,
-        [VMEM_SPEC] * 6,
-    )(image_part, text_part, image_x, text_x, mod, bias)
+        [VMEM_SPEC] * 6 + [ANY_SPEC] + [VMEM_SPEC] * n_dp,
+        [VMEM_SPEC] * 7 + [ANY_SPEC, VMEM_SPEC],
+    )(image_part, text_part, image_x, text_x, mod, bias, moved, *ffn, cot)
 
 
 def turn_kernel(
+    groups,
     valid_ref,
     image_feed,
     text_feed,
@@ -502,6 +898,7 @@
     text_cot,
     mod_ref,
     bias_ref,
+    moved_ref,
     image_out,
     text_out,
     image_grad,
@@ -509,25 +906,46 @@
     sums_ref,
     image_all,
     text_all,
+    moved_out,
     *scratch,
 ):
-    send_sems, recv_sems = scratch[-2:]
+    z_out, z_in, local_sem, send_sems, recv_sems = scratch[-5:]
     wires = Wires(send_sems, recv_sems)
-    x, y, k = wires.x, wires.y, wires.k
-    wires.meet([wires.x_next, wires.y_next, wires.k_next])
+    dp, x, y, k, tp = wires.dp, wires.x, wires.y, wires.k, wires.tp
+    meet_groups(wires, groups)
     size = len(REDUCE_KEYS)
     streams = [
         dict(zip(("part",) + REDUCE_KEYS, (part,) + scratch[i * size : (i + 1) * size]))
-        for i, part in enumerate((image_second, text_second, image_feed, text_feed))
+        for i, part in enumerate((text_second, text_feed, image_second, image_feed))
     ]
     reduce_plane(wires, streams)
+    streams = [streams[2], streams[0], streams[3], streams[1]]
+    zs = []
+    rows = text_middle.shape[0]
+    if groups > 1:
+        for i in range(2):
+            total = streams[1 + 2 * i]["total"]
+            for group in range(groups):
+                z_out[i, group] = total[group * rows : (group + 1) * rows].astype(BF16)
+            z_in[i, dp] = z_out[i, dp]
+            for offset in range(1, groups):
+                plane = lax.rem(dp + offset, groups)
+                zs.append(wires.copy(z_out.at[i, plane], z_in.at[i, dp], (plane, x, tp)))
     sums_ref[...] = jnp.zeros_like(sums_ref)
-    groups = (
+    sides = (
         (image_attention, image_middle, image_cot, image_out, image_grad, image_all),
         (text_attention, text_middle, text_cot, text_out, text_grad, text_all),
     )
-    for i, (attention, middle, cot, out, grad, gathered) in enumerate(groups):
+    for i, (attention, middle, cot, out, grad, gathered) in enumerate(sides):
         second, feed = streams[i]["total"], streams[2 + i]["total"]
+        if i == 1 and groups > 1:
+            for arrived in zs:
+                arrived.wait_recv()
+            for j, total in enumerate((second, feed)):
+                summed = z_in[j, 0].astype(F32)
+                for group in range(1, groups):
+                    summed = summed + z_in[j, group].astype(F32)
+                total[0:rows] = summed
 
         def finish(span, i=i, attention=attention, middle=middle, cot=cot, out=out, grad=grad, gathered=gathered, second=second, feed=feed):
             branch, value, arriving, pulled = attention[span], middle[span], cot[span].astype(F32), second[span]
@@ -559,25 +977,35 @@
             for t, term in enumerate(terms):
                 sums_ref[i, t : t + 1] += jnp.sum(term, axis=0, keepdims=True)
 
-        over_rows(second.shape[0], finish)
+        over_rows(middle.shape[0], finish)
+    moves = start_moves(wires, groups, moved_ref, moved_out, local_sem)
     spread_plane(wires, [image_all, text_all])
+    end_moves(moves)
     wires.finish()
 
 
-def turn_step(valid, feeds, seconds, attentions, middles, cots, mod, bias):
+def turn_step(groups, valid, feeds, seconds, attentions, middles, cots, mod, bias, moved):
     width = middles[0].shape[1]
     rows = [part.shape[0] for part in middles]
     outs = [jax.ShapeDtypeStruct((r, width), BF16) for r in rows]
     outs += [jax.ShapeDtypeStruct((r, width), F32) for r in rows]
     outs += [jax.ShapeDtypeStruct((2, 16, width), F32)]
-    outs += [jax.ShapeDtypeStruct(part.shape, BF16) for part in feeds]
+    outs += [jax.ShapeDtypeStruct((2, 2, 2, r, width), BF16) for r in rows]
+    outs += [jax.ShapeDtypeStruct(moved.shape, BF16)]
     scratch = []
-    for _ in range(2):
-        for r in rows:
-            scratch += reduce_scratch(r, width)
+    for r in (rows[1] * groups, rows[0]):
+        scratch += reduce_scratch(r, width) + reduce_scratch(r, width)
+    scratch += [pltpu.VMEM((2, groups, rows[1], width), BF16)] * 2 + [pltpu.SemaphoreType.DMA(())]
     return comm_call(
-        turn_kernel, outs, scratch, 30, 2, "turn", [VMEM_SPEC] * 13, [VMEM_SPEC] * 7
-    )(valid, *feeds, *seconds, *attentions, *middles, *cots, mod, bias)
+        functools.partial(turn_kernel, groups),
+        outs,
+        scratch,
+        30 + 4 * groups,
+        2,
+        "turn",
+        [VMEM_SPEC] * 13 + [ANY_SPEC],
+        [VMEM_SPEC] * 7 + [ANY_SPEC],
+    )(valid, *feeds, *seconds, *attentions, *middles, *cots, mod, bias, moved)
 
 
 PACKED = 24
@@ -728,23 +1156,22 @@
     )(part)
 
 
-def gather_rows(shard, ctx):
-    pairs = [(0, 1), (1, 0)]
-    kept = lax.dynamic_index_in_dim(shard, ctx, 2, keepdims=False)
-    given = lax.dynamic_index_in_dim(shard, 1 - ctx, 2, keepdims=False)
-    other = lax.ppermute(given, "ctx", pairs)
-    first, last = jnp.where(ctx == 0, kept, other), jnp.where(ctx == 0, other, kept)
-    return lax.all_gather(jnp.concatenate([first, last], 1), "dp", axis=1, tiled=True)
-
-
-def scatter_rows(grad, ctx):
-    mine = lax.psum_scatter(grad.astype(BF16), "dp", scatter_dimension=1, tiled=True)
-    rows = mine.shape[1] // 2
-    kept = lax.dynamic_slice_in_dim(mine, ctx * rows, rows, 1)
-    given = lax.dynamic_slice_in_dim(mine, (1 - ctx) * rows, rows, 1)
+def scatter_rows(grad):
+    return lax.psum_scatter(grad, "dp", scatter_dimension=0, tiled=True)
+
+
+def swap_halves(mine, ctx):
+    rows = mine.shape[0] // 2
+    kept = lax.dynamic_slice_in_dim(mine, ctx * rows, rows, 0)
+    given = lax.dynamic_slice_in_dim(mine, (1 - ctx) * rows, rows, 0)
     other = lax.ppermute(given, "ctx", [(0, 1), (1, 0)])
     first, last = jnp.where(ctx == 0, kept, other), jnp.where(ctx == 0, other, kept)
     return first.astype(F32), last.astype(F32)
+
+
+def swap_streams(mine, ctx):
+    rows, cols = mine.shape[0] // 2, mine.shape[1] // 2
+    return [part.reshape(rows, 2, cols).transpose(1, 0, 2) for part in swap_halves(mine, ctx)]
 
 
 def on_device(
@@ -774,123 +1201,186 @@
     own_rows = (image_length // tp_n, TEXT_SLOTS // tp_n)
     image_all = image_length * ctx_n
     text_all = TEXT_SLOTS * ctx_n
-    joint_pad = -(image_all + text_all) % JOINT_STEP
     pad = ((0, TEXT_SLOTS - text_length), (0, 0))
 
-    qkv_full = gather_rows(
-        qkv_weight.reshape(2, shard_rows, 3, ctx_n, half)
-        .transpose(0, 1, 3, 2, 4)
-        .reshape(2, shard_rows, ctx_n, 3 * half),
-        ctx,
-    )
-    out_full = gather_rows(out_weight.reshape(2, shard_rows, ctx_n, half), ctx)
-    up_full = gather_rows(up_weight.reshape(2, shard_rows, ctx_n, up_half), ctx)
-    down_full = gather_rows(down_weight.reshape(2, shard_rows, ctx_n, up_half), ctx)
-    qv_own = lax.dynamic_slice_in_dim(qv_bias, ctx * half, half, 2).astype(F32)
-    up_bias_own = lax.dynamic_slice_in_dim(up_bias, ctx * up_half, up_half, 1).astype(F32)
+    groups = dp_n if dp_n <= MOST_GROUPS else 1
+    wide = 1 if groups > 1 else 2
+    text_cols = up_half // groups
+    text_start = ctx * up_half + (dp * text_cols if groups > 1 else 0)
 
     tokens = (image_tokens[0], jnp.pad(text_tokens[0], pad))
     cotangents = (image_cotangent[0], jnp.pad(text_cotangent[0], pad))
+
+    def own(parts):
+        return [lax.dynamic_slice_in_dim(part, tp * rows, rows, 0) for part, rows in zip(parts, own_rows)]
+
+    tokens_own, cotangents_own = own(tokens), own(cotangents)
     cond_float = conditioning.astype(F32)
     activated_low = jax.nn.silu(cond_float).astype(BF16)
     partial_mod = jnp.einsum("nd,adkf->nakf", activated_low, ada_weight, preferred_element_type=F32)
-    mod_blocks, bias_blocks, image_blocks, text_blocks = enter(
+    (
+        mod_blocks,
+        bias_blocks,
+        image_blocks,
+        text_blocks,
+        text_gates,
+        attn_full,
+        ffn_mixed,
+    ) = enter(
+        groups,
         partial_mod.reshape(dp_n, 12, slice_width),
         ada_bias.astype(F32).reshape(12, slice_width),
         jnp.concatenate([out_bias, down_bias], 0).astype(F32),
         *[part.reshape(tp_n, rows, width) for part, rows in zip(tokens, own_rows)],
-    )
+        jnp.stack(
+            [
+                jnp.concatenate(
+                    [qkv_weight[:, :, j, c * half : (c + 1) * half] for j in range(3)]
+                    + [out_weight[:, :, c * half : (c + 1) * half]],
+                    2,
+                )
+                for c in range(ctx_n)
+            ]
+        ),
+        up_weight,
+        down_weight,
+        wide,
+    )
+    cotangents = (lax.optimization_barrier((cotangents[0], mod_blocks))[0], cotangents[1])
+    attn_full = attn_full.reshape(2, width, 4 * half)
+    ffn_blocks = [ffn_mixed.reshape(2 * wide, 2 * shard_rows, up_half)]
+    around = [(i, (i + 1) % dp_n) for i in range(dp_n)]
+    ffn_blocks.append(lax.ppermute(ffn_blocks[0], "dp", around))
     modulation = mod_blocks.transpose(1, 0, 2).reshape(2, 6, width)
     biases = bias_blocks.transpose(1, 0, 2).reshape(4, width)
     mod_rows = modulation[:, :, None]
     out_bias_rows, down_bias_rows = biases[:2, None], biases[2:, None]
     tokens_all = (image_blocks.reshape(image_all, width), text_blocks.reshape(text_all, width))
-    cotangents_all = []
-    for part in cotangents:
+    qv_own = lax.dynamic_slice_in_dim(qv_bias, ctx * half, half, 2).astype(F32)
+    up_bias_own = (
+        lax.dynamic_slice_in_dim(up_bias[0], ctx * up_half, up_half, 0).astype(F32),
+        lax.dynamic_slice_in_dim(up_bias[1], text_start, text_cols, 0).astype(F32),
+    )
+    slots = tp * own_rows[1] + lax.broadcasted_iota(jnp.int32, (own_rows[1], 1), 0)
+    valid = jnp.broadcast_to((slots < text_length).astype(F32), (own_rows[1], width))
+
+    def to_devices(weight):
+        parts = weight.reshape(shard_rows, ctx_n, dp_n, text_cols)
+        return parts.transpose(2, 1, 0, 3).reshape(dp_n * ctx_n, shard_rows, text_cols)
+
+    if groups > 1:
+        moved = jnp.concatenate([to_devices(up_weight[1]), to_devices(down_weight[1])], 2)
+    else:
+        moved = jnp.zeros((1, 8, 128), BF16)
+
+    def both_halves(part):
         other = lax.ppermute(part, "ctx", [(0, 1), (1, 0)])
         first, last = jnp.where(ctx == 0, part, other), jnp.where(ctx == 0, other, part)
-        cotangents_all.append(jnp.concatenate([first, last], 0))
-
-    def own(parts):
-        return [lax.dynamic_slice_in_dim(part, tp * rows, rows, 0) for part, rows in zip(parts, own_rows)]
-
-    tokens_own, cotangents_own = own(tokens), own(cotangents)
-    slots = tp * own_rows[1] + lax.broadcasted_iota(jnp.int32, (own_rows[1], 1), 0)
-    valid = jnp.broadcast_to((slots < text_length).astype(F32), (own_rows[1], width))
+        return jnp.concatenate([first, last], 0)
+
+    def feed_grad(stream):
+        return (both_halves(cotangents[stream]).astype(F32) * modulation[stream, 5]).astype(BF16)
 
     def blocks(part):
         return part.reshape(2, 2, 2, part.shape[0] // 8, width)
 
-    normed_low, qkv_parts = [], []
+    qv_bias_rows = jnp.concatenate([qv_own[:, 0], jnp.zeros((2, half), F32), qv_own[:, 1]], 1)[:, None]
+    normed_low, queries, keys, values, out_full = project(
+        *tokens_all, mod_rows[:, :2], attn_full, qv_bias_rows
+    )
+    queries, ffn_blocks[1] = lax.optimization_barrier((queries, ffn_blocks[1]))
+    for _ in range(dp_n - 3):
+        ffn_blocks.append(lax.ppermute(ffn_blocks[-1], "dp", around))
+    blended, lse, *out_parts = attend_forward(queries, keys, values, out_full, text_all, text_length)
+    out_parts = [blocks(part) for part in out_parts]
+    *attentions_middles, image_second, text_second, text_cots, moved_in, ffn_full = middle_step(
+        groups, *out_parts, *tokens_own, mod_rows, out_bias_rows, moved, ffn_blocks, cotangents_own[1]
+    )
+    ffn_full = ffn_full.reshape(2 * wide, width, up_half)
+    attentions, middles = attentions_middles[:2], attentions_middles[2:]
+    second_low = (image_second.reshape(-1, width), text_second.reshape(-1, width))
+
+    up_full, down_full = [ffn_full[0]], [ffn_full[wide]]
+    if groups > 1:
+        moved_in = moved_in.reshape(width, 2 * text_cols)
+        up_full.append(moved_in[:, :text_cols])
+        down_full.append(moved_in[:, text_cols:])
+        gates = text_gates.reshape(groups, 1, width)
+        feed_grads = (
+            feed_grad(0),
+            (text_cots.reshape(8, groups, own_rows[1], width).astype(F32) * gates).astype(BF16).reshape(-1, width),
+        )
+    else:
+        up_full.append(ffn_full[1])
+        down_full.append(ffn_full[3])
+        feed_grads = (feed_grad(0), feed_grad(1))
+    feed_parts, second_parts, ffn_grads, up_bias_grads = [], [], [], []
     for stream in range(2):
-        norm, _ = normalise(tokens_all[stream].astype(F32))
-        normed = (norm * (1.0 + modulation[stream, 1]) + modulation[stream, 0]).astype(BF16)
-        normed_low.append(normed)
-        bias = jnp.concatenate([qv_own[stream, 0], jnp.zeros((half,), F32), qv_own[stream, 1]])
-        qkv_parts.append((dot(normed, qkv_full[stream]) + bias).astype(BF16))
-    joint = jnp.concatenate(qkv_parts + [jnp.zeros((joint_pad, 3 * half), BF16)], 0)
-    queries, keys, values = joint[:, :half], joint[:, half : 2 * half], joint[:, 2 * half :]
-    blended, lse = attend_forward(queries, keys, values, image_all, text_length)
-    blended_parts = (blended[:image_all], blended[image_all : image_all + text_all])
-    out_parts = [
-        blocks(dot(blended_parts[s], out_full[s], ((1,), (1,))).astype(BF16)) for s in range(2)
+        feed, pulled, grads, sums = feed_forward(
+            second_low[stream], feed_grads[stream], up_full[stream], down_full[stream], up_bias_own[stream]
+        )
+        feed_parts.append(blocks(feed))
+        second_parts.append(blocks(pulled))
+        ffn_grads.append(grads)
+        up_bias_grads.append(sums[0])
+    if groups > 1:
+        ffn_mine = scatter_rows(ffn_grads[0])
+        moved = ffn_grads[1].reshape(dp_n * ctx_n, shard_rows, 2 * text_cols)
+    else:
+        ffn_mine = scatter_rows(jnp.concatenate(ffn_grads, 1))
+    image_out, text_out, image_middle_grad, text_middle_grad, sums, image_attn, text_attn, moved_in = turn_step(
+        groups, valid, feed_parts, second_parts, attentions, middles, cotangents_own, mod_rows, down_bias_rows, moved
+    )
+    attention_grad_all = (image_attn.reshape(-1, width), text_attn.reshape(-1, width))
+    if groups > 1:
+        back = (
+            moved_in.reshape(dp_n, ctx_n, shard_rows, 2, text_cols)
+            .transpose(3, 2, 1, 0, 4)
+            .reshape(2, shard_rows, ctx_n * up_half)
+            .astype(F32)
+        )
+
+    grad_queries, grad_keys, grad_values, out_weight_grads = attend_backward(
+        queries, keys, values, blended, lse, *attention_grad_all, out_full, text_length
+    )
+    out_weight_grads, ffn_mine = lax.optimization_barrier((out_weight_grads, ffn_mine))
+    out_mine = scatter_rows(out_weight_grads)
+    *normed_parts, qkv_weight_grads, joint_sums = unproject(
+        grad_queries, grad_keys, grad_values, normed_low, attn_full, text_all
+    )
+    normed_parts = [blocks(part) for part in normed_parts]
+    qkv_weight_grads, out_mine = lax.optimization_barrier((qkv_weight_grads, out_mine))
+    qkv_mine = scatter_rows(qkv_weight_grads)
+    qv_bias_grads = [
+        jnp.concatenate([joint_sums[stream, 0, :half], joint_sums[stream, 0, 2 * half :]]) for stream in range(2)
     ]
-    *attentions_middles, image_second, text_second = middle_step(
-        *out_parts, *tokens_own, mod_rows, out_bias_rows
-    )
-    attentions, middles = attentions_middles[:2], attentions_middles[2:]
-    second_low = (image_second.reshape(image_all, width), text_second.reshape(text_all, width))
-
-    feed_parts, second_parts = [], []
-    down_weight_grads, up_weight_grads, up_bias_grads = [], [], []
-    for stream in range(2):
-        hidden = dot(second_low[stream], up_full[stream]) + up_bias_own[stream]
-        gelu_out, slope = gelu_parts(hidden)
-        gelu_low = gelu_out.astype(BF16)
-        feed_parts.append(blocks(dot(gelu_low, down_full[stream], ((1,), (1,))).astype(BF16)))
-        grad_feed = (cotangents_all[stream].astype(F32) * modulation[stream, 5]).astype(BF16)
-        down_weight_grads.append(dot(grad_feed, gelu_low, ((0,), (0,))))
-        grad_hidden = (dot(grad_feed, down_full[stream]) * slope).astype(BF16)
-        up_bias_grads.append(jnp.sum(grad_hidden.astype(F32), axis=0))
-        up_weight_grads.append(dot(second_low[stream], grad_hidden, ((0,), (0,))))
-        second_parts.append(blocks(dot(grad_hidden, up_full[stream], ((1,), (1,))).astype(BF16)))
-    down_weight_grad = jnp.concatenate(scatter_rows(jnp.stack(down_weight_grads), ctx), 2)
-    up_weight_grad = jnp.concatenate(scatter_rows(jnp.stack(up_weight_grads), ctx), 2)
-    image_out, text_out, image_middle_grad, text_middle_grad, sums, image_attn, text_attn = turn_step(
-        valid, feed_parts, second_parts, attentions, middles, cotangents_own, mod_rows, down_bias_rows
-    )
-    attention_grad_all = (image_attn.reshape(image_all, width), text_attn.reshape(text_all, width))
-
-    out_weight_grads, blended_grads = [], []
-    for stream in range(2):
-        out_weight_grads.append(dot(attention_grad_all[stream], blended_parts[stream], ((0,), (0,))))
-        blended_grads.append(dot(attention_grad_all[stream], out_full[stream]).astype(BF16))
-    grad_queries, grad_keys, grad_values = attend_backward(
-        queries,
-        keys,
-        values,
-        jnp.concatenate(blended_grads + [jnp.zeros((joint_pad, half), BF16)], 0),
-        lse,
-        image_all,
-        text_length,
-    )
-    grad_joint = jnp.concatenate([grad_queries, grad_keys, grad_values], 1)
-    grad_parts = (grad_joint[:image_all], grad_joint[image_all : image_all + text_all])
-    qkv_weight_grads, qv_bias_grads, normed_parts = [], [], []
-    for stream in range(2):
-        sums_joint = jnp.sum(grad_parts[stream].astype(F32), axis=0)
-        qv_bias_grads.append(jnp.concatenate([sums_joint[:half], sums_joint[2 * half :]]))
-        qkv_weight_grads.append(dot(normed_low[stream], grad_parts[stream], ((0,), (0,))))
-        normed_parts.append(blocks(dot(grad_parts[stream], qkv_full[stream], ((1,), (1,))).astype(BF16)))
-    out_weight_grad = jnp.concatenate(scatter_rows(jnp.stack(out_weight_grads), ctx), 2)
     qkv_weight_grad = jnp.concatenate(
-        [part.reshape(2, shard_rows, 3, half) for part in scatter_rows(jnp.stack(qkv_weight_grads), ctx)], 3
-    )
-
+        [part.reshape(2, shard_rows, 3, half) for part in swap_streams(qkv_mine, ctx)], 3
+    )
+    out_weight_grad = jnp.concatenate(swap_streams(out_mine, ctx), 2)
+    ffn_halves = swap_halves(ffn_mine, ctx)
+    if groups > 1:
+        up_weight_grad, down_weight_grad = [
+            jnp.stack([jnp.concatenate([part[:, i * up_half : (i + 1) * up_half] for part in ffn_halves], 1), back[i]])
+            for i in range(2)
+        ]
+    else:
+        up_weight_grad, down_weight_grad = [
+            jnp.stack(
+                [
+                    jnp.concatenate([part[:, c * up_half : (c + 1) * up_half] for part in ffn_halves], 1)
+                    for c in (i, 2 + i)
+                ]
+            )
+            for i in range(2)
+        ]
+
+    if groups > 1:
+        up_bias_grads[1] = lax.dynamic_update_slice_in_dim(
+            jnp.zeros((up_half,), F32), up_bias_grads[1], dp * text_cols, 0
+        )
     halves = jnp.concatenate(
-        [part.reshape(-1, slice_width) for part in (*qv_bias_grads, *up_bias_grads)]
-        + [jnp.zeros((2, slice_width), F32)],
-        0,
+        [part.reshape(-1, slice_width) for part in (*qv_bias_grads, *up_bias_grads)], 0
     )
     image_outs, text_outs, image_grads, text_grads, packed, halves_all = leave_step(
         dp_n,

time: 756 us -> 628 us (0.83)
  Pallas kernels: 275 us -> 473 us
  waiting for transfers between devices: 208 us -> 29.9 us
  matrix products: 82.2 us -> 3.36 us
  local copies, waits for them, and re-layouts: 96.2 us -> 65.9 us
  other arithmetic: 53.2 us -> 28.2 us
  starting transfers between devices: 15.3 us -> 6.42 us
    pallas_call x5 -> x9, Pallas kernels: 216 us -> 411 us  [the longest x1 115 us: turn_step(): comm_call(functools.partial(turn_kernel, groups), outs, scratch, 30 + 4 *...]
    reduce_scatter x2 -> x3, waiting for transfers between devices: 117 us -> 13.6 us  [scatter_rows(): return lax.psum_scatter(grad, 'dp', scatter_dimension=0, tiled=True)]
    dot_general x24 -> x0, matrix products: 78.8 us -> none  [dot(): lax.dot_general(left, right, (dims, ((), ())), preferred_element_type=F32)]
    all_gather x4 -> x0, waiting for transfers between devices: 57.1 us -> none  [gather_rows(): lax.all_gather(jnp.concatenate([first, last], 1), 'dp', axis=1, tiled=True)]
    unnamed x114 -> x75, local copies, waits for them, and re-layouts: 43.1 us -> 10.9 us
    slice x5 -> x17, local copies, waits for them, and re-layouts: 1.65 us -> 27.7 us  [the longest x5 19.6 us: on_device(): back[i]]
    ppermute x10 -> x6, waiting for transfers between devices: 33.9 us -> 16.2 us  [the longest x3 6.91 us: swap_halves(): other = lax.ppermute(given, 'ctx', [(0, 1), (1, 0)])]
    reshape x5 -> x6, local copies, waits for them, and re-layouts: 13.9 us -> 0.82 us  [swap_streams(): part.reshape(rows, 2, cols).transpose(1, 0, 2)]
  transfers between devices with their start and end apart: 18 -> 9, of which waited for: 7 -> 5; matrix products, arithmetic and copies ran while one was open for 24% -> 12% of each run, Pallas kernels for 28% -> 41%
where the time goes in v3:
time: 628 us; the launch traced here: 621 us
  Pallas kernels  473 us (75%)
  local copies, waits for them, and re-layouts  65.9 us (10%)
  waiting for transfers between devices  29.9 us (5%)
  other arithmetic  28.2 us (4%)
  between operations  14.8 us (2%)
  starting transfers between devices  6.42 us (1%)
    pallas_call x1, Pallas kernels, turn_step(): comm_call(functools.partial(turn_kernel, groups), outs, scratch, 30 + 4 *...  115 us
    pallas_call x1, Pallas kernels, enter(): comm_call(functools.partial(enter_kernel, n_dp, groups), [jax.ShapeDtypeS...  102 us
    pallas_call x1, Pallas kernels, middle_step(): comm_call(functools.partial(middle_kernel, n_dp, groups), outs, reduce_sc...  93.4 us
    pallas_call x1, Pallas kernels, leave_step(): comm_call(functools.partial(leave_kernel, n_dp), outs, scratch, 1 + 10 +...  55.6 us
    pallas_call x2, Pallas kernels, feed_forward(): local_call(feed_kernel, rows // block_rows, [block, block, fixed(up.shape...  33.7 us
    pallas_call x1, Pallas kernels, attend_backward(): local_call(functools.partial(attend_backward_kernel, steps, heads, text_r...  23.5 us
    slice x5, local copies, waits for them, and re-layouts, on_device(): back[i]  19.6 us
    pallas_call x1, Pallas kernels, attend_forward(): local_call(functools.partial(attend_forward_kernel, steps, heads, text_ro...  18.8 us
  transfers between devices with their start and end apart: 9, of which 5 were waited for; matrix products, arithmetic and copies ran while one was open for 12% of the time, Pallas kernels for 41%

profile of v3, /device:TPU:0, one launch (start us, length us, event | category | flops | bytes accessed | tf_op | source)
XLA Modules:
  0.0 621.2 jit_solution(14607820202144109526)
XLA Ops:
  7.3 1.7 slice_bitcast_fusion.5
  11.4 1.1 pad_maximum_fusion.2.attn_ref
  13.8 101.6 %enter.1 = (f32[4,12,384]{2,1,0:T(8,128)}, f32[8,4,192]{2,1,0:T(4,128)}, bf16[2,4,128,1536]{3,2,1,0:T(8,128)(2,1)}, bf16[2,4,24,1536]{3,2,1,0:T(8,128)(2,1)}, f3...) custom-call(f32[4,12,384]{2,1,0:T(8,128)} %copy.110.part_ref, ...), custom_call_target="tpu_custom_call" | custom-call | tf_op jit(solution)/shard_map/enter/pallas_call | solution.py:727
  115.6 2.1 collective-permute-start.2
  121.8 3.1 reshape_squeeze.14
  124.9 1.3 copy.115
  126.8 1.5 pad_maximum_fusion.3.moved_ref
  128.2 11.2 %project.1 = (bf16[1280,1536]{1,0:T(8,128)(2,1)}, bf16[1280,192]{1,0:T(8,128)(2,1)}, bf16[1280,192]{1,0:T(8,128)(2,1)}, bf16[1280,192]{1,0:T(8,128)(2,1)}, bf16[2,1536,192]{2,1,0:T(8,128)(2,1)}) custom-call(bf16[1024,1536]{1,0:T(8,128)(2,1)} %bitcast.141, bf16[192,1536]{1,0:T(8,128)(2,1)} %bitcast.168, f32[2,2,1,1536]{3,2,1,0:T(1,128)} %slice.189.mod_ref, ...), custom_call_target="tpu_custom_call" | custom-call | flops 2264924160 | bytes 8847360 | tf_op jit(solution)/shard_map/project/pallas_call | solution.py:94
  140.2 2.0 dynamic-slice_bitcast_fusion
  142.1 3.2 collective-permute-done.rest_1_
  145.8 18.8 %attend_forward.1 = (bf16[1280,192]{1,0:T(8,128)(2,1)}, f32[3,1280]{1,0:T(4,128)}, bf16[1024,1536]{1,0:T(8,128)(2,1)}, bf16[192,1536]{1,0:T(8,128)(2,1)}) custom-call(bf16[1280,192]{1,0:T(8,128)(2,1)} %get-tuple-element.84.q_ref, bf16[1280,192]{1,0:T(8,128)(2,1)} %get-tuple-element.85.k_ref, bf16[1280,192]{1,0:T(8,128)(2,1)} %get-tuple-element.86.v_ref, ...), custom_call_target="tpu_custom_call" | custom-call | flops 1258291200 | bytes 4915200 | tf_op jit(solution)/shard_map/attend_forward/pallas_call | solution.py:160
  164.6 1.6 broadcast_select_fusion.1
  166.2 2.4 multiply_convert_fusion.cot_ref
  168.6 6.1 collective-permute-done.1.rest_2_
  174.7 93.4 %middle.1 = (f32[128,1536]{1,0:T(8,128)}, f32[24,1536]{1,0:T(8,128)}, f32[128,1536]{1,0:T(8,128)}, f32[24,1536]{1,0:T(8,128)}, bf16[2,2,2,128,1536]{4,3,2,1,0:T(...) custom-call(bf16[2,2,2,128,1536]{4,3,2,1,0:T(8,128)(2,1)} %bitcast.1, ...), custom_call_target="tpu_custom_call" | custom-call | tf_op jit(solution)/shard_map/middle/pallas_call | solution.py:874
  268.1 4.9 fusion.16
  273.0 23.8 %feed_forward.2 = (bf16[1024,1536]{1,0:T(8,128)(2,1)}, bf16[1024,1536]{1,0:T(8,128)(2,1)}, bf16[1536,1536]{1,0:T(8,128)(2,1)}, f32[1,768]{1,0:T(1,128)}) custom-call(bf16[1024,1536]{1,0:T(8,128)(2,1)} %bitcast.191, bf16[1024,1536]{1,0:T(8,128)(2,1)} %multiply_convert_fusion.cot_ref, bf16[1536,768]{1,0:T(8,128)(2,1)} %bitcast.154, ...), custom_call_target="tpu_custom_call" | custom-call | flops 14495514624 | bytes 56623104 | tf_op jit(solution)/shard_map/feed_forward/pallas_call | solution.py:364
  298.8 3.7 fusion.cot_ref
  302.5 1.5 fusion.20
  304.0 9.9 %feed_forward.3 = (bf16[768,1536]{1,0:T(8,128)(2,1)}, bf16[768,1536]{1,0:T(8,128)(2,1)}, bf16[1536,384]{1,0:T(8,128)(2,1)}, f32[1,192]{1,0:T(1,128)}) custom-call(bf16[768,1536]{1,0:T(8,128)(2,1)} %bitcast.192, bf16[768,1536]{1,0:T(8,128)(2,1)} %fusion.cot_ref, bf16[1536,192]{1,0:T(8,128)(2,1)} %get-tuple-element.205.up_ref, ...), custom_call_target="tpu_custom_call" | custom-call | flops 2717908992 | bytes 10616832 | tf_op jit(solution)/shard_map/feed_forward/pallas_call | solution.py:364
  314.7 115.0 %turn.1 = (bf16[128,1536]{1,0:T(8,128)(2,1)}, bf16[24,1536]{1,0:T(8,128)(2,1)}, f32[128,1536]{1,0:T(8,128)}, f32[24,1536]{1,0:T(8,128)}, f32[2,16,1536]{2,1,0:T(...) custom-call(f32[24,1536]{1,0:T(8,128)} %broadcast_in_dim.22.valid_re, ...), custom_call_target="tpu_custom_call" | custom-call | tf_op jit(solution)/shard_map/turn/pallas_call | solution.py:999
  429.8 23.5 %attend_backward.1 = (bf16[1280,192]{1,0:T(8,128)(2,1)}, bf16[1280,192]{1,0:T(8,128)(2,1)}, bf16[1280,192]{1,0:T(8,128)(2,1)}, bf16[1536,384]{1,0:T(8,128)(2,1)}) custom-call(bf16[1280,192]{1,0:T(8,128)(2,1)} %get-tuple-element.84.q_ref, bf16[1280,192]{1,0:T(8,128)(2,1)} %get-tuple-element.85.k_ref, bf16[1280,192]{1,0:T(8,128)(2,1)} %get-tuple-element.86.v_ref, ...), custom_call_target="tpu_custom_call" | custom-call | flops 3145728000 | bytes 12288000 | tf_op jit(solution)/shard_map/attend_backward/pallas_call | solution.py:253
  453.5 14.1 %unproject.1 = (bf16[1024,1536]{1,0:T(8,128)(2,1)}, bf16[192,1536]{1,0:T(8,128)(2,1)}, bf16[1536,1152]{1,0:T(8,128)(2,1)}, f32[2,1,576]{2,1,0:T(1,128)}) custom-call(bf16[1280,192]{1,0:T(8,128)(2,1)} %get-tuple-element.112.dq_ref, bf16[1280,192]{1,0:T(8,128)(2,1)} %get-tuple-element.113.dk_ref, bf16[1280,192]{1,0:T(8,128)(2,1)} %get-tuple-element.114.dv_ref, ...), custom_call_target="tpu_custom_call" | custom-call | flops 4529848320 | bytes 17694720 | tf_op jit(solution)/shard_map/unproject/pallas_call | solution.py:317
  467.7 13.6 %reduce-scatter.6.cloned.1.call-done = bf16[384,384]{1,0:T(8,128)(2,1)} async-done(((bf16[1536,384]{1,0:T(8,128)(2,1)}), bf16[384,384]{1,0:T(8,128)(2,1)}) %reduce-scatter.6.cloned.1.call-update) | async-done | bytes 294928 | tf_op jit(solution)/shard_map/reduce_scatter | solution.py:1160
  481.3 1.2 copy-done.10
  482.5 4.9 reshape.267
  488.5 55.6 %leave.1 = (bf16[4,128,1536]{2,1,0:T(8,128)(2,1)}, bf16[4,24,1536]{2,1,0:T(8,128)(2,1)}, bf16[4,128,1536]{2,1,0:T(8,128)(2,1)}, bf16[4,24,1536]{2,1,0:T(8,128)(2...) custom-call(bf16[2,2,2,128,1536]{4,3,2,1,0:T(8,128)(2,1)} %bitcast.142, bf16[2,2,2,24,1536]{4,3,2,1,0:T(8,128)(2,1)} %bitcast.169, ...), custom_call_target="tpu_custom_call" | custom-call | tf_op jit(solution)/shard_map/leave/pallas_call | solution.py:1122
  547.3 5.6 share.1
  554.8 7.2 %fusion.17 = (f32[1,192,2,4,192]{4,0,1,2,3:T(1,128)}, f32[1,192,2,4,192]{4,0,1,2,3:T(1,128)S(1)}) fusion(f32[2,192,2,4,192]{4,0,1,2,3:T(2,128)} %bitcast.138), kind=kLoop, calls=%fused_computation.82 | loop fusion | bytes 4718592 | tf_op jit(solution)/shard_map/slice | solution.py:1364
  562.8 1.1 collective-permute-start.5
  564.0 3.6 copy.126
  567.6 3.4 slice.186
  571.1 2.2 copy.125
  573.2 3.3 slice.181
  582.4 2.5 convolution_bitcast_fusion
  584.9 1.3 select_convert_fusion.1
  586.7 1.1 copy-done.1
  587.8 1.6 pad_maximum_fusion.1
  590.4 1.0 constant_dynamic-slice_fusion.4
  591.4 1.2 collective-permute-start.3
  592.6 2.8 pad_maximum_fusion
  596.3 1.0 broadcast_select_fusion.5
  598.6 6.0 collective-permute-done.3
  604.6 1.3 broadcast_select_fusion.3
  606.4 1.6 maximum_convert_fusion
  608.1 3.0 copy.129
  611.1 1.1 copy.156
  613.1 1.1 copy.157
  (171 shorter events, 30.3 us)
Async XLA Ops:
  7.2 2.0 copy-start
  7.2 2.0 copy-start.25
  7.2 446.0 %reduce-scatter.4.cloned.1.call-start = ((), (), s32[]{:S(2)}) async-start(), calls=%async_computation.3 | async-start | bytes 5898240 | tf_op jit(solution)/shard_map/reduce_scatter | solution.py:1160
  7.3 1.8 copy-start.13
  9.0 1.2 copy-start.26
  11.3 1.2 copy-start.11
  11.3 1.9 copy-start.32
  11.3 1.9 copy-start.33
  115.4 2.3 copy-start.2
  115.5 3.1 copy-start.20
  115.5 3.9 copy-start.29
  115.5 4.0 copy-start.24
  115.5 4.7 copy-start.22
  115.5 29.8 %collective-permute-start = (bf16[2,384,768]{2,1,0:T(8,128)(2,1)}, bf16[2,384,768]{2,1,0:T(8,128)(2,1)}, u32[]{:S(2)}, u32[]{:S(2)}) collective-permute-start(bf16[2,384,768]{2,1,0:T(8,128)(2,1)} %bitcast.161), channel_id=1, source_target_pairs={{0,8},{8,16},{16,24},{24,0},{1,9},{9,17},{17,25},{25,1},{2,10},{10... | collective-permute-start | bytes 3538952 | tf_op jit(solution)/shard_map/ppermute | solution.py:1253
  115.6 5.3 slice-start
  115.6 49.0 %collective-permute-start.2 = (bf16[512,1536]{1,0:T(8,128)(2,1)}, bf16[512,1536]{1,0:T(8,128)(2,1)}, u32[]{:S(2)}, u32[]{:S(2)}) collective-permute-start(bf16[512,1536]{1,0:T(8,128)(2,1)} %bitcast.149), channel_id=1, source_target_pairs={{0,4},{4,0},{1,5},{5,1},{2,6},{6,2},{3,7},{7,3},{8,12},{12,8},{9,1... | collective-permute-start | bytes 4718600 | tf_op jit(solution)/shard_map/ppermute | solution.py:1277
  118.7 3.1 copy-start.7
  128.2 11.2 %copy-start.12 = (bf16[1,77,1536]{2,1,0:T(8,128)(2,1)S(1)}, bf16[1,77,1536]{2,1,0:T(8,128)(2,1)}, u32[]{:S(2)}) copy-start(bf16[1,77,1536]{2,1,0:T(8,128)(2,1)} %param.17) | copy-start | bytes 709636
  128.2 11.2 %copy-start.16 = (bf16[1,77,1536]{2,1,0:T(8,128)(2,1)S(1)}, bf16[1,77,1536]{2,1,0:T(8,128)(2,1)}, u32[]{:S(2)}) copy-start(bf16[1,77,1536]{2,1,0:T(8,128)(2,1)} %param.30) | copy-start | bytes 709636
  128.2 11.9 %copy-start.3 = (bf16[1,512,1536]{2,1,0:T(8,128)(2,1)S(1)}, bf16[1,512,1536]{2,1,0:T(8,128)(2,1)}, u32[]{:S(2)}) copy-start(bf16[1,512,1536]{2,1,0:T(8,128)(2,1)} %param.29) | copy-start | bytes 4718596
  145.3 29.4 %collective-permute-start.1 = (bf16[2,384,768]{2,1,0:T(8,128)(2,1)}, bf16[2,384,768]{2,1,0:T(8,128)(2,1)}, u32[]{:S(2)}, u32[]{:S(2)}) collective-permute-start(bf16[2,384,768]{2,1,0:T(8,128)(2,1)} %collective-permute-done.rest_1_), channel_id=1, source_target_pairs={{0,8},{8,16},{16,24},{24,0},{1,9},{9,17},{17,25},{25,1},{2,10},{10... | collective-permute-start | bytes 3538952 | tf_op jit(solution)/shard_map/ppermute | solution.py:1293
  296.8 0.7 copy-start.23
  296.8 184.5 %reduce-scatter.6.cloned.1.call-start = ((), (), s32[]{:S(2)}) async-start(), calls=%async_computation.4 | async-start | bytes 1474560 | tf_op jit(solution)/shard_map/reduce_scatter | solution.py:1160
  298.8 3.7 copy-start.4
  453.3 137.1 %reduce-scatter.8.cloned.1.call-start = ((), (), s32[]{:S(2)}) async-start(), calls=%async_computation.5 | async-start | bytes 4423680 | tf_op jit(solution)/shard_map/reduce_scatter | solution.py:1160
  481.3 1.3 copy-start.10
  482.5 5.0 copy-start.27
  482.5 5.1 copy-start.31
  482.5 5.4 copy-start.28
  544.2 10.6 %copy-start.30 = (f32[2,3]{1,0:T(2,128)S(1)}, f32[2,3]{1,0:T(2,128)}, u32[]{:S(2)}) copy-start(f32[2,3]{1,0:T(2,128)} %constant.70) | copy-start | bytes 76
  554.8 7.2 %copy-start.8 = (bf16[384,1536]{1,0:T(8,128)(2,1)S(1)}, bf16[384,1536]{1,0:T(8,128)(2,1)}, u32[]{:S(2)}) copy-start(bf16[384,1536]{1,0:T(8,128)(2,1)} %reduce-scatter.4.cloned.1.call-done) | copy-start | bytes 3538948
  554.8 9.2 %copy-start.19 = (f32[4,2,6,384]{3,2,1,0:T(8,128)S(1)}, f32[4,2,6,384]{3,2,1,0:T(8,128)}, u32[]{:S(2)}) copy-start(f32[4,2,6,384]{3,2,1,0:T(8,128)} %get-tuple-element.136) | copy-start | bytes 221188
  562.8 22.1 %collective-permute-start.5 = (bf16[192,1536]{1,0:T(8,128)(2,1)}, bf16[192,1536]{1,0:T(8,128)(2,1)}, u32[]{:S(2)}, u32[]{:S(2)}) collective-permute-start(bf16[192,1536]{1,0:T(8,128)(2,1)} %constant_dynamic-slice_fusion.1), channel_id=1, source_target_pairs={{0,4},{4,0},{1,5},{5,1},{2,6},{6,2},{3,7},{7,3},{8,12},{12,8},{9,1... | collective-permute-start | bytes 1769480 | tf_op jit(solution)/shard_map/ppermute | solution.py:1167
  564.0 3.6 copy-start.21
  573.2 5.1 copy-start.18
  573.2 5.8 copy-start.17
  573.2 7.2 %slice-start.1 = ((f32[2,6,384]{2,1,0:T(8,128)}), f32[2,2,384]{2,1,0:T(2,128)S(1)}, s32[]{:S(2)}) async-start(f32[2,6,384]{2,1,0:T(8,128)} %copy-done.21), calls=%async_computation.7 | async-start | bytes 12288 | tf_op jit(solution)/shard_map/slice | solution.py:1414
  582.4 2.5 copy-start.9
  586.5 1.3 copy-start.1
  587.8 1.6 copy-start.14
  589.4 6.9 %collective-permute-start.4 = (bf16[192,384]{1,0:T(8,128)(2,1)S(1)}, bf16[192,384]{1,0:T(8,128)(2,1)}, u32[]{:S(2)}, u32[]{:S(2)}) collective-permute-start(bf16[192,384]{1,0:T(8,128)(2,1)S(1)} %constant_dynamic-slice_fusion.3), channel_id=1, source_target_pairs={{0,4},{4,0},{1,5},{5,1},{2,6},{6,2},{3,7},{7,3},{8,12},{12,8},{9,1... | collective-permute-start | bytes 442376 | tf_op jit(solution)/shard_map/ppermute | solution.py:1167
  591.4 4.9 copy-start.15
  591.4 13.2 %collective-permute-start.3 = (bf16[192,1152]{1,0:T(8,128)(2,1)S(1)}, bf16[192,1152]{1,0:T(8,128)(2,1)}, u32[]{:S(2)}, u32[]{:S(2)}) collective-permute-start(bf16[192,1152]{1,0:T(8,128)(2,1)S(1)} %constant_dynamic-slice_fusion.4), channel_id=1, source_target_pairs={{0,4},{4,0},{1,5},{5,1},{2,6},{6,2},{3,7},{7,3},{8,12},{12,8},{9,1... | collective-permute-start | bytes 1327112 | tf_op jit(solution)/shard_map/ppermute | solution.py:1167
  608.1 3.0 copy-start.6
  611.1 2.0 copy-start.5
Sparse Core Ops, SparseCore 0:
  296.9 91.9 reduce-scatter.3
  453.4 27.8 reduce-scatter.5
  483.6 68.9 reduce-scatter.7

commit v4 on v3

--- a/solution.py
+++ b/solution.py
@@ -178,6 +178,40 @@
     )(q, k, v, weight)
 
 
+def out_gradient_kernel(steps, image_ref, text_ref, o_ref, dw_ref, dw_sum):
+    step = pl.program_id(0)
+    wide = o_ref.shape[1]
+
+    @pl.when(step == 0)
+    def _():
+        dw_sum[...] = jnp.zeros_like(dw_sum)
+
+    def add(arriving, stream):
+        dw_sum[stream] += dot(arriving, o_ref[...], ((0,), (0,)))
+
+    by_stream(steps, image_ref, text_ref, add)
+
+    @pl.when(step == steps)
+    def _():
+        for stream in range(2):
+            dw_ref[:, stream * wide : (stream + 1) * wide] = dw_sum[stream].astype(BF16)
+
+
+def out_gradient(image, text, blended):
+    rows, wide = blended.shape
+    width = image.shape[1]
+    steps = rows // QUERY_BLOCK - 1
+    return local_call(
+        functools.partial(out_gradient_kernel, steps),
+        steps + 1,
+        [image_block((QUERY_BLOCK, width), steps - 1), fixed(text.shape), stepped((QUERY_BLOCK, wide))],
+        [(pl.BlockSpec((width, 2 * wide), lambda i: (0, 0)), jax.ShapeDtypeStruct((width, 2 * wide), BF16))],
+        [pltpu.VMEM((2, width, wide), F32)],
+        2 * rows * width * wide,
+        "out_gradient",
+    )(image, text, blended)[0]
+
+
 def attend_backward_kernel(
     steps,
     heads,
@@ -185,7 +219,6 @@
     q_ref,
     k_ref,
     v_ref,
-    o_ref,
     lse_ref,
     image_ref,
     text_ref,
@@ -193,26 +226,21 @@
     dq_ref,
     dk_ref,
     dv_ref,
-    dw_ref,
     kt_ref,
     g_ref,
     dk_sum,
     dv_sum,
-    dw_sum,
 ):
     step = pl.program_id(0)
-    wide = q_ref.shape[1]
 
     @pl.when(step == 0)
     def _():
         kt_ref[...] = k_ref[...].T
         dk_sum[...] = jnp.zeros_like(dk_sum)
         dv_sum[...] = jnp.zeros_like(dv_sum)
-        dw_sum[...] = jnp.zeros_like(dw_sum)
 
     def bring(arriving, stream):
         g_ref[...] = dot(arriving, weight_ref[0]).astype(BF16)
-        dw_sum[stream] += dot(arriving, o_ref[...], ((0,), (0,)))
 
     by_stream(steps, image_ref, text_ref, bring)
     rows = k_ref.shape[0]
@@ -239,11 +267,9 @@
     def _():
         dk_ref[...] = jnp.concatenate([dk_sum[head] for head in range(heads)], 1).astype(BF16)
         dv_ref[...] = jnp.concatenate([dv_sum[head] for head in range(heads)], 1).astype(BF16)
-        for stream in range(2):
-            dw_ref[:, stream * wide : (stream + 1) * wide] = dw_sum[stream].astype(BF16)
-
-
-def attend_backward(q, k, v, blended, lse, image, text, weight, text_rows):
+
+
+def attend_backward(q, k, v, lse, image, text, weight, text_rows):
     rows, wide = q.shape
     width = weight.shape[1]
     heads = wide // HEAD_DIM
@@ -257,7 +283,6 @@
             block,
             fixed((rows, wide)),
             fixed((rows, wide)),
-            block,
             pl.BlockSpec((heads, QUERY_BLOCK), lambda i: (0, i)),
             image_block((QUERY_BLOCK, width), steps - 1),
             fixed(text.shape),
@@ -267,18 +292,16 @@
             (block, jax.ShapeDtypeStruct((rows, wide), BF16)),
             (whole, jax.ShapeDtypeStruct((rows, wide), BF16)),
             (whole, jax.ShapeDtypeStruct((rows, wide), BF16)),
-            (pl.BlockSpec((width, 2 * wide), lambda i: (0, 0)), jax.ShapeDtypeStruct((width, 2 * wide), BF16)),
         ],
         [
             pltpu.VMEM((wide, rows), BF16),
             pltpu.VMEM((QUERY_BLOCK, wide), BF16),
             pltpu.VMEM((heads, rows, HEAD_DIM), F32),
             pltpu.VMEM((heads, rows, HEAD_DIM), F32),
-            pltpu.VMEM((2, width, wide), F32),
         ],
         10 * rows * rows * wide,
         "attend_backward",
-    )(q, k, v, blended, lse, image, text, weight)
+    )(q, k, v, lse, image, text, weight)
 
 
 def unproject_kernel(
@@ -317,7 +340,13 @@
     return local_call(
         functools.partial(unproject_kernel, steps),
         steps + 1,
-        [block, block, block, stepped((QUERY_BLOCK, width)), stream_block((1,) + weight.shape[1:], steps)],
+        [
+            block,
+            block,
+            block,
+            stepped((QUERY_BLOCK, width)),
+            stream_block((1,) + weight.shape[1:], steps),
+        ],
         [
             (image_block((QUERY_BLOCK, width), steps - 1), jax.ShapeDtypeStruct((steps * QUERY_BLOCK, width), BF16)),
             (pl.BlockSpec((text_all, width), lambda i: (0, 0)), jax.ShapeDtypeStruct((text_all, width), BF16)),
@@ -330,7 +359,24 @@
     )(dq, dk, dv, normed, weight)
 
 
-def feed_kernel(second_ref, cot_ref, up_ref, down_ref, bias_ref, feed_ref, pull_ref, dw_ref, sums_ref, up_sum, down_sum):
+def feed_kernel(
+    halves,
+    ctx_ref,
+    second_ref,
+    cot_ref,
+    other_ref,
+    gate_ref,
+    up_ref,
+    down_ref,
+    bias_ref,
+    feed_ref,
+    pull_ref,
+    dw_ref,
+    sums_ref,
+    up_sum,
+    down_sum,
+    gate_rows,
+):
     step = pl.program_id(0)
     wide = up_ref.shape[1]
 
@@ -339,8 +385,20 @@
         up_sum[...] = jnp.zeros_like(up_sum)
         down_sum[...] = jnp.zeros_like(down_sum)
         sums_ref[...] = jnp.zeros_like(sums_ref)
-
-    second, arriving = second_ref[...], cot_ref[...]
+        groups = gate_ref.shape[0]
+        if halves:
+            gate_rows[...] = gate_ref[...]
+        else:
+            rows = gate_rows.shape[0] // (2 * groups)
+            for block in range(2 * groups):
+                gate = gate_ref[block % groups : block % groups + 1]
+                gate_rows[block * rows : (block + 1) * rows] = jnp.broadcast_to(gate, (rows, gate.shape[1]))
+
+    arriving = cot_ref[...]
+    if halves:
+        arriving = jnp.where(step // halves == ctx_ref[0], arriving, other_ref[...])
+    arriving = (arriving.astype(F32) * gate_rows[...]).astype(BF16)
+    second = second_ref[...]
     hidden = dot(second, up_ref[...]) + bias_ref[...]
     gelu_out, slope = gelu_parts(hidden)
     gelu_low = gelu_out.astype(BF16)
@@ -357,24 +415,132 @@
         dw_ref[:, wide:] = down_sum[...].astype(BF16)
 
 
-def feed_forward(second, arriving, up, down, bias):
-    (rows, width), wide = second.shape, up.shape[1]
-    block_rows = QUERY_BLOCK if rows % QUERY_BLOCK == 0 else rows
-    block = stepped((block_rows, width))
-    return local_call(
-        feed_kernel,
-        rows // block_rows,
-        [block, block, fixed(up.shape), fixed(down.shape), fixed((1, wide))],
-        [
-            (block, jax.ShapeDtypeStruct((rows, width), BF16)),
-            (block, jax.ShapeDtypeStruct((rows, width), BF16)),
-            (pl.BlockSpec((width, 2 * wide), lambda i: (0, 0)), jax.ShapeDtypeStruct((width, 2 * wide), BF16)),
-            (pl.BlockSpec((1, wide), lambda i: (0, 0)), jax.ShapeDtypeStruct((1, wide), F32)),
+def feed_forward(ctx, second, cot, other, gate, up, down, bias):
+    (up, up_at), (down, down_at) = up, down
+    (rows, width), wide, groups = second.shape, up.shape[2], gate.shape[0]
+    if other is None:
+        block_rows, halves, gate_rows = 2 * TEXT_SLOTS // 4 * groups, 0, 2 * TEXT_SLOTS // 4 * groups
+        other, last = cot[:8], 0
+        cot_spec = pl.BlockSpec((block_rows, width), lambda i, c: (i, 0))
+        other_spec = pl.BlockSpec((8, width), lambda i, c: (0, 0))
+    else:
+        block_rows = min(QUERY_BLOCK, cot.shape[0])
+        halves, gate_rows = cot.shape[0] // block_rows, 1
+        last = halves - 1
+        cot_spec = pl.BlockSpec((block_rows, width), lambda i, c: (jnp.clip(i - c[0] * halves, 0, last), 0))
+        other_spec = pl.BlockSpec((block_rows, width), lambda i, c: (jnp.clip(i - (1 - c[0]) * halves, 0, last), 0))
+    block = pl.BlockSpec((block_rows, width), lambda i, c: (i, 0))
+
+    def once(shape):
+        return pl.BlockSpec(shape, lambda i, c: (0, 0), pipeline_mode=pl.Buffered(1))
+
+    flops = 12 * rows * width * wide
+    return pl.pallas_call(
+        functools.partial(feed_kernel, halves),
+        grid_spec=pltpu.PrefetchScalarGridSpec(
+            num_scalar_prefetch=1,
+            grid=(rows // block_rows,),
+            in_specs=[
+                block,
+                cot_spec,
+                other_spec,
+                once(gate.shape),
+                pl.BlockSpec(
+                    (None,) + up.shape[1:], lambda i, c: (up_at, 0, 0), pipeline_mode=pl.Buffered(1)
+                ),
+                pl.BlockSpec(
+                    (None,) + down.shape[1:], lambda i, c: (down_at, 0, 0), pipeline_mode=pl.Buffered(1)
+                ),
+                once((1, wide)),
+            ],
+            out_specs=[
+                block,
+                block,
+                pl.BlockSpec((width, 2 * wide), lambda i, c: (0, 0)),
+                pl.BlockSpec((1, wide), lambda i, c: (0, 0)),
+            ],
+            scratch_shapes=[pltpu.VMEM((width, wide), F32)] * 2 + [pltpu.VMEM((gate_rows, width), F32)],
+        ),
+        out_shape=[
+            jax.ShapeDtypeStruct((rows, width), BF16),
+            jax.ShapeDtypeStruct((rows, width), BF16),
+            jax.ShapeDtypeStruct((width, 2 * wide), BF16),
+            jax.ShapeDtypeStruct((1, wide), F32),
         ],
-        [pltpu.VMEM((width, wide), F32)] * 2,
-        12 * rows * width * wide,
-        "feed_forward",
-    )(second, arriving, up, down, bias.reshape(1, wide))
+        compiler_params=pltpu.CompilerParams(vmem_limit_bytes=VMEM_LIMIT),
+        cost_estimate=pl.CostEstimate(flops=flops, bytes_accessed=flops // 256, transcendentals=0),
+        name="feed_forward",
+    )(ctx, second, cot, other, gate, up, down, bias.reshape(1, wide))
+
+
+def place_feed_kernel(ctx_ref, mine_ref, other_ref, moved_ref, up_ref, down_ref):
+    ctx = ctx_ref[0]
+    cols = mine_ref.shape[2] // 2
+    text_cols = moved_ref.shape[2] // 2
+    groups = moved_ref.shape[0] // 2
+
+    def place(span):
+        kept, other = mine_ref[ctx, span], other_ref[span]
+        for c in range(2):
+            part = jnp.where(ctx == c, kept, other).astype(F32)
+            up_ref[0, span, c * cols : (c + 1) * cols] = part[:, :cols]
+            down_ref[0, span, c * cols : (c + 1) * cols] = part[:, cols:]
+            for group in range(groups):
+                start = c * cols + group * text_cols
+                text = moved_ref[group * 2 + c, span].astype(F32)
+                up_ref[1, span, start : start + text_cols] = text[:, :text_cols]
+                down_ref[1, span, start : start + text_cols] = text[:, text_cols:]
+
+    over_rows(other_ref.shape[0], place)
+
+
+def place_feed(ctx, mine, other, moved):
+    rows, cols = other.shape
+    shape = jax.ShapeDtypeStruct((2, rows, cols), F32)
+    return pl.pallas_call(
+        place_feed_kernel,
+        in_specs=[pl.BlockSpec(memory_space=pltpu.SMEM)] + [pl.BlockSpec(memory_space=pltpu.VMEM)] * 3,
+        out_specs=[pl.BlockSpec(memory_space=pltpu.VMEM)] * 2,
+        out_shape=[shape, shape],
+        compiler_params=pltpu.CompilerParams(vmem_limit_bytes=VMEM_LIMIT),
+        name="place_feed",
+    )(ctx, mine.reshape(2, rows, cols), other, moved)
+
+
+def place_heads_kernel(kinds, ctx_ref, mine_ref, other_ref, out_ref):
+    ctx = ctx_ref[0]
+    half = out_ref.shape[3] // 2
+
+    def place(span):
+        kept, other = mine_ref[ctx, span], other_ref[span]
+        for c in range(2):
+            part = jnp.where(ctx == c, kept, other).astype(F32)
+            for s in range(2):
+                for j in range(kinds):
+                    start = (kinds * s + j) * half
+                    out_ref[s, j, span, c * half : (c + 1) * half] = part[:, start : start + half]
+
+    over_rows(other_ref.shape[0], place)
+
+
+def place_heads(kinds, ctx, mine, other):
+    rows, cols = other.shape
+    return pl.pallas_call(
+        functools.partial(place_heads_kernel, kinds),
+        in_specs=[pl.BlockSpec(memory_space=pltpu.SMEM)] + [pl.BlockSpec(memory_space=pltpu.VMEM)] * 2,
+        out_specs=pl.BlockSpec(memory_space=pltpu.VMEM),
+        out_shape=jax.ShapeDtypeStruct((2, kinds, rows, cols // kinds), F32),
+        compiler_params=pltpu.CompilerParams(vmem_limit_bytes=VMEM_LIMIT),
+        name="place_heads",
+    )(ctx, mine.reshape(2, rows, cols), other)
+
+
+def place_qkv(ctx, mine, other):
+    return place_heads(3, ctx, mine, other).transpose(0, 2, 1, 3)
+
+
+def place_out(ctx, mine, other):
+    return place_heads(1, ctx, mine, other)[:, 0]
 
 
 def normalise(inputs):
@@ -457,74 +623,84 @@
     lax.fori_loop(0, rows // step, one, 0)
 
 
+def reduce_first(wires, s):
+    return wires.copy(s["part"].at[:, :, 1 - wires.k], s["core"], wires.k_next)
+
+
+def reduce_add(wires, s, arrived):
+    k = wires.k
+    part, core, held = s["part"], s["core"], s["held"]
+    arrived.wait_recv()
+    for i in range(2):
+        for j in range(2):
+
+            def add(span, i=i, j=j):
+                held[i, j, span] = (part[i, j, k, span].astype(F32) + core[i, j, span].astype(F32)).astype(BF16)
+
+            over_rows(part.shape[3], add)
+
+
+def reduce_second(wires, s):
+    held = s["held"]
+    cut = held.shape[3] // 2
+    return (
+        wires.copy(held.at[:, 1 - wires.y, :, pl.ds(0, cut)], s["along_y"], wires.y_next),
+        wires.copy(held.at[1 - wires.x, :, :, pl.ds(cut, cut)], s["along_x"], wires.x_next),
+    )
+
+
+def reduce_third(wires, s, second):
+    x, y = wires.x, wires.y
+    held, along_y, along_x, out_x, out_y = s["held"], s["along_y"], s["along_x"], s["out_x"], s["out_y"]
+    cut = held.shape[3] // 2
+    for arrived in second:
+        arrived.wait_recv()
+
+    def add(span):
+        out_x[span] = (held[1 - x, y, span, :cut].astype(F32) + along_y[1 - x, span].astype(F32)).astype(BF16)
+        out_y[span] = (held[x, 1 - y, span, cut:].astype(F32) + along_x[1 - y, span].astype(F32)).astype(BF16)
+
+    over_rows(held.shape[2], add)
+    return (
+        wires.copy(out_x, s["last_x"], wires.x_next),
+        wires.copy(out_y, s["last_y"], wires.y_next),
+    )
+
+
+def reduce_last(wires, s, third):
+    x, y = wires.x, wires.y
+    held, along_y, along_x, last_x, last_y, total = (
+        s["held"],
+        s["along_y"],
+        s["along_x"],
+        s["last_x"],
+        s["last_y"],
+        s["total"],
+    )
+    cut = held.shape[3] // 2
+    for arrived in third:
+        arrived.wait_recv()
+
+    def add(span):
+        total[span, :cut] = (
+            held[x, y, span, :cut].astype(F32) + along_y[x, span].astype(F32) + last_x[span].astype(F32)
+        )
+        total[span, cut:] = (
+            held[x, y, span, cut:].astype(F32) + along_x[y, span].astype(F32) + last_y[span].astype(F32)
+        )
+
+    over_rows(held.shape[2], add)
+
+
 def reduce_plane(wires, streams):
-    x, y, k = wires.x, wires.y, wires.k
-    first = [wires.copy(s["part"].at[:, :, 1 - k], s["core"], wires.k_next) for s in streams]
+    first = [reduce_first(wires, s) for s in streams]
     second = []
     for s, arrived in zip(streams, first):
-        part, core, held = s["part"], s["core"], s["held"]
-        rows, width = part.shape[3], part.shape[4]
-        cut = width // 2
-        arrived.wait_recv()
-        for i in range(2):
-            for j in range(2):
-
-                def add(span, i=i, j=j):
-                    held[i, j, span] = (part[i, j, k, span].astype(F32) + core[i, j, span].astype(F32)).astype(BF16)
-
-                over_rows(rows, add)
-        second.append(
-            (
-                wires.copy(held.at[:, 1 - y, :, pl.ds(0, cut)], s["along_y"], wires.y_next),
-                wires.copy(held.at[1 - x, :, :, pl.ds(cut, cut)], s["along_x"], wires.x_next),
-            )
-        )
-    third = []
-    for s, (from_y, from_x) in zip(streams, second):
-        held, along_y, along_x, out_x, out_y = s["held"], s["along_y"], s["along_x"], s["out_x"], s["out_y"]
-        rows, width = held.shape[2], held.shape[3]
-        cut = width // 2
-        from_y.wait_recv()
-        from_x.wait_recv()
-
-        def add(span):
-            out_x[span] = (
-                held[1 - x, y, span, :cut].astype(F32) + along_y[1 - x, span].astype(F32)
-            ).astype(BF16)
-            out_y[span] = (
-                held[x, 1 - y, span, cut:].astype(F32) + along_x[1 - y, span].astype(F32)
-            ).astype(BF16)
-
-        over_rows(rows, add)
-        third.append(
-            (
-                wires.copy(out_x, s["last_x"], wires.x_next),
-                wires.copy(out_y, s["last_y"], wires.y_next),
-            )
-        )
-    for s, (from_x, from_y) in zip(streams, third):
-        held, along_y, along_x, last_x, last_y, total = (
-            s["held"],
-            s["along_y"],
-            s["along_x"],
-            s["last_x"],
-            s["last_y"],
-            s["total"],
-        )
-        rows, width = held.shape[2], held.shape[3]
-        cut = width // 2
-        from_x.wait_recv()
-        from_y.wait_recv()
-
-        def add(span):
-            total[span, :cut] = (
-                held[x, y, span, :cut].astype(F32) + along_y[x, span].astype(F32) + last_x[span].astype(F32)
-            )
-            total[span, cut:] = (
-                held[x, y, span, cut:].astype(F32) + along_x[y, span].astype(F32) + last_y[span].astype(F32)
-            )
-
-        over_rows(rows, add)
+        reduce_add(wires, s, arrived)
+        second.append(reduce_second(wires, s))
+    third = [reduce_third(wires, s, arrived) for s, arrived in zip(streams, second)]
+    for s, arrived in zip(streams, third):
+        reduce_last(wires, s, arrived)
 
 
 REDUCE_KEYS = ("core", "held", "along_y", "along_x", "out_x", "out_y", "last_x", "last_y", "total")
@@ -614,6 +790,7 @@
     gates_out,
     attn_out,
     ffn_out,
+    moved_out,
     mod_in,
     send_sems,
     recv_sems,
@@ -635,6 +812,7 @@
     rows_out[me] = rows_ref[...]
     for arrived in sums:
         arrived.wait_recv()
+    ring = {(s, 0): wires.copy(attn_ref.at[x, s], attn_out.at[s, dp, x], z_next) for s in range(2)}
     total = bias_ref[...]
     for source in range(count):
         total = total + mod_in[source]
@@ -650,8 +828,6 @@
         ]
         for lane in range(4):
             gates_out[dp, lane] = mod_ref[lane, 11]
-
-    ring = {(s, 0): wires.copy(attn_ref.at[x, s], attn_out.at[s, dp, x], z_next) for s in range(2)}
 
     def pass_on(turn, side):
         for s in range(2):
@@ -697,6 +873,12 @@
             for s in range(wide):
                 first, last = weight[s, span, :cols], weight[s, span, cols:]
                 ffn_out[i * wide + s, x, span] = jnp.where(x == 0, first, last)
+            if groups > 1:
+                text_cols = cols // groups
+                for peer in range(count):
+                    start = (peer % 2) * cols + (peer // 2) * text_cols
+                    text = weight[1, span, start : start + text_cols]
+                    moved_out[peer, span, i * text_cols : (i + 1) * text_cols] = text
 
     over_rows(image_ref.shape[1], keep_tokens)
     over_rows(attn_ref.shape[2], keep_weights)
@@ -734,13 +916,14 @@
             jax.ShapeDtypeStruct((groups, 4, slice_width), F32),
             jax.ShapeDtypeStruct((2, n_dp, 2) + attn.shape[2:], BF16),
             jax.ShapeDtypeStruct((2 * wide, 2, rows, cols), BF16),
+            jax.ShapeDtypeStruct((2 * groups, rows, 2 * cols // groups) if groups > 1 else (1, 8, 128), BF16),
         ],
         [pltpu.VMEM((count, kinds, slice_width), F32)],
         2 * (count - 1) + 2 + 4 * n_dp + 16 + groups + 5,
         0,
         "enter",
         [VMEM_SPEC] * 8,
-        [VMEM_SPEC] * 7,
+        [VMEM_SPEC] * 8,
     )(partial_mod, ada_bias, bias_rows, image, text, attn, up, down)
 
 
@@ -825,20 +1008,23 @@
             for i in range(block.shape[0]):
                 ffn_out[i, lax.rem(dp + n_dp - turn, n_dp), span] = block[i, span]
 
-    reduce_plane(wires, streams)
+    image, text = streams
+    first = reduce_first(wires, text), reduce_first(wires, image)
+    reduce_add(wires, text, first[0])
+    text_second = reduce_second(wires, text)
+    reduce_add(wires, image, first[1])
+    image_second = reduce_second(wires, image)
     for arrived in cots:
         arrived.wait_recv()
-    gathers, started = [image_all, text_all], []
     if groups > 1:
-        gathers, started = [cots_all] + gathers, [spread_first(wires, cots_all)]
-    zs = []
-    for i, tokens, attention, middle, gathered in (
-        (1, text_x, text_attention, text_middle, text_all.at[:, :, :, dp if groups > 1 else 0]),
-        (0, image_x, image_attention, image_middle, image_all),
-    ):
+        cots_first = spread_first(wires, cots_all)
+    text_third = reduce_third(wires, text, text_second)
+    image_third = reduce_third(wires, image, image_second)
+
+    def second_rows(i, tokens, attention, middle, gathered):
         total = streams[i]["total"]
 
-        def finish(span, i=i, tokens=tokens, attention=attention, middle=middle, gathered=gathered, total=total):
+        def finish(span):
             branch = total[span] + bias_ref[i]
             attention[span] = branch
             value = tokens[span].astype(F32) + mod_ref[i, 2] * branch
@@ -847,15 +1033,29 @@
             gathered[x, y, k, span] = (norm * (1.0 + mod_ref[i, 4]) + mod_ref[i, 3]).astype(BF16)
 
         over_rows(total.shape[0], finish)
-        if i == 1:
-            for offset in range(1, groups):
-                block = text_all.at[x, y, k, dp]
-                zs.append(wires.copy(block, block, (lax.rem(dp + offset, groups), x, tp)))
+
+    reduce_last(wires, text, text_third)
+    second_rows(1, text_x, text_attention, text_middle, text_all.at[:, :, :, dp if groups > 1 else 0])
+    zs = []
+    for offset in range(1, groups):
+        block = text_all.at[x, y, k, dp]
+        zs.append(wires.copy(block, block, (lax.rem(dp + offset, groups), x, tp)))
+    if groups > 1:
+        cots_second = spread_second(wires, cots_all, cots_first)
+    reduce_last(wires, image, image_third)
+    second_rows(0, image_x, image_attention, image_middle, image_all)
+    image_first = spread_first(wires, image_all)
     for arrived in zs:
         arrived.wait_recv()
+    text_first = spread_first(wires, text_all)
     moves = start_moves(wires, groups, moved_ref, moved_out, local_sem)
+    thirds = [spread_third(wires, cots_all, cots_second)] if groups > 1 else []
     over_rows(ffn_out.shape[2], keep)
-    spread_plane(wires, gathers, started)
+    image_next = spread_second(wires, image_all, image_first)
+    text_next = spread_second(wires, text_all, text_first)
+    thirds += [spread_third(wires, image_all, image_next), spread_third(wires, text_all, text_next)]
+    for arrived in thirds:
+        arrived.wait_recv()
     end_moves(moves)
     last.wait_recv()
     wires.finish()
@@ -918,68 +1118,105 @@
         dict(zip(("part",) + REDUCE_KEYS, (part,) + scratch[i * size : (i + 1) * size]))
         for i, part in enumerate((text_second, text_feed, image_second, image_feed))
     ]
-    reduce_plane(wires, streams)
-    streams = [streams[2], streams[0], streams[3], streams[1]]
-    zs = []
+    pulls, feeds = (streams[2], streams[0]), (streams[3], streams[1])
+    order = [pulls[1], pulls[0], feeds[1], feeds[0]]
     rows = text_middle.shape[0]
-    if groups > 1:
-        for i in range(2):
-            total = streams[1 + 2 * i]["total"]
+
+    def to_planes(i, total):
+        copies = []
+        if groups > 1:
             for group in range(groups):
                 z_out[i, group] = total[group * rows : (group + 1) * rows].astype(BF16)
             z_in[i, dp] = z_out[i, dp]
             for offset in range(1, groups):
                 plane = lax.rem(dp + offset, groups)
-                zs.append(wires.copy(z_out.at[i, plane], z_in.at[i, dp], (plane, x, tp)))
+                copies.append(wires.copy(z_out.at[i, plane], z_in.at[i, dp], (plane, x, tp)))
+        return copies
+
+    def from_planes(i, total, copies):
+        for arrived in copies:
+            arrived.wait_recv()
+        if groups > 1:
+            summed = z_in[i, 0].astype(F32)
+            for group in range(1, groups):
+                summed = summed + z_in[i, group].astype(F32)
+            total[0:rows] = summed
+
     sums_ref[...] = jnp.zeros_like(sums_ref)
     sides = (
         (image_attention, image_middle, image_cot, image_out, image_grad, image_all),
         (text_attention, text_middle, text_cot, text_out, text_grad, text_all),
     )
-    for i, (attention, middle, cot, out, grad, gathered) in enumerate(sides):
-        second, feed = streams[i]["total"], streams[2 + i]["total"]
-        if i == 1 and groups > 1:
-            for arrived in zs:
-                arrived.wait_recv()
-            for j, total in enumerate((second, feed)):
-                summed = z_in[j, 0].astype(F32)
-                for group in range(1, groups):
-                    summed = summed + z_in[j, group].astype(F32)
-                total[0:rows] = summed
-
-        def finish(span, i=i, attention=attention, middle=middle, cot=cot, out=out, grad=grad, gathered=gathered, second=second, feed=feed):
-            branch, value, arriving, pulled = attention[span], middle[span], cot[span].astype(F32), second[span]
-            fed = feed[span] + bias_ref[i]
-            gated_branch = mod_ref[i, 2] * branch
-            gated_feed = mod_ref[i, 5] * fed
-            result = value + gated_feed
-            out[span] = result.astype(BF16)
+
+    def add_sums(i, start, terms):
+        for t, term in enumerate(terms):
+            sums_ref[i, start + t : start + t + 1] += jnp.sum(term, axis=0, keepdims=True)
+
+    def pull_side(i):
+        attention, middle, cot, _, grad, gathered = sides[i]
+        total = pulls[i]["total"]
+
+        def finish(span):
+            branch, value, arriving, pulled = attention[span], middle[span], cot[span].astype(F32), total[span]
             norm, spread = normalise(value)
             grad_middle = arriving + normalise_back(pulled * (1.0 + mod_ref[i, 4]), norm, spread)
             grad[span] = grad_middle
             low = (grad_middle * mod_ref[i, 2]).astype(BF16)
             gathered[x, y, k, span] = low
+            add_sums(i, 0, (grad_middle * branch, pulled, pulled * norm))
+            add_sums(i, 5, (low.astype(F32),))
+
+        over_rows(middle.shape[0], finish)
+
+    def feed_side(i):
+        attention, middle, cot, out, _, _ = sides[i]
+        total = feeds[i]["total"]
+
+        def finish(span):
+            branch, value, arriving = attention[span], middle[span], cot[span].astype(F32)
+            fed = total[span] + bias_ref[i]
+            gated_branch = mod_ref[i, 2] * branch
+            gated_feed = mod_ref[i, 5] * fed
+            result = value + gated_feed
+            out[span] = result.astype(BF16)
             if i == 1:
                 kept = valid_ref[span]
                 result, gated_branch, gated_feed = result * kept, gated_branch * kept, gated_feed * kept
             own_feed = (arriving * mod_ref[i, 5]).astype(BF16).astype(F32)
-            terms = (
-                grad_middle * branch,
-                pulled,
-                pulled * norm,
-                arriving * fed,
-                own_feed,
-                low.astype(F32),
-                result * result,
-                gated_branch * gated_branch,
-                gated_feed * gated_feed,
-            )
-            for t, term in enumerate(terms):
-                sums_ref[i, t : t + 1] += jnp.sum(term, axis=0, keepdims=True)
+            add_sums(i, 3, (arriving * fed, own_feed))
+            add_sums(i, 6, (result * result, gated_branch * gated_branch, gated_feed * gated_feed))
 
         over_rows(middle.shape[0], finish)
+
+    first = [reduce_first(wires, s) for s in order]
+    pull_second = []
+    for s, arrived in zip(order[:2], first[:2]):
+        reduce_add(wires, s, arrived)
+        pull_second.append(reduce_second(wires, s))
+    for s, arrived in zip(order[2:], first[2:]):
+        reduce_add(wires, s, arrived)
+    pull_third = [reduce_third(wires, s, arrived) for s, arrived in zip(order[:2], pull_second)]
+    feed_second = [reduce_second(wires, s) for s in order[2:]]
+    reduce_last(wires, pulls[1], pull_third[0])
+    planes = to_planes(0, pulls[1]["total"])
+    reduce_last(wires, pulls[0], pull_third[1])
+    pull_side(0)
+    spread_one = [spread_first(wires, image_all)]
+    from_planes(0, pulls[1]["total"], planes)
+    pull_side(1)
+    spread_one.append(spread_first(wires, text_all))
+    feed_third = [reduce_third(wires, s, arrived) for s, arrived in zip(order[2:], feed_second)]
+    spread_two = [spread_second(wires, block, arrived) for block, arrived in zip((image_all, text_all), spread_one)]
+    reduce_last(wires, feeds[1], feed_third[0])
+    planes = to_planes(1, feeds[1]["total"])
     moves = start_moves(wires, groups, moved_ref, moved_out, local_sem)
-    spread_plane(wires, [image_all, text_all])
+    reduce_last(wires, feeds[0], feed_third[1])
+    spread_three = [spread_third(wires, block, arrived) for block, arrived in zip((image_all, text_all), spread_two)]
+    feed_side(0)
+    from_planes(1, feeds[1]["total"], planes)
+    feed_side(1)
+    for arrived in spread_three:
+        arrived.wait_recv()
     end_moves(moves)
     wires.finish()
 
@@ -1024,12 +1261,16 @@
     sums_ref,
     mod_ref,
     halves_ref,
+    ffn_mine,
+    out_mine,
     image_outs,
     text_outs,
     image_grads,
     text_grads,
     packed_out,
     halves_out,
+    ffn_other,
+    out_other,
     *scratch,
 ):
     send_sems, recv_sems = scratch[-2:]
@@ -1051,6 +1292,12 @@
         for i, part in enumerate((image_part, text_part))
     ]
     reduce_plane(wires, streams)
+    given = ffn_other.shape[0]
+    given = pl.ds(pl.multiple_of((1 - x) * given, given), given)
+    swaps = [
+        wires.copy(mine.at[given], other, wires.x_next)
+        for mine, other in ((ffn_mine, ffn_other), (out_mine, out_other))
+    ]
     local_sums[...] = jnp.zeros_like(local_sums)
     for i, (tokens, grad, all_grads) in enumerate(
         ((image_x, image_grad, image_grads), (text_x, text_grad, text_grads))
@@ -1095,12 +1342,12 @@
     for final, arrived in zip(finals, along_y):
         arrived.wait_recv()
         across.append(wires.copy(final.at[far], final.at[far], wires.k_next))
-    for arrived in across:
+    for arrived in across + swaps:
         arrived.wait_recv()
     wires.finish()
 
 
-def leave_step(n_dp, parts, tokens, grads, outs_own, sums, mod, halves):
+def leave_step(n_dp, parts, tokens, grads, outs_own, sums, mod, halves, ffn_mine, out_mine):
     width = tokens[0].shape[1]
     rows = [part.shape[0] for part in tokens]
     wide = width // 4
@@ -1109,6 +1356,7 @@
         jax.ShapeDtypeStruct((n_dp, PACKED, wide), F32),
         jax.ShapeDtypeStruct((n_dp, 2) + halves.shape, F32),
     ]
+    outs += [jax.ShapeDtypeStruct((mine.shape[0] // 2, mine.shape[1]), BF16) for mine in (ffn_mine, out_mine)]
     scratch = []
     for r in rows:
         scratch += reduce_scratch(r, width)
@@ -1123,12 +1371,12 @@
         functools.partial(leave_kernel, n_dp),
         outs,
         scratch,
-        1 + 10 + 7 + 8 + 2 * (n_dp - 1) + 4,
+        1 + 10 + 7 + 8 + 2 * (n_dp - 1) + 6,
         3,
         "leave",
-        [VMEM_SPEC] * 11,
-        [VMEM_SPEC] * 6,
-    )(*parts, *tokens, *grads, *outs_own, sums, mod, halves)
+        [VMEM_SPEC] * 11 + [ANY_SPEC] * 2,
+        [VMEM_SPEC] * 6 + [ANY_SPEC] * 2,
+    )(*parts, *tokens, *grads, *outs_own, sums, mod, halves, ffn_mine, out_mine)
 
 
 def share_kernel(part_ref, out_ref, send_sems, recv_sems):
@@ -1158,20 +1406,6 @@
 
 def scatter_rows(grad):
     return lax.psum_scatter(grad, "dp", scatter_dimension=0, tiled=True)
-
-
-def swap_halves(mine, ctx):
-    rows = mine.shape[0] // 2
-    kept = lax.dynamic_slice_in_dim(mine, ctx * rows, rows, 0)
-    given = lax.dynamic_slice_in_dim(mine, (1 - ctx) * rows, rows, 0)
-    other = lax.ppermute(given, "ctx", [(0, 1), (1, 0)])
-    first, last = jnp.where(ctx == 0, kept, other), jnp.where(ctx == 0, other, kept)
-    return first.astype(F32), last.astype(F32)
-
-
-def swap_streams(mine, ctx):
-    rows, cols = mine.shape[0] // 2, mine.shape[1] // 2
-    return [part.reshape(rows, 2, cols).transpose(1, 0, 2) for part in swap_halves(mine, ctx)]
 
 
 def on_device(
@@ -1226,6 +1460,7 @@
         text_gates,
         attn_full,
         ffn_mixed,
+        moved,
     ) = enter(
         groups,
         partial_mod.reshape(dp_n, 12, slice_width),
@@ -1247,6 +1482,7 @@
         wide,
     )
     cotangents = (lax.optimization_barrier((cotangents[0], mod_blocks))[0], cotangents[1])
+    image_other = lax.ppermute(cotangents[0], "ctx", [(0, 1), (1, 0)])
     attn_full = attn_full.reshape(2, width, 4 * half)
     ffn_blocks = [ffn_mixed.reshape(2 * wide, 2 * shard_rows, up_half)]
     around = [(i, (i + 1) % dp_n) for i in range(dp_n)]
@@ -1264,22 +1500,10 @@
     slots = tp * own_rows[1] + lax.broadcasted_iota(jnp.int32, (own_rows[1], 1), 0)
     valid = jnp.broadcast_to((slots < text_length).astype(F32), (own_rows[1], width))
 
-    def to_devices(weight):
-        parts = weight.reshape(shard_rows, ctx_n, dp_n, text_cols)
-        return parts.transpose(2, 1, 0, 3).reshape(dp_n * ctx_n, shard_rows, text_cols)
-
-    if groups > 1:
-        moved = jnp.concatenate([to_devices(up_weight[1]), to_devices(down_weight[1])], 2)
-    else:
-        moved = jnp.zeros((1, 8, 128), BF16)
-
-    def both_halves(part):
-        other = lax.ppermute(part, "ctx", [(0, 1), (1, 0)])
-        first, last = jnp.where(ctx == 0, part, other), jnp.where(ctx == 0, other, part)
-        return jnp.concatenate([first, last], 0)
-
-    def feed_grad(stream):
-        return (both_halves(cotangents[stream]).astype(F32) * modulation[stream, 5]).astype(BF16)
+    own_ctx = jnp.full((1,), ctx, jnp.int32)
+
+    def other_half(part):
+        return lax.ppermute(part, "ctx", [(0, 1), (1, 0)])
 
     def blocks(part):
         return part.reshape(2, 2, 2, part.shape[0] // 8, width)
@@ -1300,24 +1524,21 @@
     attentions, middles = attentions_middles[:2], attentions_middles[2:]
     second_low = (image_second.reshape(-1, width), text_second.reshape(-1, width))
 
-    up_full, down_full = [ffn_full[0]], [ffn_full[wide]]
+    up_full, down_full = [(ffn_full, 0)], [(ffn_full, wide)]
     if groups > 1:
         moved_in = moved_in.reshape(width, 2 * text_cols)
-        up_full.append(moved_in[:, :text_cols])
-        down_full.append(moved_in[:, text_cols:])
-        gates = text_gates.reshape(groups, 1, width)
-        feed_grads = (
-            feed_grad(0),
-            (text_cots.reshape(8, groups, own_rows[1], width).astype(F32) * gates).astype(BF16).reshape(-1, width),
-        )
+        up_full.append((moved_in[None, :, :text_cols], 0))
+        down_full.append((moved_in[None, :, text_cols:], 0))
+        text_feed = (text_cots.reshape(-1, width), None, text_gates.reshape(groups, width))
     else:
-        up_full.append(ffn_full[1])
-        down_full.append(ffn_full[3])
-        feed_grads = (feed_grad(0), feed_grad(1))
+        up_full.append((ffn_full, 1))
+        down_full.append((ffn_full, 3))
+        text_feed = (cotangents[1], other_half(cotangents[1]), mod_rows[1, 5])
+    arrivals = ((cotangents[0], image_other, mod_rows[0, 5]), text_feed)
     feed_parts, second_parts, ffn_grads, up_bias_grads = [], [], [], []
     for stream in range(2):
         feed, pulled, grads, sums = feed_forward(
-            second_low[stream], feed_grads[stream], up_full[stream], down_full[stream], up_bias_own[stream]
+            own_ctx, second_low[stream], *arrivals[stream], up_full[stream], down_full[stream], up_bias_own[stream]
         )
         feed_parts.append(blocks(feed))
         second_parts.append(blocks(pulled))
@@ -1332,39 +1553,51 @@
         groups, valid, feed_parts, second_parts, attentions, middles, cotangents_own, mod_rows, down_bias_rows, moved
     )
     attention_grad_all = (image_attn.reshape(-1, width), text_attn.reshape(-1, width))
-    if groups > 1:
-        back = (
-            moved_in.reshape(dp_n, ctx_n, shard_rows, 2, text_cols)
-            .transpose(3, 2, 1, 0, 4)
-            .reshape(2, shard_rows, ctx_n * up_half)
-            .astype(F32)
-        )
-
-    grad_queries, grad_keys, grad_values, out_weight_grads = attend_backward(
-        queries, keys, values, blended, lse, *attention_grad_all, out_full, text_length
-    )
+    out_weight_grads = out_gradient(*attention_grad_all, blended)
     out_weight_grads, ffn_mine = lax.optimization_barrier((out_weight_grads, ffn_mine))
     out_mine = scatter_rows(out_weight_grads)
+    grad_queries, grad_keys, grad_values = attend_backward(
+        queries, keys, values, lse, *attention_grad_all, out_full, text_length
+    )
     *normed_parts, qkv_weight_grads, joint_sums = unproject(
         grad_queries, grad_keys, grad_values, normed_low, attn_full, text_all
     )
     normed_parts = [blocks(part) for part in normed_parts]
     qkv_weight_grads, out_mine = lax.optimization_barrier((qkv_weight_grads, out_mine))
     qkv_mine = scatter_rows(qkv_weight_grads)
+
+    def given(mine):
+        return lax.dynamic_slice_in_dim(mine, (1 - ctx) * shard_rows, shard_rows, 0)
+
     qv_bias_grads = [
         jnp.concatenate([joint_sums[stream, 0, :half], joint_sums[stream, 0, 2 * half :]]) for stream in range(2)
     ]
-    qkv_weight_grad = jnp.concatenate(
-        [part.reshape(2, shard_rows, 3, half) for part in swap_streams(qkv_mine, ctx)], 3
-    )
-    out_weight_grad = jnp.concatenate(swap_streams(out_mine, ctx), 2)
-    ffn_halves = swap_halves(ffn_mine, ctx)
+    qkv_weight_grad = place_qkv(own_ctx, qkv_mine, other_half(given(qkv_mine)))
     if groups > 1:
-        up_weight_grad, down_weight_grad = [
-            jnp.stack([jnp.concatenate([part[:, i * up_half : (i + 1) * up_half] for part in ffn_halves], 1), back[i]])
-            for i in range(2)
-        ]
+        up_bias_grads[1] = lax.dynamic_update_slice_in_dim(
+            jnp.zeros((up_half,), F32), up_bias_grads[1], dp * text_cols, 0
+        )
+    halves = jnp.concatenate(
+        [part.reshape(-1, slice_width) for part in (*qv_bias_grads, *up_bias_grads)], 0
+    )
+    image_outs, text_outs, image_grads, text_grads, packed, halves_all, ffn_other, out_other = leave_step(
+        dp_n,
+        normed_parts,
+        tokens_own,
+        (image_middle_grad, text_middle_grad),
+        (image_out, text_out),
+        sums,
+        mod_rows,
+        halves,
+        ffn_mine,
+        out_mine,
+    )
+    out_weight_grad = place_out(own_ctx, out_mine, out_other)
+    if groups > 1:
+        up_weight_grad, down_weight_grad = place_feed(own_ctx, ffn_mine, ffn_other, moved_in)
     else:
+        kept, other = lax.dynamic_slice_in_dim(ffn_mine, ctx * shard_rows, shard_rows, 0), ffn_other
+        ffn_halves = [jnp.where(ctx == c, kept, other).astype(F32) for c in range(2)]
         up_weight_grad, down_weight_grad = [
             jnp.stack(
                 [
@@ -1374,24 +1607,6 @@
             )
             for i in range(2)
         ]
-
-    if groups > 1:
-        up_bias_grads[1] = lax.dynamic_update_slice_in_dim(
-            jnp.zeros((up_half,), F32), up_bias_grads[1], dp * text_cols, 0
-        )
-    halves = jnp.concatenate(
-        [part.reshape(-1, slice_width) for part in (*qv_bias_grads, *up_bias_grads)], 0
-    )
-    image_outs, text_outs, image_grads, text_grads, packed, halves_all = leave_step(
-        dp_n,
-        normed_parts,
-        tokens_own,
-        (image_middle_grad, text_middle_grad),
-        (image_out, text_out),
-        sums,
-        mod_rows,
-        halves,
-    )
     grad_mod_low = packed[:, :12].astype(BF16)
     ada_bias_grad = jnp.sum(grad_mod_low.astype(F32), axis=0).reshape(2, 6, slice_width)
     grad_mod_low = grad_mod_low.reshape(dp_n, 2, 6, slice_width)

time: 628 us -> 566 us (0.901)
  local copies, waits for them, and re-layouts: 65.9 us -> 28.5 us
  other arithmetic: 28.2 us -> 10.5 us
  waiting for transfers between devices: 29.9 us -> 23.6 us
    slice x13 -> x1, local copies, waits for them, and re-layouts: 27 us -> 1.35 us  [feed_forward(): other, last = (cot[:8], 0)]
    pallas_call x2 -> x6, Pallas kernels: 33.7 us -> 51.2 us  [the longest x2 34.8 us: feed_forward(): pl.pallas_call(functools.partial(feed_kernel, halves), grid_spec=pltpu.Pr...]
    pallas_call x1, Pallas kernels: 115 us -> 103 us  [turn_step(): comm_call(functools.partial(turn_kernel, groups), outs, scratch, 30 + 4 *...]
    reduce_scatter x3, waiting for transfers between devices: 13.6 us -> 2.36 us  [scatter_rows(): return lax.psum_scatter(grad, 'dp', scatter_dimension=0, tiled=True)]
    pallas_call x1, Pallas kernels: 55.6 us -> 65.1 us  [leave_step(): comm_call(functools.partial(leave_kernel, n_dp), outs, scratch, 1 + 10 +...]
    convert_element_type x3 -> x0, other arithmetic: 7.42 us -> none  [the longest x1 3.71 us: on_device(): (text_cots.reshape(8, groups, own_rows[1], width).astype(F32) * gates).as...]
    ppermute x1, waiting for transfers between devices: 3.21 us -> 10.6 us  [on_device(): ffn_blocks.append(lax.ppermute(ffn_blocks[0], 'dp', around))]
  transfers between devices with their start and end apart: 9 -> 7, of which waited for: 5 -> 4; matrix products, arithmetic and copies ran while one was open for 12% -> 5% of each run, Pallas kernels for 41% -> 63%
where the time goes in v4:
time: 566 us; the launch traced here: 564 us
  Pallas kernels  478 us (84%)
  local copies, waits for them, and re-layouts  28.5 us (5%)
  waiting for transfers between devices  23.6 us (4%)
  between operations  14.1 us (2%)
  other arithmetic  10.5 us (2%)
  starting transfers between devices  5.81 us (1%)
    pallas_call x1, Pallas kernels, turn_step(): comm_call(functools.partial(turn_kernel, groups), outs, scratch, 30 + 4 *...  103 us
    pallas_call x1, Pallas kernels, enter(): comm_call(functools.partial(enter_kernel, n_dp, groups), [jax.ShapeDtypeS...  96.6 us
    pallas_call x1, Pallas kernels, middle_step(): comm_call(functools.partial(middle_kernel, n_dp, groups), outs, reduce_sc...  91.3 us
    pallas_call x1, Pallas kernels, leave_step(): comm_call(functools.partial(leave_kernel, n_dp), outs, scratch, 1 + 10 +...  65.1 us
    pallas_call x2, Pallas kernels, feed_forward(): pl.pallas_call(functools.partial(feed_kernel, halves), grid_spec=pltpu.Pr...  34.8 us
    pallas_call x1, Pallas kernels, attend_backward(): local_call(functools.partial(attend_backward_kernel, steps, heads, text_r...  21.1 us
    pallas_call x1, Pallas kernels, attend_forward(): local_call(functools.partial(attend_forward_kernel, steps, heads, text_ro...  18.7 us
    pallas_call x1, Pallas kernels, unproject(): local_call(functools.partial(unproject_kernel, steps), steps + 1, [block,...  14.2 us
  transfers between devices with their start and end apart: 7, of which 4 were waited for; matrix products, arithmetic and copies ran while one was open for 5% of the time, Pallas kernels for 63%

profile of v4, /device:TPU:0, one launch (start us, length us, event | category | flops | bytes accessed | tf_op | source)
XLA Modules:
  0.0 564.1 jit_solution(14379367754190749277)
XLA Ops:
  7.3 1.7 slice_bitcast_fusion.7
  11.4 1.1 pad_maximum_fusion.attn_ref
  12.5 0.7 pad.11
  13.8 96.6 %enter.1 = (f32[4,12,384]{2,1,0:T(8,128)}, f32[8,4,192]{2,1,0:T(4,128)}, bf16[2,4,128,1536]{3,2,1,0:T(8,128)(2,1)}, bf16[2,4,24,1536]{3,2,1,0:T(8,128)(2,1)}, f3...) custom-call(f32[4,12,384]{2,1,0:T(8,128)} %copy.84.part_ref, ...), custom_call_target="tpu_custom_call" | custom-call | tf_op jit(solution)/shard_map/enter/pallas_call | solution.py:909
  111.1 1.9 collective-permute-start.2
  113.1 0.9 copy.85
  116.1 11.1 %project.1 = (bf16[1280,1536]{1,0:T(8,128)(2,1)}, bf16[1280,192]{1,0:T(8,128)(2,1)}, bf16[1280,192]{1,0:T(8,128)(2,1)}, bf16[1280,192]{1,0:T(8,128)(2,1)}, bf16[2,1536,192]{2,1,0:T(8,128)(2,1)}) custom-call(bf16[1024,1536]{1,0:T(8,128)(2,1)} %bitcast.122, bf16[192,1536]{1,0:T(8,128)(2,1)} %bitcast.144, f32[2,2,1,1536]{3,2,1,0:T(1,128)} %slice.143.mod_ref, ...), custom_call_target="tpu_custom_call" | custom-call | flops 2264924160 | bytes 8847360 | tf_op jit(solution)/shard_map/project/pallas_call | solution.py:94
  127.2 10.6 %collective-permute-done.rest_1_ = bf16[2,384,768]{2,1,0:T(8,128)(2,1)S(1)} collective-permute-done((bf16[2,384,768]{2,1,0:T(8,128)(2,1)}, bf16[2,384,768]{2,1,0:T(8,128)(2,1)S(1)}, u32[]{:S(2)}, u32[]{:S(2)}) %collective-permute-start) | collective-permute-done | bytes 1179680 | tf_op jit(solution)/shard_map/ppermute | solution.py:1489
  137.8 1.5 collective-permute-start.1
  140.0 1.3 dynamic-slice_convert_fusion.bias_ref
  141.2 0.7 pad_dynamic-slice_fusion
  141.9 2.0 dynamic-slice_bitcast_fusion
  144.6 18.7 %attend_forward.1 = (bf16[1280,192]{1,0:T(8,128)(2,1)}, f32[3,1280]{1,0:T(4,128)}, bf16[1024,1536]{1,0:T(8,128)(2,1)}, bf16[192,1536]{1,0:T(8,128)(2,1)}) custom-call(bf16[1280,192]{1,0:T(8,128)(2,1)} %get-tuple-element.88.q_ref, bf16[1280,192]{1,0:T(8,128)(2,1)} %get-tuple-element.89.k_ref, bf16[1280,192]{1,0:T(8,128)(2,1)} %get-tuple-element.90.v_ref, ...), custom_call_target="tpu_custom_call" | custom-call | flops 1258291200 | bytes 4915200 | tf_op jit(solution)/shard_map/attend_forward/pallas_call | solution.py:160
  163.3 2.6 collective-permute-done.1.rest_2_
  165.9 91.3 %middle.1 = (f32[128,1536]{1,0:T(8,128)}, f32[24,1536]{1,0:T(8,128)}, f32[128,1536]{1,0:T(8,128)}, f32[24,1536]{1,0:T(8,128)}, bf16[2,2,2,128,1536]{4,3,2,1,0:T(...) custom-call(bf16[2,2,2,128,1536]{4,3,2,1,0:T(8,128)(2,1)} %bitcast.1, ...), custom_call_target="tpu_custom_call" | custom-call | tf_op jit(solution)/shard_map/middle/pallas_call | solution.py:1074
  257.2 24.4 %feed_forward.2 = (bf16[1024,1536]{1,0:T(8,128)(2,1)}, bf16[1024,1536]{1,0:T(8,128)(2,1)}, bf16[1536,1536]{1,0:T(8,128)(2,1)}, f32[1,768]{1,0:T(1,128)}) custom-call(s32[1]{0:T(128)} %bitcast.21.ctx_ref, bf16[1024,1536]{1,0:T(8,128)(2,1)} %bitcast.174, bf16[512,1536]{1,0:T(8,128)(2,1)} %bitcast.156, bf16[512,1536]{1,0:T(8,128)(2,1)} %collective-permute-done.2.other_ref, ...), custom_call_target="tpu_custom_call" | custom-call | flops 14495514624 | bytes 56623104 | tf_op jit(solution)/shard_map/feed_forward/pallas_call | solution.py:438
  283.0 0.7 broadcast_in_dim.36.bias_ref
  283.7 1.3 fusion.7.bias_ref
  285.0 1.3 slice.148.other_ref
  286.3 1.5 slice_bitcast_fusion
  287.8 10.4 %feed_forward.3 = (bf16[768,1536]{1,0:T(8,128)(2,1)}, bf16[768,1536]{1,0:T(8,128)(2,1)}, bf16[1536,384]{1,0:T(8,128)(2,1)}, f32[1,192]{1,0:T(1,128)}) custom-call(s32[1]{0:T(128)} %bitcast.21.ctx_ref, bf16[768,1536]{1,0:T(8,128)(2,1)} %bitcast.175, bf16[768,1536]{1,0:T(8,128)(2,1)} %bitcast.171, bf16[8,1536]{1,0:T(8,128)(2,1)} %slice.148.other_ref, ...), custom_call_target="tpu_custom_call" | custom-call | flops 2717908992 | bytes 10616832 | tf_op jit(solution)/shard_map/feed_forward/pallas_call | solution.py:438
  298.2 0.7 broadcast_in_dim.31.valid_ref
  298.9 102.7 %turn.1 = (bf16[128,1536]{1,0:T(8,128)(2,1)}, bf16[24,1536]{1,0:T(8,128)(2,1)}, f32[128,1536]{1,0:T(8,128)}, f32[24,1536]{1,0:T(8,128)}, f32[2,16,1536]{2,1,0:T(...) custom-call(f32[24,1536]{1,0:T(8,128)} %broadcast_in_dim.31.valid_re, ...), custom_call_target="tpu_custom_call" | custom-call | tf_op jit(solution)/shard_map/turn/pallas_call | solution.py:1236
  401.6 6.2 %out_gradient.1 = bf16[1536,384]{1,0:T(8,128)(2,1)} custom-call(bf16[1024,1536]{1,0:T(8,128)(2,1)} %bitcast.123, bf16[192,1536]{1,0:T(8,128)(2,1)} %bitcast.147, bf16[1280,192]{1,0:T(8,128)(2,1)} %get-tuple-element.130.o_ref), custom_call_target="tpu_custom_call" | custom-call | flops 754974720 | bytes 2949120 | tf_op jit(solution)/shard_map/out_gradient/pallas_call | solution.py:204
  408.2 21.1 %attend_backward.1 = (bf16[1280,192]{1,0:T(8,128)(2,1)}, bf16[1280,192]{1,0:T(8,128)(2,1)}, bf16[1280,192]{1,0:T(8,128)(2,1)}) custom-call(bf16[1280,192]{1,0:T(8,128)(2,1)} %get-tuple-element.88.q_ref, bf16[1280,192]{1,0:T(8,128)(2,1)} %get-tuple-element.89.k_ref, bf16[1280,192]{1,0:T(8,128)(2,1)} %get-tuple-element.90.v_ref, ...), custom_call_target="tpu_custom_call" | custom-call | flops 3145728000 | bytes 12288000 | tf_op jit(solution)/shard_map/attend_backward/pallas_call | solution.py:279
  429.3 14.2 %unproject.1 = (bf16[1024,1536]{1,0:T(8,128)(2,1)}, bf16[192,1536]{1,0:T(8,128)(2,1)}, bf16[1536,1152]{1,0:T(8,128)(2,1)}, f32[2,1,576]{2,1,0:T(1,128)}) custom-call(bf16[1280,192]{1,0:T(8,128)(2,1)} %get-tuple-element.116.dq_ref, bf16[1280,192]{1,0:T(8,128)(2,1)} %get-tuple-element.117.dk_ref, bf16[1280,192]{1,0:T(8,128)(2,1)} %get-tuple-element.118.dv_ref, ...), custom_call_target="tpu_custom_call" | custom-call | flops 4529848320 | bytes 17694720 | tf_op jit(solution)/shard_map/unproject/pallas_call | solution.py:340
  443.6 2.3 reduce-scatter.6.cloned.1.call-done.out_mine
  447.7 65.1 %leave.1 = (bf16[4,128,1536]{2,1,0:T(8,128)(2,1)}, bf16[4,24,1536]{2,1,0:T(8,128)(2,1)}, bf16[4,128,1536]{2,1,0:T(8,128)(2,1)}, bf16[4,24,1536]{2,1,0:T(8,128)(2...) custom-call(bf16[2,2,2,128,1536]{4,3,2,1,0:T(8,128)(2,1)} %bitcast.1, ...), custom_call_target="tpu_custom_call" | custom-call | tf_op jit(solution)/shard_map/leave/pallas_call | solution.py:1370
  512.8 1.0 reduce_sum.48
  513.8 0.9 convert_reduce_fusion
  514.7 0.9 slice_reduce_fusion
  516.8 6.1 %share.1 = f32[4,14,384]{2,1,0:T(8,128)} custom-call(f32[14,384]{1,0:T(8,128)} %select_maximum_fusion.part_ref), custom_call_target="tpu_custom_call" | custom-call | tf_op jit(solution)/shard_map/share/pallas_call | solution.py:1395
  522.9 0.9 slice_bitcast_fusion.8
  526.0 0.7 slice.152
  526.7 0.7 slice.153
  528.1 0.7 reshape.216
  529.4 2.3 place_heads.3
  531.7 4.8 place_feed.1
  536.5 0.8 slice_reduce_fusion.2
  537.3 1.1 constant_dynamic-slice_fusion.2
  538.4 1.2 collective-permute-start.3
  540.1 2.5 convolution_bitcast_fusion
  542.6 8.0 %collective-permute-done.3.other_ref = bf16[192,1152]{1,0:T(8,128)(2,1)S(1)} collective-permute-done((bf16[192,1152]{1,0:T(8,128)(2,1)S(1)}, bf16[192,1152]{1,0:T(8,128)(2,1)S(1)}, u32[]{:S(2)}, u32[]{:S(2)}) %collective-permute-start.3) | collective-permute-done | bytes 442400 | tf_op jit(solution)/shard_map/ppermute | solution.py:1506
  550.6 0.8 copy-done.8
  551.4 3.1 place_heads.2
  554.5 1.1 copy.114
  555.6 0.8 copy-done.2
  556.4 1.1 copy.115
  (112 shorter events, 15.7 us)
Async XLA Ops:
  7.2 2.0 copy-start
  7.2 2.0 copy-start.15
  7.2 400.6 %reduce-scatter.4.cloned.1.call-start = ((), (), s32[]{:S(2)}) async-start(), calls=%async_computation.3 | async-start | bytes 5898240 | tf_op jit(solution)/shard_map/reduce_scatter | solution.py:1408
  7.3 1.8 copy-start.7
  9.0 1.2 copy-start.16
  11.3 1.2 copy-start.6
  11.3 1.9 copy-start.22
  11.4 1.9 copy-start.23
  13.8 99.2 %copy-start.19 = (bf16[2,2,384]{2,1,0:T(2,128)(2,1)S(1)}, bf16[2,2,384]{2,1,0:T(2,128)(2,1)}, u32[]{:S(2)}) copy-start(bf16[2,2,384]{2,1,0:T(2,128)(2,1)} %param.22) | copy-start | bytes 9220
  13.8 101.6 %copy-start.14 = (bf16[2,1536]{1,0:T(2,128)(2,1)S(1)}, bf16[2,1536]{1,0:T(2,128)(2,1)}, u32[]{:S(2)}) copy-start(bf16[2,1536]{1,0:T(2,128)(2,1)} %param.26) | copy-start | bytes 18436
  110.5 27.3 %collective-permute-start = (bf16[2,384,768]{2,1,0:T(8,128)(2,1)}, bf16[2,384,768]{2,1,0:T(8,128)(2,1)S(1)}, u32[]{:S(2)}, u32[]{:S(2)}) collective-permute-start(bf16[2,384,768]{2,1,0:T(8,128)(2,1)} %bitcast.138), channel_id=1, source_target_pairs={{0,8},{8,16},{16,24},{24,0},{1,9},{9,17},{17,25},{25,1},{2,10},{10... | collective-permute-start | bytes 3538952 | tf_op jit(solution)/shard_map/ppermute | solution.py:1489
  111.1 146.1 %collective-permute-start.2 = (bf16[512,1536]{1,0:T(8,128)(2,1)}, bf16[512,1536]{1,0:T(8,128)(2,1)}, u32[]{:S(2)}, u32[]{:S(2)}) collective-permute-start(bf16[512,1536]{1,0:T(8,128)(2,1)} %bitcast.155), channel_id=1, source_target_pairs={{0,4},{4,0},{1,5},{5,1},{2,6},{6,2},{3,7},{7,3},{8,12},{12,8},{9,1... | collective-permute-start | bytes 4718600 | tf_op jit(solution)/shard_map/ppermute | solution.py:1485
  114.1 29.8 %copy-start.4 = (f32[2,6,1,1536]{3,2,1,0:T(1,128)}, f32[2,6,1,1536]{3,2,1,0:T(1,128)S(1)}, u32[]{:S(2)}) copy-start(f32[2,6,1,1536]{3,2,1,0:T(1,128)S(1)} %broadcast_in_dim_reshape.3.mod_ref) | copy-start | bytes 221188
  116.1 23.2 %copy-start.12 = (f32[8,4,192]{2,1,0:T(4,128)S(1)}, f32[8,4,192]{2,1,0:T(4,128)}, u32[]{:S(2)}) copy-start(f32[8,4,192]{2,1,0:T(4,128)} %get-tuple-element.95) | copy-start | bytes 73732
  116.1 25.2 %copy-start.9 = (bf16[1,77,1536]{2,1,0:T(8,128)(2,1)S(1)}, bf16[1,77,1536]{2,1,0:T(8,128)(2,1)}, u32[]{:S(2)}) copy-start(bf16[1,77,1536]{2,1,0:T(8,128)(2,1)} %param.30) | copy-start | bytes 709636
  137.8 25.6 %copy-start.5 = (bf16[2,384,768]{2,1,0:T(8,128)(2,1)}, bf16[2,384,768]{2,1,0:T(8,128)(2,1)S(1)}, u32[]{:S(2)}) copy-start(bf16[2,384,768]{2,1,0:T(8,128)(2,1)S(1)} %collective-permute-done.rest_1_) | copy-start | bytes 3538948
  137.8 28.1 %collective-permute-start.1 = (bf16[2,384,768]{2,1,0:T(8,128)(2,1)S(1)}, bf16[2,384,768]{2,1,0:T(8,128)(2,1)}, u32[]{:S(2)}, u32[]{:S(2)}) collective-permute-start(bf16[2,384,768]{2,1,0:T(8,128)(2,1)S(1)} %collective-permute-done.rest_1_), channel_id=1, source_target_pairs={{0,8},{8,16},{16,24},{24,0},{1,9},{9,17},{17,25},{25,1},{2,10},{10... | collective-permute-start | bytes 3538952 | tf_op jit(solution)/shard_map/ppermute | solution.py:1517
  281.6 0.7 copy-start.13
  281.6 4.7 copy-start.1
  281.7 164.3 %reduce-scatter.6.cloned.1.call-start = ((), (), s32[]{:S(2)}) async-start(), calls=%async_computation.4 | async-start | bytes 1474560 | tf_op jit(solution)/shard_map/reduce_scatter | solution.py:1408
  407.9 129.4 %reduce-scatter.8.cloned.1.call-start = ((), (), s32[]{:S(2)}) async-start(), calls=%async_computation.5 | async-start | bytes 4423680 | tf_op jit(solution)/shard_map/reduce_scatter | solution.py:1408
  445.9 0.7 copy-start.17
  445.9 0.9 copy-start.21
  445.9 1.1 copy-start.18
  512.8 12.5 %copy-start.20 = (f32[2,3]{1,0:T(2,128)S(1)}, f32[2,3]{1,0:T(2,128)}, u32[]{:S(2)}) copy-start(f32[2,3]{1,0:T(2,128)} %constant.70) | copy-start | bytes 76
  512.8 13.2 %copy-start.11 = (bf16[4,24,1536]{2,1,0:T(8,128)(2,1)S(1)}, bf16[4,24,1536]{2,1,0:T(8,128)(2,1)}, u32[]{:S(2)}) copy-start(bf16[4,24,1536]{2,1,0:T(8,128)(2,1)} %get-tuple-element.137) | copy-start | bytes 884740
  515.6 11.1 %copy-start.10 = (bf16[4,24,1536]{2,1,0:T(8,128)(2,1)S(1)}, bf16[4,24,1536]{2,1,0:T(8,128)(2,1)}, u32[]{:S(2)}) copy-start(bf16[4,24,1536]{2,1,0:T(8,128)(2,1)} %get-tuple-element.139) | copy-start | bytes 884740
  538.4 12.3 %collective-permute-start.3 = (bf16[192,1152]{1,0:T(8,128)(2,1)S(1)}, bf16[192,1152]{1,0:T(8,128)(2,1)S(1)}, u32[]{:S(2)}, u32[]{:S(2)}) collective-permute-start(bf16[192,1152]{1,0:T(8,128)(2,1)S(1)} %constant_dynamic-slice_fusion.2), channel_id=1, source_target_pairs={{0,4},{4,0},{1,5},{5,1},{2,6},{6,2},{3,7},{7,3},{8,12},{12,8},{9,1... | collective-permute-start | bytes 1327112 | tf_op jit(solution)/shard_map/ppermute | solution.py:1506
  542.6 11.9 %copy-start.3 = (bf16[4,128,1536]{2,1,0:T(8,128)(2,1)S(1)}, bf16[4,128,1536]{2,1,0:T(8,128)(2,1)}, u32[]{:S(2)}) copy-start(bf16[4,128,1536]{2,1,0:T(8,128)(2,1)} %get-tuple-element.136) | copy-start | bytes 4718596
  550.6 0.8 copy-start.8
  554.5 2.0 copy-start.2
Sparse Core Ops, SparseCore 0:
  281.8 107.0 reduce-scatter.3
  408.0 37.8 reduce-scatter.5
  448.8 73.8 reduce-scatter.7

commit v5 on v4

--- a/solution.py
+++ b/solution.py
@@ -473,6 +473,135 @@
     )(ctx, second, cot, other, gate, up, down, bias.reshape(1, wide))
 
 
+def feed_moving_kernel(
+    groups,
+    halves,
+    second_ref,
+    own_ref,
+    other_ref,
+    gate_ref,
+    up_ref,
+    down_ref,
+    bias_ref,
+    moved_ref,
+    feed_ref,
+    pull_ref,
+    dw_ref,
+    sums_ref,
+    moved_out,
+    up_sum,
+    down_sum,
+    local_sem,
+    send_sems,
+    recv_sems,
+):
+    step = pl.program_id(0)
+    dp, x, tp = lax.axis_index("dp"), lax.axis_index("ctx"), lax.axis_index("tp")
+    wide = up_ref.shape[1]
+    block_rows = second_ref.shape[0]
+    count = groups * 2
+    me = dp * 2 + x
+    peers = [lax.rem(me + offset, count) for offset in range(1, count)]
+    devices = [(peer // 2, peer % 2, tp) for peer in peers]
+    local = pltpu.make_async_copy(moved_ref.at[me], moved_out.at[me], local_sem)
+    moves = [
+        pltpu.make_async_remote_copy(
+            src_ref=moved_ref.at[peer],
+            dst_ref=moved_out.at[me],
+            send_sem=send_sems.at[i],
+            recv_sem=recv_sems.at[i],
+            device_id=device,
+            device_id_type=MESH,
+        )
+        for i, (peer, device) in enumerate(zip(peers, devices))
+    ]
+
+    @pl.when(step == 0)
+    def _():
+        barrier = pltpu.get_barrier_semaphore()
+        for device in devices:
+            pl.semaphore_signal(barrier, inc=1, device_id=device, device_id_type=MESH)
+        pl.semaphore_wait(barrier, len(devices))
+        local.start()
+        for move in moves:
+            move.start()
+        up_sum[...] = jnp.zeros_like(up_sum)
+        down_sum[...] = jnp.zeros_like(down_sum)
+        sums_ref[...] = jnp.zeros_like(sums_ref)
+
+    rows = pl.ds(pl.multiple_of(lax.rem(step, halves) * block_rows, block_rows), block_rows)
+    arriving = jnp.where(step // halves == x, own_ref[rows], other_ref[rows])
+    arriving = (arriving.astype(F32) * gate_ref[...]).astype(BF16)
+    second = second_ref[...]
+    hidden = dot(second, up_ref[...]) + bias_ref[...]
+    gelu_out, slope = gelu_parts(hidden)
+    gelu_low = gelu_out.astype(BF16)
+    feed_ref[...] = dot(gelu_low, down_ref[...], ((1,), (1,))).astype(BF16)
+    down_sum[...] += dot(arriving, gelu_low, ((0,), (0,)))
+    pulled = (dot(arriving, down_ref[...]) * slope).astype(BF16)
+    sums_ref[...] += jnp.sum(pulled.astype(F32), axis=0, keepdims=True)
+    up_sum[...] += dot(second, pulled, ((0,), (0,)))
+    pull_ref[...] = dot(pulled, up_ref[...], ((1,), (1,))).astype(BF16)
+
+    @pl.when(step == pl.num_programs(0) - 1)
+    def _():
+        dw_ref[:, :wide] = up_sum[...].astype(BF16)
+        dw_ref[:, wide:] = down_sum[...].astype(BF16)
+        local.wait()
+        for move in moves:
+            move.wait()
+
+
+def feed_forward_moving(groups, second, own, other, gate, up, down, bias, moved):
+    (up, up_at), (down, down_at) = up, down
+    (rows, width), wide = second.shape, up.shape[2]
+    block_rows = min(QUERY_BLOCK, own.shape[0])
+    block = stepped((block_rows, width))
+    peers = 2 * groups - 1
+
+    def weight(shape, place):
+        return pl.BlockSpec((None,) + shape[1:], lambda i: (place, 0, 0), pipeline_mode=pl.Buffered(1))
+
+    return pl.pallas_call(
+        functools.partial(feed_moving_kernel, groups, own.shape[0] // block_rows),
+        grid=(rows // block_rows,),
+        in_specs=[
+            block,
+            fixed(own.shape),
+            fixed(other.shape),
+            fixed(gate.shape),
+            weight(up.shape, up_at),
+            weight(down.shape, down_at),
+            fixed((1, wide)),
+            pl.BlockSpec(memory_space=pl.ANY),
+        ],
+        out_specs=[
+            block,
+            block,
+            pl.BlockSpec((width, 2 * wide), lambda i: (0, 0)),
+            pl.BlockSpec((1, wide), lambda i: (0, 0)),
+            pl.BlockSpec(memory_space=pl.ANY),
+        ],
+        out_shape=[
+            jax.ShapeDtypeStruct((rows, width), BF16),
+            jax.ShapeDtypeStruct((rows, width), BF16),
+            jax.ShapeDtypeStruct((width, 2 * wide), BF16),
+            jax.ShapeDtypeStruct((1, wide), F32),
+            jax.ShapeDtypeStruct(moved.shape, BF16),
+        ],
+        scratch_shapes=[pltpu.VMEM((width, wide), F32)] * 2
+        + [
+            pltpu.SemaphoreType.DMA(()),
+            pltpu.SemaphoreType.DMA((peers,)),
+            pltpu.SemaphoreType.DMA((peers,)),
+        ],
+        compiler_params=pltpu.CompilerParams(
+            collective_id=5, has_side_effects=True, vmem_limit_bytes=VMEM_LIMIT
+        ),
+        name="feed_moving",
+    )(second, own, other, gate, up, down, bias.reshape(1, wide), moved)
+
+
 def place_feed_kernel(ctx_ref, mine_ref, other_ref, moved_ref, up_ref, down_ref):
     ctx = ctx_ref[0]
     cols = mine_ref.shape[2] // 2
@@ -505,6 +634,32 @@
         compiler_params=pltpu.CompilerParams(vmem_limit_bytes=VMEM_LIMIT),
         name="place_feed",
     )(ctx, mine.reshape(2, rows, cols), other, moved)
+
+
+def place_tokens_kernel(image_out, text_out, image_grad, text_grad, *outs):
+    for source, place in zip((image_out, image_grad), outs[::2]):
+        rows = source.shape[1]
+        for block in range(source.shape[0]):
+            place[0, block * rows : (block + 1) * rows] = source[block]
+    for source, place in zip((text_out, text_grad), outs[1::2]):
+        rows, length = source.shape[1], place.shape[1]
+        for block in range(source.shape[0]):
+            used = min(rows, length - block * rows)
+            place[0, block * rows : block * rows + used] = source[block, :used]
+
+
+def place_tokens(parts, image_length, text_length):
+    shapes = [
+        jax.ShapeDtypeStruct((1, length, parts[0].shape[2]), BF16) for length in (image_length, text_length) * 2
+    ]
+    return pl.pallas_call(
+        place_tokens_kernel,
+        in_specs=[pl.BlockSpec(memory_space=pltpu.VMEM)] * 4,
+        out_specs=[pl.BlockSpec(memory_space=pltpu.VMEM)] * 4,
+        out_shape=shapes,
+        compiler_params=pltpu.CompilerParams(vmem_limit_bytes=VMEM_LIMIT),
+        name="place_tokens",
+    )(*parts)
 
 
 def place_heads_kernel(kinds, ctx_ref, mine_ref, other_ref, out_ref):
@@ -925,6 +1080,11 @@
         [VMEM_SPEC] * 8,
         [VMEM_SPEC] * 8,
     )(partial_mod, ada_bias, bias_rows, image, text, attn, up, down)
+
+
+def meet_planes(wires, groups):
+    planes = [(lax.rem(wires.dp + offset, groups), wires.x, wires.tp) for offset in range(1, groups)]
+    wires.meet(planes + [wires.x_next, wires.y_next, wires.k_next])
 
 
 def meet_groups(wires, groups, more=()):
@@ -1098,7 +1258,6 @@
     text_cot,
     mod_ref,
     bias_ref,
-    moved_ref,
     image_out,
     text_out,
     image_grad,
@@ -1106,13 +1265,12 @@
     sums_ref,
     image_all,
     text_all,
-    moved_out,
     *scratch,
 ):
-    z_out, z_in, local_sem, send_sems, recv_sems = scratch[-5:]
+    z_out, z_in, send_sems, recv_sems = scratch[-4:]
     wires = Wires(send_sems, recv_sems)
     dp, x, y, k, tp = wires.dp, wires.x, wires.y, wires.k, wires.tp
-    meet_groups(wires, groups)
+    meet_planes(wires, groups)
     size = len(REDUCE_KEYS)
     streams = [
         dict(zip(("part",) + REDUCE_KEYS, (part,) + scratch[i * size : (i + 1) * size]))
@@ -1209,7 +1367,6 @@
     spread_two = [spread_second(wires, block, arrived) for block, arrived in zip((image_all, text_all), spread_one)]
     reduce_last(wires, feeds[1], feed_third[0])
     planes = to_planes(1, feeds[1]["total"])
-    moves = start_moves(wires, groups, moved_ref, moved_out, local_sem)
     reduce_last(wires, feeds[0], feed_third[1])
     spread_three = [spread_third(wires, block, arrived) for block, arrived in zip((image_all, text_all), spread_two)]
     feed_side(0)
@@ -1217,22 +1374,20 @@
     feed_side(1)
     for arrived in spread_three:
         arrived.wait_recv()
-    end_moves(moves)
     wires.finish()
 
 
-def turn_step(groups, valid, feeds, seconds, attentions, middles, cots, mod, bias, moved):
+def turn_step(groups, valid, feeds, seconds, attentions, middles, cots, mod, bias):
     width = middles[0].shape[1]
     rows = [part.shape[0] for part in middles]
     outs = [jax.ShapeDtypeStruct((r, width), BF16) for r in rows]
     outs += [jax.ShapeDtypeStruct((r, width), F32) for r in rows]
     outs += [jax.ShapeDtypeStruct((2, 16, width), F32)]
     outs += [jax.ShapeDtypeStruct((2, 2, 2, r, width), BF16) for r in rows]
-    outs += [jax.ShapeDtypeStruct(moved.shape, BF16)]
     scratch = []
     for r in (rows[1] * groups, rows[0]):
         scratch += reduce_scratch(r, width) + reduce_scratch(r, width)
-    scratch += [pltpu.VMEM((2, groups, rows[1], width), BF16)] * 2 + [pltpu.SemaphoreType.DMA(())]
+    scratch += [pltpu.VMEM((2, groups, rows[1], width), BF16)] * 2
     return comm_call(
         functools.partial(turn_kernel, groups),
         outs,
@@ -1240,9 +1395,9 @@
         30 + 4 * groups,
         2,
         "turn",
-        [VMEM_SPEC] * 13 + [ANY_SPEC],
-        [VMEM_SPEC] * 7 + [ANY_SPEC],
-    )(valid, *feeds, *seconds, *attentions, *middles, *cots, mod, bias, moved)
+        [VMEM_SPEC] * 13,
+        [VMEM_SPEC] * 7,
+    )(valid, *feeds, *seconds, *attentions, *middles, *cots, mod, bias)
 
 
 PACKED = 24
@@ -1536,21 +1691,26 @@
         text_feed = (cotangents[1], other_half(cotangents[1]), mod_rows[1, 5])
     arrivals = ((cotangents[0], image_other, mod_rows[0, 5]), text_feed)
     feed_parts, second_parts, ffn_grads, up_bias_grads = [], [], [], []
+    done = {}
+    for stream in (1, 0):
+        operands = (second_low[stream], *arrivals[stream], up_full[stream], down_full[stream], up_bias_own[stream])
+        if groups > 1 and stream == 0:
+            moved = done[1][2].reshape(dp_n * ctx_n, shard_rows, 2 * text_cols)
+            *done[0], moved_in = feed_forward_moving(groups, *operands, moved)
+        else:
+            done[stream] = feed_forward(own_ctx, *operands)
     for stream in range(2):
-        feed, pulled, grads, sums = feed_forward(
-            own_ctx, second_low[stream], *arrivals[stream], up_full[stream], down_full[stream], up_bias_own[stream]
-        )
+        feed, pulled, grads, sums = done[stream]
         feed_parts.append(blocks(feed))
         second_parts.append(blocks(pulled))
         ffn_grads.append(grads)
         up_bias_grads.append(sums[0])
     if groups > 1:
         ffn_mine = scatter_rows(ffn_grads[0])
-        moved = ffn_grads[1].reshape(dp_n * ctx_n, shard_rows, 2 * text_cols)
     else:
         ffn_mine = scatter_rows(jnp.concatenate(ffn_grads, 1))
-    image_out, text_out, image_middle_grad, text_middle_grad, sums, image_attn, text_attn, moved_in = turn_step(
-        groups, valid, feed_parts, second_parts, attentions, middles, cotangents_own, mod_rows, down_bias_rows, moved
+    image_out, text_out, image_middle_grad, text_middle_grad, sums, image_attn, text_attn = turn_step(
+        groups, valid, feed_parts, second_parts, attentions, middles, cotangents_own, mod_rows, down_bias_rows
     )
     attention_grad_all = (image_attn.reshape(-1, width), text_attn.reshape(-1, width))
     out_weight_grads = out_gradient(*attention_grad_all, blended)
@@ -1572,7 +1732,6 @@
     qv_bias_grads = [
         jnp.concatenate([joint_sums[stream, 0, :half], joint_sums[stream, 0, 2 * half :]]) for stream in range(2)
     ]
-    qkv_weight_grad = place_qkv(own_ctx, qkv_mine, other_half(given(qkv_mine)))
     if groups > 1:
         up_bias_grads[1] = lax.dynamic_update_slice_in_dim(
             jnp.zeros((up_half,), F32), up_bias_grads[1], dp * text_cols, 0
@@ -1592,6 +1751,19 @@
         ffn_mine,
         out_mine,
     )
+    grad_mod_low = packed[:, :12].astype(BF16)
+    ada_bias_grad = jnp.sum(grad_mod_low.astype(F32), axis=0).reshape(2, 6, slice_width)
+    grad_mod_low = grad_mod_low.reshape(dp_n, 2, 6, slice_width)
+    ada_weight_grad = jnp.einsum("nd,nakf->adkf", activated_low, grad_mod_low, preferred_element_type=F32)
+    cond_partial = jnp.einsum("nakf,adkf->nd", grad_mod_low, ada_weight, preferred_element_type=F32)
+    totals = jnp.sum(packed[:, 12:22], axis=0)
+    cond_rows = jnp.pad(cond_partial, ((0, -dp_n % 2), (0, slice_width - shard_rows)))
+    shared = share(jnp.concatenate([totals, cond_rows], 0))
+    shared, qkv_given, image_outs, text_outs, out_other, ffn_other = lax.optimization_barrier(
+        (shared, given(qkv_mine), image_outs, text_outs, out_other, ffn_other)
+    )
+    qkv_other = other_half(qkv_given)
+    final_tokens = place_tokens((image_outs, text_outs, image_grads, text_grads), image_length, text_length)
     out_weight_grad = place_out(own_ctx, out_mine, out_other)
     if groups > 1:
         up_weight_grad, down_weight_grad = place_feed(own_ctx, ffn_mine, ffn_other, moved_in)
@@ -1607,14 +1779,7 @@
             )
             for i in range(2)
         ]
-    grad_mod_low = packed[:, :12].astype(BF16)
-    ada_bias_grad = jnp.sum(grad_mod_low.astype(F32), axis=0).reshape(2, 6, slice_width)
-    grad_mod_low = grad_mod_low.reshape(dp_n, 2, 6, slice_width)
-    ada_weight_grad = jnp.einsum("nd,nakf->adkf", activated_low, grad_mod_low, preferred_element_type=F32)
-    cond_partial = jnp.einsum("nakf,adkf->nd", grad_mod_low, ada_weight, preferred_element_type=F32)
-    totals = jnp.sum(packed[:, 12:22], axis=0)
-    cond_rows = jnp.pad(cond_partial, ((0, -dp_n % 2), (0, slice_width - shard_rows)))
-    shared = share(jnp.concatenate([totals, cond_rows], 0))
+    qkv_weight_grad = place_qkv(own_ctx, qkv_mine, qkv_other)
     cond_total = jnp.sum(shared[:, 10 : 10 + dp_n, :shard_rows], axis=0)
     cond_grad = jax.vjp(jax.nn.silu, cond_float)[1](cond_total)[0]
     full = shared[:, :10].transpose(1, 0, 2).reshape(2, 5, width)
@@ -1635,10 +1800,7 @@
         .reshape(2, ctx_n * up_half)
     )
     return (
-        image_outs.reshape(1, image_length, width),
-        text_outs.reshape(1, TEXT_SLOTS, width)[:, :text_length],
-        image_grads.reshape(1, image_length, width),
-        text_grads.reshape(1, TEXT_SLOTS, width)[:, :text_length],
+        *final_tokens,
         cond_grad,
         ada_weight_grad,
         ada_bias_grad,

time: 566 us -> 550 us (0.972)
  Pallas kernels: 478 us -> 468 us
    pallas_call x0 -> x2, Pallas kernels: none -> 36.3 us  [the longest x1 32.4 us: feed_forward_moving(): pl.pallas_call(functools.partial(feed_moving_kernel, groups, own.shape[0]...]
    pallas_call x2 -> x1, Pallas kernels: 34.8 us -> 10.4 us  [feed_forward(): pl.pallas_call(functools.partial(feed_kernel, halves), grid_spec=pltpu.Pr...]
    pallas_call x1, Pallas kernels: 103 us -> 84.3 us  [turn_step(): comm_call(functools.partial(turn_kernel, groups), outs, scratch, 30 + 4 *...]
    ppermute x1, waiting for transfers between devices: 8.01 us -> 0.01 us  [other_half(): return lax.ppermute(part, 'ctx', [(0, 1), (1, 0)])]
    reduce_scatter x3, waiting for transfers between devices: 2.36 us -> 9.68 us  [scatter_rows(): return lax.psum_scatter(grad, 'dp', scatter_dimension=0, tiled=True)]
  transfers between devices with their start and end apart: 7 -> 7, of which waited for: 4 -> 3; matrix products, arithmetic and copies ran while one was open for 5% -> 5% of each run, Pallas kernels for 63% -> 62%
where the time goes in v5:
time: 550 us; the launch traced here: 546 us
  Pallas kernels  468 us (85%)
  local copies, waits for them, and re-layouts  23.4 us (4%)
  waiting for transfers between devices  23.2 us (4%)
  between operations  14.1 us (3%)
  other arithmetic  8.34 us (2%)
    pallas_call x1, Pallas kernels, enter(): comm_call(functools.partial(enter_kernel, n_dp, groups), [jax.ShapeDtypeS...  96.6 us
    pallas_call x1, Pallas kernels, middle_step(): comm_call(functools.partial(middle_kernel, n_dp, groups), outs, reduce_sc...  91.2 us
    pallas_call x1, Pallas kernels, turn_step(): comm_call(functools.partial(turn_kernel, groups), outs, scratch, 30 + 4 *...  84.3 us
    pallas_call x1, Pallas kernels, leave_step(): comm_call(functools.partial(leave_kernel, n_dp), outs, scratch, 1 + 10 +...  62.9 us
    pallas_call x1, Pallas kernels, feed_forward_moving(): pl.pallas_call(functools.partial(feed_moving_kernel, groups, own.shape[0]...  32.4 us
    pallas_call x1, Pallas kernels, attend_backward(): local_call(functools.partial(attend_backward_kernel, steps, heads, text_r...  21.1 us
    pallas_call x1, Pallas kernels, attend_forward(): local_call(functools.partial(attend_forward_kernel, steps, heads, text_ro...  18.7 us
    pallas_call x1, Pallas kernels, unproject(): local_call(functools.partial(unproject_kernel, steps), steps + 1, [block,...  14.2 us
  transfers between devices with their start and end apart: 7, of which 3 were waited for; matrix products, arithmetic and copies ran while one was open for 5% of the time, Pallas kernels for 62%

profile of v5, /device:TPU:0, one launch (start us, length us, event | category | flops | bytes accessed | tf_op | source)
XLA Modules:
  0.0 546.4 jit_solution(16479423920110681875)
XLA Ops:
  7.3 1.7 slice_bitcast_fusion.7
  9.5 0.7 copy.84.part_ref
  11.4 1.1 pad_maximum_fusion.attn_ref
  12.5 0.7 pad.11
  13.8 96.6 %enter.1 = (f32[4,12,384]{2,1,0:T(8,128)}, f32[8,4,192]{2,1,0:T(4,128)}, bf16[2,4,128,1536]{3,2,1,0:T(8,128)(2,1)}, bf16[2,4,24,1536]{3,2,1,0:T(8,128)(2,1)}, f3...) custom-call(f32[4,12,384]{2,1,0:T(8,128)} %copy.84.part_ref, ...), custom_call_target="tpu_custom_call" | custom-call | tf_op jit(solution)/shard_map/enter/pallas_call | solution.py:1064
  110.4 0.6 collective-permute-start
  111.1 1.9 collective-permute-start.2
  113.1 0.9 copy.85
  114.1 0.6 slice.135.mod_ref
  115.5 11.1 %project.1 = (bf16[1280,1536]{1,0:T(8,128)(2,1)}, bf16[1280,192]{1,0:T(8,128)(2,1)}, bf16[1280,192]{1,0:T(8,128)(2,1)}, bf16[1280,192]{1,0:T(8,128)(2,1)}, bf16[2,1536,192]{2,1,0:T(8,128)(2,1)}) custom-call(bf16[1024,1536]{1,0:T(8,128)(2,1)} %bitcast.120, bf16[192,1536]{1,0:T(8,128)(2,1)} %bitcast.143, f32[2,2,1,1536]{3,2,1,0:T(1,128)} %slice.135.mod_ref, ...), custom_call_target="tpu_custom_call" | custom-call | flops 2264924160 | bytes 8847360 | tf_op jit(solution)/shard_map/project/pallas_call | solution.py:94
  126.6 11.3 %collective-permute-done.rest_1_ = bf16[2,384,768]{2,1,0:T(8,128)(2,1)} collective-permute-done((bf16[2,384,768]{2,1,0:T(8,128)(2,1)}, bf16[2,384,768]{2,1,0:T(8,128)(2,1)}, u32[]{:S(2)}, u32[]{:S(2)}) %collective-permute-start) | collective-permute-done | bytes 1179680 | tf_op jit(solution)/shard_map/ppermute | solution.py:1644
  137.9 1.5 collective-permute-start.1
  139.3 0.6 fusion.7.bias_ref
  140.0 0.7 broadcast_in_dim.32.bias_ref
  141.9 2.0 dynamic-slice_bitcast_fusion
  143.8 0.7 pad_dynamic-slice_fusion
  145.1 18.7 %attend_forward.1 = (bf16[1280,192]{1,0:T(8,128)(2,1)}, f32[3,1280]{1,0:T(4,128)}, bf16[1024,1536]{1,0:T(8,128)(2,1)}, bf16[192,1536]{1,0:T(8,128)(2,1)}) custom-call(bf16[1280,192]{1,0:T(8,128)(2,1)} %get-tuple-element.98.q_ref, bf16[1280,192]{1,0:T(8,128)(2,1)} %get-tuple-element.99.k_ref, bf16[1280,192]{1,0:T(8,128)(2,1)} %get-tuple-element.100.v_ref, ...), custom_call_target="tpu_custom_call" | custom-call | flops 1258291200 | bytes 4915200 | tf_op jit(solution)/shard_map/attend_forward/pallas_call | solution.py:160
  163.9 2.2 collective-permute-done.1.rest_2_
  166.1 91.2 %middle.1 = (f32[128,1536]{1,0:T(8,128)}, f32[24,1536]{1,0:T(8,128)}, f32[128,1536]{1,0:T(8,128)}, f32[24,1536]{1,0:T(8,128)}, bf16[2,2,2,128,1536]{4,3,2,1,0:T(...) custom-call(bf16[2,2,2,128,1536]{4,3,2,1,0:T(8,128)(2,1)} %bitcast.1, ...), custom_call_target="tpu_custom_call" | custom-call | tf_op jit(solution)/shard_map/middle/pallas_call | solution.py:1234
  257.3 1.3 slice.140.other_ref
  258.7 2.8 slice_bitcast_fusion
  261.5 10.4 %feed_forward.1 = (bf16[768,1536]{1,0:T(8,128)(2,1)}, bf16[768,1536]{1,0:T(8,128)(2,1)}, bf16[1536,384]{1,0:T(8,128)(2,1)}, f32[1,192]{1,0:T(1,128)}) custom-call(s32[1]{0:T(128)} %bitcast.30.ctx_ref, bf16[768,1536]{1,0:T(8,128)(2,1)} %bitcast.167, bf16[768,1536]{1,0:T(8,128)(2,1)} %bitcast.166, bf16[8,1536]{1,0:T(8,128)(2,1)} %slice.140.other_ref, ...), custom_call_target="tpu_custom_call" | custom-call | flops 2717908992 | bytes 10616832 | tf_op jit(solution)/shard_map/feed_forward/pallas_call | solution.py:438
  271.9 32.4 %feed_moving.1 = (bf16[1024,1536]{1,0:T(8,128)(2,1)}, bf16[1024,1536]{1,0:T(8,128)(2,1)}, bf16[1536,1536]{1,0:T(8,128)(2,1)}, f32[1,768]{1,0:T(1,128)}, bf16[8,192,384]{2,1,0:T(8,128)(2,1)}) custom-call(bf16[1024,1536]{1,0:T(8,128)(2,1)} %bitcast.126, bf16[512,1536]{1,0:T(8,128)(2,1)} %bitcast.128, bf16[512,1536]{1,0:T(8,128)(2,1)} %collective-permute-done.2.other_ref, ...), custom_call_target="tpu_custom_call" | custom-call | tf_op jit(solution)/shard_map/feed_moving/pallas_call | solution.py:565
  304.6 0.7 broadcast_in_dim.36.bias_ref
  305.3 0.7 broadcast_in_dim.31.valid_ref
  306.1 84.3 %turn.1 = (bf16[128,1536]{1,0:T(8,128)(2,1)}, bf16[24,1536]{1,0:T(8,128)(2,1)}, f32[128,1536]{1,0:T(8,128)}, f32[24,1536]{1,0:T(8,128)}, f32[2,16,1536]{2,1,0:T(...) custom-call(f32[24,1536]{1,0:T(8,128)} %broadcast_in_dim.31.valid_ref, ...), custom_call_target="tpu_custom_call" | custom-call | tf_op jit(solution)/shard_map/turn/pallas_call | solution.py:1391
  390.4 6.2 %out_gradient.1 = bf16[1536,384]{1,0:T(8,128)(2,1)} custom-call(bf16[1024,1536]{1,0:T(8,128)(2,1)} %bitcast.123, bf16[192,1536]{1,0:T(8,128)(2,1)} %bitcast.146, bf16[1280,192]{1,0:T(8,128)(2,1)} %get-tuple-element.140.o_ref), custom_call_target="tpu_custom_call" | custom-call | flops 754974720 | bytes 2949120 | tf_op jit(solution)/shard_map/out_gradient/pallas_call | solution.py:204
  396.7 9.7 %reduce-scatter.4.cloned.1.call-done.ffn_mine = bf16[384,1536]{1,0:T(8,128)(2,1)} async-done(((bf16[1536,1536]{1,0:T(8,128)(2,1)}), bf16[384,1536]{1,0:T(8,128)(2,1)}) %reduce-scatter.4.cloned.1.call-update) | async-done | bytes 1179664 | tf_op jit(solution)/shard_map/reduce_scatter | solution.py:1563
  406.4 21.1 %attend_backward.1 = (bf16[1280,192]{1,0:T(8,128)(2,1)}, bf16[1280,192]{1,0:T(8,128)(2,1)}, bf16[1280,192]{1,0:T(8,128)(2,1)}) custom-call(bf16[1280,192]{1,0:T(8,128)(2,1)} %get-tuple-element.98.q_ref, bf16[1280,192]{1,0:T(8,128)(2,1)} %get-tuple-element.99.k_ref, bf16[1280,192]{1,0:T(8,128)(2,1)} %get-tuple-element.100.v_ref, ...), custom_call_target="tpu_custom_call" | custom-call | flops 3145728000 | bytes 12288000 | tf_op jit(solution)/shard_map/attend_backward/pallas_call | solution.py:279
  427.6 14.2 %unproject.1 = (bf16[1024,1536]{1,0:T(8,128)(2,1)}, bf16[192,1536]{1,0:T(8,128)(2,1)}, bf16[1536,1152]{1,0:T(8,128)(2,1)}, f32[2,1,576]{2,1,0:T(1,128)}) custom-call(bf16[1280,192]{1,0:T(8,128)(2,1)} %get-tuple-element.126.dq_ref, bf16[1280,192]{1,0:T(8,128)(2,1)} %get-tuple-element.127.dk_ref, bf16[1280,192]{1,0:T(8,128)(2,1)} %get-tuple-element.128.dv_ref, ...), custom_call_target="tpu_custom_call" | custom-call | flops 4529848320 | bytes 17694720 | tf_op jit(solution)/shard_map/unproject/pallas_call | solution.py:340
  441.8 0.6 copy-done.14
  443.5 62.9 %leave.1 = (bf16[4,128,1536]{2,1,0:T(8,128)(2,1)}, bf16[4,24,1536]{2,1,0:T(8,128)(2,1)}, bf16[4,128,1536]{2,1,0:T(8,128)(2,1)}, bf16[4,24,1536]{2,1,0:T(8,128)(2...) custom-call(bf16[2,2,2,128,1536]{4,3,2,1,0:T(8,128)(2,1)} %bitcast.1, ...), custom_call_target="tpu_custom_call" | custom-call | tf_op jit(solution)/shard_map/leave/pallas_call | solution.py:1525
  506.4 0.9 reduce_sum.48
  507.3 0.9 convert_reduce_fusion
  508.3 0.9 slice_reduce_fusion
  509.8 0.6 select_maximum_fusion.part_ref
  510.4 5.3 share.1
  515.7 0.6 copy.93
  516.4 0.7 reshape.200
  517.1 0.6 reshape.204
  517.7 2.5 convolution_bitcast_fusion
  520.2 1.0 constant_dynamic-slice_fusion.2
  521.4 1.1 collective-permute-start.3
  524.4 2.3 place_heads.3
  526.7 4.8 place_feed.1
  531.5 3.8 place_tokens.1
  536.0 0.8 copy-done.7
  536.7 3.1 place_heads.2
  (103 shorter events, 9.9 us)
Async XLA Ops:
  7.2 2.0 copy-start
  7.2 2.0 copy-start.12
  7.2 399.1 %reduce-scatter.4.cloned.1.call-start = ((), (), s32[]{:S(2)}) async-start(), calls=%async_computation.3 | async-start | bytes 5898240 | tf_op jit(solution)/shard_map/reduce_scatter | solution.py:1563
  7.3 1.8 copy-start.5
  9.0 1.2 copy-start.13
  11.3 1.2 copy-start.3
  11.3 1.9 copy-start.19
  11.3 1.9 copy-start.20
  13.8 97.2 %copy-start.1 = (bf16[1,512,1536]{2,1,0:T(8,128)(2,1)S(1)}, bf16[1,512,1536]{2,1,0:T(8,128)(2,1)}, u32[]{:S(2)}) copy-start(bf16[1,512,1536]{2,1,0:T(8,128)(2,1)} %param.29) | copy-start | bytes 4718596
  13.8 99.2 %copy-start.16 = (bf16[2,2,384]{2,1,0:T(2,128)(2,1)S(1)}, bf16[2,2,384]{2,1,0:T(2,128)(2,1)}, u32[]{:S(2)}) copy-start(bf16[2,2,384]{2,1,0:T(2,128)(2,1)} %param.22) | copy-start | bytes 9220
  110.4 27.4 %collective-permute-start = (bf16[2,384,768]{2,1,0:T(8,128)(2,1)}, bf16[2,384,768]{2,1,0:T(8,128)(2,1)}, u32[]{:S(2)}, u32[]{:S(2)}) collective-permute-start(bf16[2,384,768]{2,1,0:T(8,128)(2,1)} %bitcast.137), channel_id=1, source_target_pairs={{0,8},{8,16},{16,24},{24,0},{1,9},{9,17},{17,25},{25,1},{2,10},{10... | collective-permute-start | bytes 3538952 | tf_op jit(solution)/shard_map/ppermute | solution.py:1644
  111.1 160.8 %collective-permute-start.2 = (bf16[512,1536]{1,0:T(8,128)(2,1)S(1)}, bf16[512,1536]{1,0:T(8,128)(2,1)}, u32[]{:S(2)}, u32[]{:S(2)}) collective-permute-start(bf16[512,1536]{1,0:T(8,128)(2,1)S(1)} %bitcast.129), channel_id=1, source_target_pairs={{0,4},{4,0},{1,5},{5,1},{2,6},{6,2},{3,7},{7,3},{8,12},{12,8},{9,1... | collective-permute-start | bytes 4718600 | tf_op jit(solution)/shard_map/ppermute | solution.py:1640
  114.1 30.4 %copy-start.2 = (f32[2,6,1,1536]{3,2,1,0:T(1,128)}, f32[2,6,1,1536]{3,2,1,0:T(1,128)S(1)}, u32[]{:S(2)}) copy-start(f32[2,6,1,1536]{3,2,1,0:T(1,128)S(1)} %broadcast_in_dim_reshape.3.mod_ref) | copy-start | bytes 221188
  115.4 11.1 %copy-start.9 = (f32[8,4,192]{2,1,0:T(4,128)S(1)}, f32[8,4,192]{2,1,0:T(4,128)}, u32[]{:S(2)}) copy-start(f32[8,4,192]{2,1,0:T(4,128)} %get-tuple-element.105) | copy-start | bytes 73732
  115.4 11.1 %copy-start.11 = (bf16[2,1536]{1,0:T(2,128)(2,1)S(1)}, bf16[2,1536]{1,0:T(2,128)(2,1)}, u32[]{:S(2)}) copy-start(bf16[2,1536]{1,0:T(2,128)(2,1)} %param.26) | copy-start | bytes 18436
  115.5 25.2 %copy-start.10 = (f32[4,4,384]{2,1,0:T(4,128)S(1)}, f32[4,4,384]{2,1,0:T(4,128)}, u32[]{:S(2)}) copy-start(f32[4,4,384]{2,1,0:T(4,128)} %get-tuple-element.113) | copy-start | bytes 73732
  137.9 28.2 %collective-permute-start.1 = (bf16[2,384,768]{2,1,0:T(8,128)(2,1)}, bf16[2,384,768]{2,1,0:T(8,128)(2,1)}, u32[]{:S(2)}, u32[]{:S(2)}) collective-permute-start(bf16[2,384,768]{2,1,0:T(8,128)(2,1)} %collective-permute-done.rest_1_), channel_id=1, source_target_pairs={{0,8},{8,16},{16,24},{24,0},{1,9},{9,17},{17,25},{25,1},{2,10},{10... | collective-permute-start | bytes 3538952 | tf_op jit(solution)/shard_map/ppermute | solution.py:1672
  141.3 2.5 copy-start.4
  141.3 2.5 copy-start.8
  304.4 137.4 %reduce-scatter.6.cloned.1.call-start = ((), (), s32[]{:S(2)}) async-start(), calls=%async_computation.4 | async-start | bytes 1474560 | tf_op jit(solution)/shard_map/reduce_scatter | solution.py:1563
  406.4 113.8 %reduce-scatter.8.cloned.1.call-start = ((), (), s32[]{:S(2)}) async-start(), calls=%async_computation.5 | async-start | bytes 4423680 | tf_op jit(solution)/shard_map/reduce_scatter | solution.py:1563
  441.8 0.7 copy-start.14
  441.8 0.9 copy-start.15
  441.8 0.9 copy-start.18
  517.7 3.5 copy-start.6
  517.7 4.8 copy-start.17
  521.4 14.6 %collective-permute-start.3 = (bf16[192,1152]{1,0:T(8,128)(2,1)S(1)}, bf16[192,1152]{1,0:T(8,128)(2,1)S(1)}, u32[]{:S(2)}, u32[]{:S(2)}) collective-permute-start(bf16[192,1152]{1,0:T(8,128)(2,1)S(1)} %constant_dynamic-slice_fusion.2), channel_id=1, source_target_pairs={{0,4},{4,0},{1,5},{5,1},{2,6},{6,2},{3,7},{7,3},{8,12},{12,8},{9,1... | collective-permute-start | bytes 1327112 | tf_op jit(solution)/shard_map/ppermute | solution.py:1661
  536.0 0.8 copy-start.7
Sparse Core Ops, SparseCore 0:
  304.5 101.8 reduce-scatter.3
  409.2 31.3 reduce-scatter.5
  443.0 71.4 reduce-scatter.7

commit v6 on v5

--- a/solution.py
+++ b/solution.py
@@ -688,6 +688,33 @@
         compiler_params=pltpu.CompilerParams(vmem_limit_bytes=VMEM_LIMIT),
         name="place_heads",
     )(ctx, mine.reshape(2, rows, cols), other)
+
+
+def place_all_kernel(ctx_ref, out_mine, out_other, ffn_mine, ffn_other, moved, *rest):
+    tokens, (out_ref, up_ref, down_ref), placed = rest[:4], rest[4:7], rest[7:]
+    place_heads_kernel(1, ctx_ref, out_mine, out_other, out_ref)
+    place_feed_kernel(ctx_ref, ffn_mine, ffn_other, moved, up_ref, down_ref)
+    place_tokens_kernel(*tokens, *placed)
+
+
+def place_all(ctx, out_mine, out_other, ffn_mine, ffn_other, moved, tokens, image_length, text_length):
+    rows, out_cols = out_other.shape
+    cols = ffn_other.shape[1]
+    vmem = pl.BlockSpec(memory_space=pltpu.VMEM)
+    out, up, down, *placed = pl.pallas_call(
+        place_all_kernel,
+        in_specs=[pl.BlockSpec(memory_space=pltpu.SMEM)] + [vmem] * 9,
+        out_specs=[vmem] * 7,
+        out_shape=[
+            jax.ShapeDtypeStruct((2, 1, rows, out_cols), F32),
+            jax.ShapeDtypeStruct((2, rows, cols), F32),
+            jax.ShapeDtypeStruct((2, rows, cols), F32),
+        ]
+        + [jax.ShapeDtypeStruct((1, n, tokens[0].shape[2]), BF16) for n in (image_length, text_length) * 2],
+        compiler_params=pltpu.CompilerParams(vmem_limit_bytes=VMEM_LIMIT),
+        name="place_all",
+    )(ctx, out_mine.reshape(2, rows, out_cols), out_other, ffn_mine.reshape(2, rows, cols), ffn_other, moved, *tokens)
+    return out[:, 0], up, down, placed
 
 
 def place_qkv(ctx, mine, other):
@@ -1763,11 +1790,14 @@
         (shared, given(qkv_mine), image_outs, text_outs, out_other, ffn_other)
     )
     qkv_other = other_half(qkv_given)
-    final_tokens = place_tokens((image_outs, text_outs, image_grads, text_grads), image_length, text_length)
-    out_weight_grad = place_out(own_ctx, out_mine, out_other)
+    last_tokens = (image_outs, text_outs, image_grads, text_grads)
     if groups > 1:
-        up_weight_grad, down_weight_grad = place_feed(own_ctx, ffn_mine, ffn_other, moved_in)
+        out_weight_grad, up_weight_grad, down_weight_grad, final_tokens = place_all(
+            own_ctx, out_mine, out_other, ffn_mine, ffn_other, moved_in, last_tokens, image_length, text_length
+        )
     else:
+        final_tokens = place_tokens(last_tokens, image_length, text_length)
+        out_weight_grad = place_out(own_ctx, out_mine, out_other)
         kept, other = lax.dynamic_slice_in_dim(ffn_mine, ctx * shard_rows, shard_rows, 0), ffn_other
         ffn_halves = [jnp.where(ctx == c, kept, other).astype(F32) for c in range(2)]
         up_weight_grad, down_weight_grad = [

time: 550 us -> 547 us (level)
  transfers between devices with their start and end apart: 7 -> 7, of which waited for: 3 -> 4; matrix products, arithmetic and copies ran while one was open for 5% -> 5% of each run, Pallas kernels for 62% -> 61%
where the time goes in v6:
time: 547 us; the launch traced here: 544 us
  Pallas kernels  465 us (85%)
  waiting for transfers between devices  24 us (4%)
  local copies, waits for them, and re-layouts  23.4 us (4%)
  between operations  14.1 us (3%)
  other arithmetic  8.34 us (2%)
    pallas_call x1, Pallas kernels, enter(): comm_call(functools.partial(enter_kernel, n_dp, groups), [jax.ShapeDtypeS...  96.6 us
    pallas_call x1, Pallas kernels, middle_step(): comm_call(functools.partial(middle_kernel, n_dp, groups), outs, reduce_sc...  91.2 us
    pallas_call x1, Pallas kernels, turn_step(): comm_call(functools.partial(turn_kernel, groups), outs, scratch, 30 + 4 *...  84.4 us
    pallas_call x1, Pallas kernels, leave_step(): comm_call(functools.partial(leave_kernel, n_dp), outs, scratch, 1 + 10 +...  62.8 us
    pallas_call x1, Pallas kernels, feed_forward_moving(): pl.pallas_call(functools.partial(feed_moving_kernel, groups, own.shape[0]...  32.4 us
    pallas_call x1, Pallas kernels, attend_backward(): local_call(functools.partial(attend_backward_kernel, steps, heads, text_r...  21.2 us
    pallas_call x1, Pallas kernels, attend_forward(): local_call(functools.partial(attend_forward_kernel, steps, heads, text_ro...  18.7 us
    pallas_call x1, Pallas kernels, unproject(): local_call(functools.partial(unproject_kernel, steps), steps + 1, [block,...  14.2 us
  transfers between devices with their start and end apart: 7, of which 4 were waited for; matrix products, arithmetic and copies ran while one was open for 5% of the time, Pallas kernels for 61%

profile of v6, /device:TPU:0, one launch (start us, length us, event | category | flops | bytes accessed | tf_op | source)
XLA Modules:
  0.0 544.0 jit_solution(18154156513331133034)
XLA Ops:
  7.3 1.7 slice_bitcast_fusion.7
  9.5 0.7 copy.84.part_ref
  11.4 1.1 pad_maximum_fusion.attn_ref
  12.5 0.7 pad.11
  13.8 96.6 %enter.1 = (f32[4,12,384]{2,1,0:T(8,128)}, f32[8,4,192]{2,1,0:T(4,128)}, bf16[2,4,128,1536]{3,2,1,0:T(8,128)(2,1)}, bf16[2,4,24,1536]{3,2,1,0:T(8,128)(2,1)}, f3...) custom-call(f32[4,12,384]{2,1,0:T(8,128)} %copy.84.part_ref, ...), custom_call_target="tpu_custom_call" | custom-call | tf_op jit(solution)/shard_map/enter/pallas_call | solution.py:1091
  110.4 0.6 collective-permute-start
  111.1 1.9 collective-permute-start.2
  113.1 0.9 copy.85
  114.1 0.6 slice.135.mod_ref
  115.5 11.1 %project.1 = (bf16[1280,1536]{1,0:T(8,128)(2,1)}, bf16[1280,192]{1,0:T(8,128)(2,1)}, bf16[1280,192]{1,0:T(8,128)(2,1)}, bf16[1280,192]{1,0:T(8,128)(2,1)}, bf16[2,1536,192]{2,1,0:T(8,128)(2,1)}) custom-call(bf16[1024,1536]{1,0:T(8,128)(2,1)} %bitcast.120, bf16[192,1536]{1,0:T(8,128)(2,1)} %bitcast.143, f32[2,2,1,1536]{3,2,1,0:T(1,128)} %slice.135.mod_ref, ...), custom_call_target="tpu_custom_call" | custom-call | flops 2264924160 | bytes 8847360 | tf_op jit(solution)/shard_map/project/pallas_call | solution.py:94
  126.6 11.2 %collective-permute-done.rest_1_ = bf16[2,384,768]{2,1,0:T(8,128)(2,1)} collective-permute-done((bf16[2,384,768]{2,1,0:T(8,128)(2,1)}, bf16[2,384,768]{2,1,0:T(8,128)(2,1)}, u32[]{:S(2)}, u32[]{:S(2)}) %collective-permute-start) | collective-permute-done | bytes 1179680 | tf_op jit(solution)/shard_map/ppermute | solution.py:1671
  137.9 1.5 collective-permute-start.1
  139.3 0.6 fusion.7.bias_ref
  140.0 0.7 broadcast_in_dim.33.bias_ref
  140.7 0.6 copy.105
  141.9 2.0 dynamic-slice_bitcast_fusion
  143.8 0.7 pad_dynamic-slice_fusion
  145.1 18.7 %attend_forward.1 = (bf16[1280,192]{1,0:T(8,128)(2,1)}, f32[3,1280]{1,0:T(4,128)}, bf16[1024,1536]{1,0:T(8,128)(2,1)}, bf16[192,1536]{1,0:T(8,128)(2,1)}) custom-call(bf16[1280,192]{1,0:T(8,128)(2,1)} %get-tuple-element.99.q_ref, bf16[1280,192]{1,0:T(8,128)(2,1)} %get-tuple-element.100.k_ref, bf16[1280,192]{1,0:T(8,128)(2,1)} %get-tuple-element.101.v_ref, ...), custom_call_target="tpu_custom_call" | custom-call | flops 1258291200 | bytes 4915200 | tf_op jit(solution)/shard_map/attend_forward/pallas_call | solution.py:160
  163.9 2.2 collective-permute-done.1.rest_2_
  166.1 91.2 %middle.1 = (f32[128,1536]{1,0:T(8,128)}, f32[24,1536]{1,0:T(8,128)}, f32[128,1536]{1,0:T(8,128)}, f32[24,1536]{1,0:T(8,128)}, bf16[2,2,2,128,1536]{4,3,2,1,0:T(...) custom-call(bf16[2,2,2,128,1536]{4,3,2,1,0:T(8,128)(2,1)} %bitcast.1, ...), custom_call_target="tpu_custom_call" | custom-call | tf_op jit(solution)/shard_map/middle/pallas_call | solution.py:1261
  257.3 1.3 slice.140.other_ref
  258.7 2.8 slice_bitcast_fusion
  261.5 10.4 %feed_forward.1 = (bf16[768,1536]{1,0:T(8,128)(2,1)}, bf16[768,1536]{1,0:T(8,128)(2,1)}, bf16[1536,384]{1,0:T(8,128)(2,1)}, f32[1,192]{1,0:T(1,128)}) custom-call(s32[1]{0:T(128)} %bitcast.ctx_ref, bf16[768,1536]{1,0:T(8,128)(2,1)} %bitcast.166, bf16[768,1536]{1,0:T(8,128)(2,1)} %bitcast.165, bf16[8,1536]{1,0:T(8,128)(2,1)} %slice.140.other_ref, ...), custom_call_target="tpu_custom_call" | custom-call | flops 2717908992 | bytes 10616832 | tf_op jit(solution)/shard_map/feed_forward/pallas_call | solution.py:438
  271.9 32.4 %feed_moving.1 = (bf16[1024,1536]{1,0:T(8,128)(2,1)}, bf16[1024,1536]{1,0:T(8,128)(2,1)}, bf16[1536,1536]{1,0:T(8,128)(2,1)}, f32[1,768]{1,0:T(1,128)}, bf16[8,192,384]{2,1,0:T(8,128)(2,1)}) custom-call(bf16[1024,1536]{1,0:T(8,128)(2,1)} %bitcast.126, bf16[512,1536]{1,0:T(8,128)(2,1)} %bitcast.128, bf16[512,1536]{1,0:T(8,128)(2,1)} %collective-permute-done.2.other_ref, ...), custom_call_target="tpu_custom_call" | custom-call | tf_op jit(solution)/shard_map/feed_moving/pallas_call | solution.py:565
  304.7 0.7 broadcast_in_dim.36.bias_ref
  305.3 0.7 broadcast_in_dim.32.valid_ref
  306.1 84.4 %turn.1 = (bf16[128,1536]{1,0:T(8,128)(2,1)}, bf16[24,1536]{1,0:T(8,128)(2,1)}, f32[128,1536]{1,0:T(8,128)}, f32[24,1536]{1,0:T(8,128)}, f32[2,16,1536]{2,1,0:T(...) custom-call(f32[24,1536]{1,0:T(8,128)} %broadcast_in_dim.32.valid_ref, ...), custom_call_target="tpu_custom_call" | custom-call | tf_op jit(solution)/shard_map/turn/pallas_call | solution.py:1418
  390.5 6.2 %out_gradient.1 = bf16[1536,384]{1,0:T(8,128)(2,1)} custom-call(bf16[1024,1536]{1,0:T(8,128)(2,1)} %bitcast.123, bf16[192,1536]{1,0:T(8,128)(2,1)} %bitcast.145, bf16[1280,192]{1,0:T(8,128)(2,1)} %get-tuple-element.132.o_ref), custom_call_target="tpu_custom_call" | custom-call | flops 754974720 | bytes 2949120 | tf_op jit(solution)/shard_map/out_gradient/pallas_call | solution.py:204
  396.7 9.6 %reduce-scatter.4.cloned.1.call-done.ffn_mine = bf16[384,1536]{1,0:T(8,128)(2,1)} async-done(((bf16[1536,1536]{1,0:T(8,128)(2,1)}), bf16[384,1536]{1,0:T(8,128)(2,1)}) %reduce-scatter.4.cloned.1.call-update) | async-done | bytes 1179664 | tf_op jit(solution)/shard_map/reduce_scatter | solution.py:1590
  406.4 21.2 %attend_backward.1 = (bf16[1280,192]{1,0:T(8,128)(2,1)}, bf16[1280,192]{1,0:T(8,128)(2,1)}, bf16[1280,192]{1,0:T(8,128)(2,1)}) custom-call(bf16[1280,192]{1,0:T(8,128)(2,1)} %get-tuple-element.99.q_ref, bf16[1280,192]{1,0:T(8,128)(2,1)} %get-tuple-element.100.k_ref, bf16[1280,192]{1,0:T(8,128)(2,1)} %get-tuple-element.101.v_ref, ...), custom_call_target="tpu_custom_call" | custom-call | flops 3145728000 | bytes 12288000 | tf_op jit(solution)/shard_map/attend_backward/pallas_call | solution.py:279
  427.6 14.2 %unproject.1 = (bf16[1024,1536]{1,0:T(8,128)(2,1)}, bf16[192,1536]{1,0:T(8,128)(2,1)}, bf16[1536,1152]{1,0:T(8,128)(2,1)}, f32[2,1,576]{2,1,0:T(1,128)}) custom-call(bf16[1280,192]{1,0:T(8,128)(2,1)} %get-tuple-element.127.dq_ref, bf16[1280,192]{1,0:T(8,128)(2,1)} %get-tuple-element.128.dk_ref, bf16[1280,192]{1,0:T(8,128)(2,1)} %get-tuple-element.129.dv_ref, ...), custom_call_target="tpu_custom_call" | custom-call | flops 4529848320 | bytes 17694720 | tf_op jit(solution)/shard_map/unproject/pallas_call | solution.py:340
  441.8 0.6 copy-done.14
  443.6 62.8 %leave.1 = (bf16[4,128,1536]{2,1,0:T(8,128)(2,1)}, bf16[4,24,1536]{2,1,0:T(8,128)(2,1)}, bf16[4,128,1536]{2,1,0:T(8,128)(2,1)}, bf16[4,24,1536]{2,1,0:T(8,128)(2...) custom-call(bf16[2,2,2,128,1536]{4,3,2,1,0:T(8,128)(2,1)} %bitcast.1, ...), custom_call_target="tpu_custom_call" | custom-call | tf_op jit(solution)/shard_map/leave/pallas_call | solution.py:1552
  506.4 0.9 reduce_sum.48
  507.3 0.9 convert_reduce_fusion
  508.3 0.9 slice_reduce_fusion
  509.8 0.6 select_maximum_fusion.part_ref
  510.4 5.3 share.1
  515.7 0.6 copy.93
  516.4 0.7 reshape.202
  517.1 0.6 reshape.204
  517.7 2.5 convolution_bitcast_fusion
  520.2 1.0 constant_dynamic-slice_fusion.2
  521.4 1.0 collective-permute-start.3
  524.4 7.7 %place_all.1 = (f32[2,1,192,384]{3,2,1,0:T(8,128)}, f32[2,192,1536]{2,1,0:T(8,128)}, f32[2,192,1536]{2,1,0:T(8,128)}, bf16[1,512,1536]{2,1,0:T(8,128)(2,1)}, bf1...) custom-call(s32[1]{0:T(128)} %bitcast.ctx_ref, ...), custom_call_target="tpu_custom_call" | custom-call | tf_op jit(solution)/shard_map/place_all/pallas_call | solution.py:704
  532.8 0.8 collective-permute-done.3.other_ref
  533.6 0.8 copy-done.7
  534.4 3.1 place_heads.1
  (101 shorter events, 9.3 us)
Async XLA Ops:
  7.2 2.0 copy-start
  7.2 2.0 copy-start.12
  7.2 399.1 %reduce-scatter.4.cloned.1.call-start = ((), (), s32[]{:S(2)}) async-start(), calls=%async_computation.3 | async-start | bytes 5898240 | tf_op jit(solution)/shard_map/reduce_scatter | solution.py:1590
  7.3 1.8 copy-start.5
  9.0 1.2 copy-start.13
  11.3 1.2 copy-start.3
  11.3 1.9 copy-start.19
  11.3 1.9 copy-start.20
  13.8 97.2 %copy-start.1 = (bf16[1,512,1536]{2,1,0:T(8,128)(2,1)S(1)}, bf16[1,512,1536]{2,1,0:T(8,128)(2,1)}, u32[]{:S(2)}) copy-start(bf16[1,512,1536]{2,1,0:T(8,128)(2,1)} %param.29) | copy-start | bytes 4718596
  13.8 99.2 %copy-start.16 = (bf16[2,2,384]{2,1,0:T(2,128)(2,1)S(1)}, bf16[2,2,384]{2,1,0:T(2,128)(2,1)}, u32[]{:S(2)}) copy-start(bf16[2,2,384]{2,1,0:T(2,128)(2,1)} %param.22) | copy-start | bytes 9220
  110.4 27.4 %collective-permute-start = (bf16[2,384,768]{2,1,0:T(8,128)(2,1)}, bf16[2,384,768]{2,1,0:T(8,128)(2,1)}, u32[]{:S(2)}, u32[]{:S(2)}) collective-permute-start(bf16[2,384,768]{2,1,0:T(8,128)(2,1)} %bitcast.137), channel_id=1, source_target_pairs={{0,8},{8,16},{16,24},{24,0},{1,9},{9,17},{17,25},{25,1},{2,10},{10... | collective-permute-start | bytes 3538952 | tf_op jit(solution)/shard_map/ppermute | solution.py:1671
  111.1 160.8 %collective-permute-start.2 = (bf16[512,1536]{1,0:T(8,128)(2,1)S(1)}, bf16[512,1536]{1,0:T(8,128)(2,1)}, u32[]{:S(2)}, u32[]{:S(2)}) collective-permute-start(bf16[512,1536]{1,0:T(8,128)(2,1)S(1)} %bitcast.129), channel_id=1, source_target_pairs={{0,4},{4,0},{1,5},{5,1},{2,6},{6,2},{3,7},{7,3},{8,12},{12,8},{9,1... | collective-permute-start | bytes 4718600 | tf_op jit(solution)/shard_map/ppermute | solution.py:1667
  114.1 30.4 %copy-start.2 = (f32[2,6,1,1536]{3,2,1,0:T(1,128)}, f32[2,6,1,1536]{3,2,1,0:T(1,128)S(1)}, u32[]{:S(2)}) copy-start(f32[2,6,1,1536]{3,2,1,0:T(1,128)S(1)} %broadcast_in_dim_reshape.3.mod_ref) | copy-start | bytes 221188
  115.4 11.1 %copy-start.9 = (f32[8,4,192]{2,1,0:T(4,128)S(1)}, f32[8,4,192]{2,1,0:T(4,128)}, u32[]{:S(2)}) copy-start(f32[8,4,192]{2,1,0:T(4,128)} %get-tuple-element.106) | copy-start | bytes 73732
  115.5 11.1 %copy-start.11 = (bf16[2,1536]{1,0:T(2,128)(2,1)S(1)}, bf16[2,1536]{1,0:T(2,128)(2,1)}, u32[]{:S(2)}) copy-start(bf16[2,1536]{1,0:T(2,128)(2,1)} %param.26) | copy-start | bytes 18436
  115.5 25.2 %copy-start.10 = (f32[4,4,384]{2,1,0:T(4,128)S(1)}, f32[4,4,384]{2,1,0:T(4,128)}, u32[]{:S(2)}) copy-start(f32[4,4,384]{2,1,0:T(4,128)} %get-tuple-element.114) | copy-start | bytes 73732
  137.9 28.2 %collective-permute-start.1 = (bf16[2,384,768]{2,1,0:T(8,128)(2,1)}, bf16[2,384,768]{2,1,0:T(8,128)(2,1)}, u32[]{:S(2)}, u32[]{:S(2)}) collective-permute-start(bf16[2,384,768]{2,1,0:T(8,128)(2,1)} %collective-permute-done.rest_1_), channel_id=1, source_target_pairs={{0,8},{8,16},{16,24},{24,0},{1,9},{9,17},{17,25},{25,1},{2,10},{10... | collective-permute-start | bytes 3538952 | tf_op jit(solution)/shard_map/ppermute | solution.py:1699
  141.3 2.5 copy-start.4
  141.3 2.5 copy-start.8
  304.4 137.4 %reduce-scatter.6.cloned.1.call-start = ((), (), s32[]{:S(2)}) async-start(), calls=%async_computation.4 | async-start | bytes 1474560 | tf_op jit(solution)/shard_map/reduce_scatter | solution.py:1590
  406.4 113.8 %reduce-scatter.8.cloned.1.call-start = ((), (), s32[]{:S(2)}) async-start(), calls=%async_computation.5 | async-start | bytes 4423680 | tf_op jit(solution)/shard_map/reduce_scatter | solution.py:1590
  441.8 0.7 copy-start.14
  441.8 0.9 copy-start.15
  441.8 0.9 copy-start.18
  517.7 3.5 copy-start.6
  517.7 4.8 copy-start.17
  521.4 12.2 %collective-permute-start.3 = (bf16[192,1152]{1,0:T(8,128)(2,1)S(1)}, bf16[192,1152]{1,0:T(8,128)(2,1)S(1)}, u32[]{:S(2)}, u32[]{:S(2)}) collective-permute-start(bf16[192,1152]{1,0:T(8,128)(2,1)S(1)} %constant_dynamic-slice_fusion.2), channel_id=1, source_target_pairs={{0,4},{4,0},{1,5},{5,1},{2,6},{6,2},{3,7},{7,3},{8,12},{12,8},{9,1... | collective-permute-start | bytes 1327112 | tf_op jit(solution)/shard_map/ppermute | solution.py:1688
  533.6 0.8 copy-start.7
Sparse Core Ops, SparseCore 0:
  304.5 101.7 reduce-scatter.3
  409.2 31.4 reduce-scatter.5
  443.0 71.4 reduce-scatter.7
